TPU v7x, 32 devices: a whole 2x2x4 slice. The times are simulated.
32 devices in a mesh: seq: 16 (over z, y, core), head: 2 (over x).
Axes of the slice: x: 2, y: 2, z: 4, core: 2. Of those that a mesh axis runs over, the one named last changes fastest.
Arguments:
- query_rows: bfloat16 [24576, 2048], P('seq', 'head'), may hold values from -8 to 8
- key_rows: bfloat16 [24576, 2048], P('seq', 'head'), may hold values from -8 to 8
- value_rows: bfloat16 [24576, 2048], P('seq', 'head'), may hold values from -6 to 6
- head_phase: int32 [16], P('head'), may hold values from 0 to 15, each once
- out_weight: bfloat16 [2048, 2048], P('head'), may hold values from -0.125 to 0.125
Outputs:
- projected: bfloat16 [24576, 2048], P(('seq', 'head'))
Inputs may be any that keep to these rules, and one draw needn't show every extreme that they name: `head_phase`: the 16 heads have distinct phases.
All inputs are finite; a program needn't handle non-finite values.
Results may differ from a plain program's by a relative error of at most 0.006.
Values may be sent and summed in bfloat16 or wider, within the bound.
No kernel may reach another device: no remote copies, remote signals or barrier semaphores. Data moves between devices by JAX's collectives and lax.ppermute only.
A program may use at most 256 MiB of HBM per device.

v0:
```python
import math

import jax
import jax.numpy as jnp
from jax import lax
from jax.sharding import PartitionSpec as P


def swapped(value, axis, bit):
    mask = 2**bit
    pairs = [(source, source ^ mask) for source in range(lax.axis_size(axis))]
    return lax.ppermute(value, axis, pairs)


def halve(block, parity, axis):
    shape = block.shape
    shaped = block.reshape(shape[:axis] + (shape[axis] // 2, 2) + shape[axis + 1 :])
    even = lax.index_in_dim(shaped, 0, axis + 1, keepdims=False)
    odd = lax.index_in_dim(shaped, 1, axis + 1, keepdims=False)
    chooser = parity.reshape((-1,) + (1,) * (even.ndim - 1))
    return jnp.where(chooser == 0, even, odd)


def restore(block, fresh, parity, axis):
    shape = block.shape
    shaped = block.reshape(shape[:axis] + (shape[axis] // 2, 2) + shape[axis + 1 :])
    slots = lax.broadcasted_iota(jnp.int32, shaped.shape, axis + 1)
    chooser = parity.reshape((-1,) + (1,) * (shaped.ndim - 1))
    return jnp.where(slots == chooser, jnp.expand_dims(fresh, axis + 1), shaped).reshape(shape)


def attend(queries, key_values, score_scale):

    def score_tile(query_block):
        scores = (
            jnp.einsum(
                "gqd,gkd->gqk", query_block, key_values[:, 0], preferred_element_type=jnp.float32
            )
            * score_scale
        )
        row_peak = jnp.max(scores, axis=2)
        weights = jnp.exp(scores - row_peak[:, :, None])
        row_total = jnp.sum(weights, axis=2)
        row_mixed = jnp.einsum(
            "gqk,gkd->gqd",
            weights.astype(jnp.bfloat16),
            key_values[:, 1],
            preferred_element_type=jnp.float32,
        )
        return (row_peak, row_total, row_mixed)

    query_count = queries.shape[1]
    if query_count > 512 and query_count % 512 == 0:
        results = [
            score_tile(queries[:, first : first + 512]) for first in range(0, query_count, 512)
        ]
        return (
            jnp.concatenate([item[0] for item in results], axis=1),
            jnp.concatenate([item[1] for item in results], axis=1),
            jnp.concatenate([item[2] for item in results], axis=1),
        )
    return score_tile(queries)


def body(query_rows, key_rows, value_rows, head_phase, out_weight):
    groups = head_phase.shape[0]
    head_width = query_rows.shape[1] // groups
    levels = lax.axis_size("seq").bit_length() - 1
    score_scale = 1.0 / math.sqrt(head_width)
    bits = [head_phase // 2**level_index % 2 for level_index in range(levels + 1)]

    def head_cols(block, group_index):
        return block[:, group_index * head_width : (group_index + 1) * head_width]

    query_levels = [
        jnp.stack([head_cols(query_rows, group_index) for group_index in range(groups)])
    ]
    own_levels = [
        jnp.stack(
            [
                jnp.stack([head_cols(key_rows, group_index), head_cols(value_rows, group_index)])
                for group_index in range(groups)
            ]
        )
    ]
    for level_index in range(1, levels + 1):
        query_levels.append(halve(query_levels[-1], bits[level_index - 1], 1))
        own_levels.append(halve(own_levels[-1], bits[level_index - 1], 2))
    key_values = {0: own_levels[0]}
    for level_index in range(1, levels + 1):
        block_rows = own_levels[level_index]
        for bit_index in range(level_index):
            block_rows = jnp.concatenate(
                (block_rows, swapped(block_rows, "seq", bit_index)), axis=2
            )
        key_values[level_index] = block_rows
    outcomes = [
        attend(query_levels[level_index], key_values[level_index], score_scale)
        for level_index in range(levels + 1)
    ]
    peak_now, total_now, sum_now = outcomes[levels]
    for level_index in range(levels - 1, -1, -1):
        level_peak, level_total, level_sum = outcomes[level_index]
        parity = bits[level_index]
        old_peak = halve(level_peak, parity, 1)
        old_total = halve(level_total, parity, 1)
        old_sum = halve(level_sum, parity, 1)
        new_peak = jnp.maximum(old_peak, peak_now)
        keep_scale = jnp.exp(old_peak - new_peak)
        fresh_scale = jnp.exp(peak_now - new_peak)
        new_total = old_total * keep_scale + total_now * fresh_scale
        new_sum = old_sum * keep_scale[:, :, None] + sum_now * fresh_scale[:, :, None]
        peak_now = restore(level_peak, new_peak, parity, 1)
        total_now = restore(level_total, new_total, parity, 1)
        sum_now = restore(level_sum, new_sum, parity, 1)
    normed = (sum_now / total_now[:, :, None]).astype(jnp.bfloat16)
    attended = jnp.concatenate([normed[group_index] for group_index in range(groups)], axis=1)
    return lax.psum_scatter(
        jnp.dot(attended, out_weight, preferred_element_type=jnp.float32).astype(jnp.bfloat16),
        "head",
        scatter_dimension=0,
        tiled=True,
    )


def solution(mesh):
    in_specs = (P("seq", "head"), P("seq", "head"), P("seq", "head"), P("head"), P("head", None))
    out_specs = P(("seq", "head"), None)
    return jax.shard_map(body, mesh=mesh, in_specs=in_specs, out_specs=out_specs, check_vma=False)
```

profile of v0, /device:TPU:0, one launch (start us, length us, event | category | flops | bytes accessed | tf_op | source)
XLA Modules:
  0.0 491.9 jit_solution(9219640155964292089)
XLA Ops:
  7.8 2.8 slice_bitcast_fusion.38
  12.5 2.1 slice_bitcast_fusion.37
  19.1 2.1 bitcast_select_fusion
  23.1 1.9 fusion.136
  28.0 10.4 %multiply_reduce_fusion.2 = (f32[8,512]{1,0:T(8,128)S(1)}, f32[8,512,1536]{2,1,0:T(8,128)}) fusion(bf16[8,2,1536,128]{3,2,0,1:T(8,128)(2,1)S(1)} %fusion.73, bf16[8,1536,128]{2,1,0:T(8,128)(2,1)S(1)} %bitcast_dynamic-update-slice_fusion), kind=kOutput, calls=%fused_computation.8 | convolution fusion | flops 1623191552 | bytes 29376512 | tf_op jit(solution)/shard_map/gqd,gkd->gqk/dot_general | solution.py:36
  38.4 10.1 %multiply_reduce_fusion.1 = (f32[8,512]{1,0:T(8,128)S(1)}, f32[8,512,1536]{2,1,0:T(8,128)}) fusion(bf16[8,2,1536,128]{3,2,0,1:T(8,128)(2,1)S(1)} %fusion.73, bf16[8,1536,128]{2,1,0:T(8,128)(2,1)S(1)} %bitcast_dynamic-update-slice_fusion), kind=kOutput, calls=%fused_computation.7 | convolution fusion | flops 1623191552 | bytes 29376512 | tf_op jit(solution)/shard_map/gqd,gkd->gqk/dot_general | solution.py:36
  48.5 11.5 %fusion.6 = f32[8,512]{1,0:T(8,128)S(1)} fusion(f32[8,512,1536]{2,1,0:T(8,128)} %get-tuple-element.128, f32[8,512]{1,0:T(8,128)S(1)} %get-tuple-element.127), kind=kLoop, calls=%fused_computation.14 | loop fusion | flops 18870272 | bytes 25198592 | tf_op jit(solution)/shard_map/reduce_sum | solution.py:43
  60.0 11.6 %fusion.14 = f32[8,512,128]{2,1,0:T(8,128)} fusion(f32[8,512,1536]{2,1,0:T(8,128)} %get-tuple-element.128, f32[8,512]{1,0:T(8,128)S(1)} %get-tuple-element.127, bf16[8,2,1536,128]{3,2,0,1:T(8,128)(2,1)S(1)} %fusion.73), kind=kOutput, calls=%fused_computation.23 | convolution fusion | flops 1629487104 | bytes 30425088 | tf_op jit(solution)/shard_map/gqk,gkd->gqd/dot_general | solution.py:44
  71.6 10.1 %multiply_reduce_fusion.3 = (f32[8,512]{1,0:T(8,128)S(1)}, f32[8,512,1536]{2,1,0:T(8,128)}) fusion(bf16[8,2,1536,128]{3,2,0,1:T(8,128)(2,1)S(1)} %fusion.73, bf16[8,1536,128]{2,1,0:T(8,128)(2,1)S(1)} %bitcast_dynamic-update-slice_fusion), kind=kOutput, calls=%fused_computation.9 | convolution fusion | flops 1623191552 | bytes 29376512 | tf_op jit(solution)/shard_map/gqd,gkd->gqk/dot_general | solution.py:36
  81.7 11.7 %fusion.16 = f32[8,512,128]{2,1,0:T(8,128)} fusion(f32[8,512,1536]{2,1,0:T(8,128)} %get-tuple-element.130, f32[8,512]{1,0:T(8,128)S(1)} %get-tuple-element.129, bf16[8,2,1536,128]{3,2,0,1:T(8,128)(2,1)S(1)} %fusion.73), kind=kOutput, calls=%fused_computation.24 | convolution fusion | flops 1629487104 | bytes 30425088 | tf_op jit(solution)/shard_map/gqk,gkd->gqd/dot_general | solution.py:44
  93.4 19.6 %fusion.2 = (f32[8,512]{1,0:T(8,128)S(1)}, f32[8,512]{1,0:T(8,128)S(1)}) fusion(f32[8,512,1536]{2,1,0:T(8,128)} %get-tuple-element.132, f32[8,512]{1,0:T(8,128)S(1)} %get-tuple-element.131, f32[8,512]{1,0:T(8,128)S(1)} %get-tuple-element.129, f32[8,512,1536]{2,1,0:T(8,128)} %get-tuple-element.130), kind=kLoop, calls=%fused_computation.10 | loop fusion | flops 37740544 | bytes 50397184 | tf_op jit(solution)/shard_map/reduce_sum | solution.py:43
  113.1 11.7 %fusion.18 = f32[8,512,128]{2,1,0:T(8,128)} fusion(f32[8,512,1536]{2,1,0:T(8,128)} %get-tuple-element.132, f32[8,512]{1,0:T(8,128)S(1)} %get-tuple-element.131, bf16[8,2,1536,128]{3,2,0,1:T(8,128)(2,1)S(1)} %fusion.73), kind=kOutput, calls=%fused_computation.25 | convolution fusion | flops 1629487104 | bytes 30425088 | tf_op jit(solution)/shard_map/gqk,gkd->gqd/dot_general | solution.py:44
  131.5 2.0 copy.194
  133.5 2.0 copy.134
  135.5 3.1 fusion.141
  138.5 3.1 fusion.142
  141.9 1.5 pad_maximum_fusion.9
  143.4 3.2 collective-permute-start.7
  146.6 3.0 pad_maximum_fusion
  151.7 13.3 %collective-permute-done.7 = bf16[8,2,192,128]{3,2,0,1:T(8,128)(2,1)S(1)} collective-permute-done((bf16[8,2,192,128]{3,2,0,1:T(8,128)(2,1)S(1)}, bf16[8,2,192,128]{3,2,0,1:T(8,128)(2,1)S(1)}, u32[]{:S(2)}, u32[]{:S(2)}) %collective-permute-start.7) | collective-permute-done | bytes 786464 | tf_op jit(solution)/shard_map/ppermute | solution.py:12
  165.8 2.3 pad_maximum_fusion.8
  168.1 2.1 collective-permute-start.8
  171.7 1.5 iota.110
  173.8 1.6 iota.107
  179.2 1.7 copy.218
  180.9 1.7 copy.217
  182.7 1.7 copy.232
  184.4 1.9 copy.231
  186.3 13.3 %fusion.132 = (f32[8,768,1,128]{3,2,1,0:T(1,128)}, f32[8,768,1,128]{3,2,1,0:T(1,128)}) fusion(f32[8,768,2,128]{3,2,1,0:T(2,128)} %bitcast.391), kind=kLoop, calls=%fused_computation.284 | loop fusion | bytes 12582912 | tf_op jit(solution)/shard_map/slice | solution.py:19
  199.6 1.8 constant_dynamic-update-slice_fusion.3
  201.4 2.2 constant_dynamic-update-slice_fusion.2
  203.5 3.4 pad_maximum_fusion.4
  206.9 1.5 collective-permute-start.2
  208.5 3.3 pad_maximum_fusion.5
  212.2 2.9 pad_maximum_fusion.6
  215.2 2.6 collective-permute-start.9
  217.8 2.9 constant_dynamic-update-slice_fusion.1
  220.7 17.9 %multiply_reduce_fusion = (f32[8,768]{1,0:T(8,128)}, f32[8,768,1536]{2,1,0:T(8,128)}) fusion(bf16[8,2,768,128]{3,2,0,1:T(8,128)(2,1)} %bitcast_select_fusion, bf16[8,2,768,128]{3,2,0,1:T(8,128)(2,1)} %collective-permute-done, pred[8]{0:T(512)(128)(4,1)S(1)} %get-tuple-element.113, bf16[8,768,2,128]{3,1,0,2:T(8,128)(2,1)} %copy-done.7), kind=kOutput, calls=%fused_computation.1 | convolution fusion | flops 2441865216 | bytes 47210504 | tf_op jit(solution)/shard_map/gqd,gkd->gqk/dot_general | solution.py:36
  239.5 17.5 %fusion = f32[8,768]{1,0:T(8,128)} fusion(f32[8,768,1536]{2,1,0:T(8,128)} %get-tuple-element.126, f32[8,768]{1,0:T(8,128)} %get-tuple-element.125), kind=kLoop, calls=%fused_computation.2 | loop fusion | flops 28305408 | bytes 37797888 | tf_op jit(solution)/shard_map/reduce_sum | solution.py:43
  257.0 1.7 copy.197
  258.7 2.2 fusion.146
  260.9 1.6 copy.234
  262.5 1.6 copy.233
  267.2 17.4 %fusion.8 = f32[8,768,128]{2,1,0:T(8,128)} fusion(f32[8,768,1536]{2,1,0:T(8,128)} %get-tuple-element.126, f32[8,768]{1,0:T(8,128)} %get-tuple-element.125, bf16[8,2,768,128]{3,2,0,1:T(8,128)(2,1)} %collective-permute-done, bf16[8,2,768,128]{3,2,0,1:T(8,128)(2,1)} %bitcast_select_fusion), kind=kOutput, calls=%fused_computation.16 | convolution fusion | flops 2450522112 | bytes 47210496 | tf_op jit(solution)/shard_map/gqk,gkd->gqd/dot_general | solution.py:44
  284.7 7.7 %fusion.134 = (f32[8,384,1,128]{3,2,1,0:T(1,128)}, f32[8,384,1,128]{3,2,1,0:T(1,128)}) fusion(f32[8,384,2,128]{3,2,1,0:T(2,128)} %bitcast.395), kind=kLoop, calls=%fused_computation.286 | loop fusion | bytes 6291456 | tf_op jit(solution)/shard_map/slice | solution.py:19
  292.4 2.8 pad_maximum_fusion.1
  295.2 11.0 %multiply_reduce_fusion.4 = (f32[8,384]{1,0:T(8,128)S(1)}, f32[8,384,1536]{2,1,0:T(8,128)}) fusion(bf16[8,2,1536,128]{3,2,0,1:T(8,128)(2,1)S(1)} %pad_maximum_fusion.1, pred[8]{0:T(512)(128)(4,1)S(1)} %copy-done.55, bf16[8,384,2,128]{3,1,0,2:T(8,128)(2,1)} %copy-done.8), kind=kOutput, calls=%fused_computation.20 | convolution fusion | flops 1217786880 | bytes 23605760 | tf_op jit(solution)/shard_map/gqd,gkd->gqk/dot_general | solution.py:36
  306.3 9.6 %fusion.12 = f32[8,384]{1,0:T(8,128)S(1)} fusion(f32[8,384,1536]{2,1,0:T(8,128)} %get-tuple-element.124, f32[8,384]{1,0:T(8,128)S(1)} %get-tuple-element.123), kind=kLoop, calls=%fused_computation.21 | loop fusion | flops 14152704 | bytes 18898944 | tf_op jit(solution)/shard_map/reduce_sum | solution.py:43
  316.7 9.3 %fusion.26 = f32[8,384,128]{2,1,0:T(8,128)S(1)} fusion(f32[8,384,1536]{2,1,0:T(8,128)} %get-tuple-element.124, f32[8,384]{1,0:T(8,128)S(1)} %get-tuple-element.123, bf16[8,2,1536,128]{3,2,0,1:T(8,128)(2,1)} %copy-done.1), kind=kOutput, calls=%fused_computation.32 | convolution fusion | flops 1222115328 | bytes 23605248 | tf_op jit(solution)/shard_map/gqk,gkd->gqd/dot_general | solution.py:44
  326.0 2.7 fusion.138
  328.7 16.2 %collective-permute-done.5 = bf16[8,2,768,128]{3,2,0,1:T(8,128)(2,1)} collective-permute-done((bf16[8,2,768,128]{3,2,0,1:T(8,128)(2,1)}, bf16[8,2,768,128]{3,2,0,1:T(8,128)(2,1)}, u32[]{:S(2)}, u32[]{:S(2)}) %collective-permute-start.5) | collective-permute-done | bytes 3145760 | tf_op jit(solution)/shard_map/ppermute | solution.py:12
  344.9 3.1 pad_maximum_fusion.2
  348.1 5.5 %multiply_reduce_fusion.5 = (f32[8,192]{1,0:T(8,128)S(1)}, f32[8,192,1536]{2,1,0:T(8,128)}) fusion(bf16[8,2,1536,128]{3,2,0,1:T(8,128)(2,1)S(1)} %pad_maximum_fusion.2, pred[8]{0:T(512)(128)(4,1)S(1)} %copy-done.57, bf16[8,192,2,128]{3,1,0,2:T(8,128)(2,1)S(1)} %copy-done.23), kind=kOutput, calls=%fused_computation.36 | convolution fusion | flops 608893440 | bytes 13376000 | tf_op jit(solution)/shard_map/gqd,gkd->gqk/dot_general | solution.py:36
  353.7 5.4 %fusion.30 = f32[8,192]{1,0:T(8,128)S(1)} fusion(f32[8,192,1536]{2,1,0:T(8,128)} %get-tuple-element.122, f32[8,192]{1,0:T(8,128)S(1)} %get-tuple-element.121), kind=kLoop, calls=%fused_computation.37 | loop fusion | flops 7076352 | bytes 9449472 | tf_op jit(solution)/shard_map/reduce_sum | solution.py:43
  359.7 6.0 %fusion.32 = f32[8,192,128]{2,1,0:T(8,128)S(1)} fusion(f32[8,192,1536]{2,1,0:T(8,128)} %get-tuple-element.122, f32[8,192]{1,0:T(8,128)S(1)} %get-tuple-element.121, bf16[8,2,1536,128]{3,2,0,1:T(8,128)(2,1)} %copy-done.2), kind=kOutput, calls=%fused_computation.46 | convolution fusion | flops 611057664 | bytes 13375488 | tf_op jit(solution)/shard_map/gqk,gkd->gqd/dot_general | solution.py:44
  366.5 4.2 constant_dynamic-update-slice_fusion
  370.7 3.2 multiply_reduce_fusion.6
  373.9 2.1 copy-done
  380.4 4.5 fusion.60
  391.6 1.9 multiply_add_fusion
  393.6 2.3 broadcast_in_dim.318
  396.4 2.9 divide_convert_fusion
  401.5 8.8 %convolution_convert_fusion = bf16[1536,2048]{1,0:T(8,128)(2,1)} fusion(bf16[1536,1024]{1,0:T(8,128)(2,1)S(1)} %fusion.76, bf16[1024,2048]{1,0:T(8,128)(2,1)S(1)} %copy-done.66), kind=kOutput, calls=%fused_computation.39 | convolution fusion | flops 6445596672 | bytes 13631488 | tf_op jit(solution)/shard_map/dot_general | solution.py:119
  410.3 74.5 %reduce-scatter.2.cloned.1.call-done = bf16[768,2048]{1,0:T(8,128)(2,1)} async-done(((bf16[1536,2048]{1,0:T(8,128)(2,1)}), bf16[768,2048]{1,0:T(8,128)(2,1)}) %reduce-scatter.2.cloned.1.call-update) | async-done | bytes 3145744 | tf_op jit(solution)/shard_map/reduce_scatter | solution.py:118
  (287 shorter events, 47.8 us)
Async XLA Ops:
  6.5 478.3 %reduce-scatter.2.cloned.1.call-start = ((), (), s32[]{:S(2)}) async-start(), calls=%async_computation.1 | async-start | bytes 9437184 | tf_op jit(solution)/shard_map/reduce_scatter | solution.py:118
  7.8 14.2 %copy-start.60 = (pred[8]{0:T(512)(128)(4,1)}, pred[8]{0:T(512)(128)(4,1)S(1)}, u32[]{:S(2)}) copy-start(pred[8]{0:T(512)(128)(4,1)S(1)} %get-tuple-element.18) | copy-start | bytes 28
  7.8 133.9 %copy-start.54 = (pred[8]{0:T(512)(128)(4,1)}, pred[8]{0:T(512)(128)(4,1)S(1)}, u32[]{:S(2)}) copy-start(pred[8]{0:T(512)(128)(4,1)S(1)} %get-tuple-element.117) | copy-start | bytes 28
  7.8 162.4 %copy-start.56 = (pred[8]{0:T(512)(128)(4,1)}, pred[8]{0:T(512)(128)(4,1)S(1)}, u32[]{:S(2)}) copy-start(pred[8]{0:T(512)(128)(4,1)S(1)} %get-tuple-element.115) | copy-start | bytes 28
  10.6 1.9 copy-start.28
  18.2 131.5 %collective-permute-start.3 = (bf16[8,2,192,128]{3,2,0,1:T(8,128)(2,1)S(1)}, bf16[8,2,192,128]{3,2,0,1:T(8,128)(2,1)S(1)}, u32[]{:S(2)}, u32[]{:S(2)}) collective-permute-start(bf16[8,2,192,128]{3,2,0,1:T(8,128)(2,1)S(1)} %bitcast_select_fusion.4), channel_id=1, source_target_pairs={{0,2},{2,0},{4,6},{6,4},{8,10},{10,8},{12,14},{14,12},{16,18},{18,... | collective-permute-start | bytes 2359304 | tf_op jit(solution)/shard_map/ppermute | solution.py:12
  18.9 184.6 %collective-permute-start.1 = (bf16[8,2,384,128]{3,2,0,1:T(8,128)(2,1)S(1)}, bf16[8,2,384,128]{3,2,0,1:T(8,128)(2,1)}, u32[]{:S(2)}, u32[]{:S(2)}) collective-permute-start(bf16[8,2,384,128]{3,2,0,1:T(8,128)(2,1)S(1)} %bitcast_select_fusion.1), channel_id=1, source_target_pairs={{0,2},{2,0},{4,6},{6,4},{8,10},{10,8},{12,14},{14,12},{16,18},{18,... | collective-permute-start | bytes 4718600 | tf_op jit(solution)/shard_map/ppermute | solution.py:12
  21.1 1.9 copy-start.3
  21.1 199.6 %collective-permute-start = (bf16[8,2,768,128]{3,2,0,1:T(8,128)(2,1)}, bf16[8,2,768,128]{3,2,0,1:T(8,128)(2,1)}, u32[]{:S(2)}, u32[]{:S(2)}) collective-permute-start(bf16[8,2,768,128]{3,2,0,1:T(8,128)(2,1)} %bitcast_select_fusion), channel_id=1, source_target_pairs={{0,2},{2,0},{4,6},{6,4},{8,10},{10,8},{12,14},{14,12},{16,18},{18,... | collective-permute-start | bytes 9437192 | tf_op jit(solution)/shard_map/ppermute | solution.py:12
  22.9 118.9 %collective-permute-start.6 = (bf16[8,2,96,128]{3,2,0,1:T(8,128)(2,1)S(1)}, bf16[8,2,96,128]{3,2,0,1:T(8,128)(2,1)}, u32[]{:S(2)}, u32[]{:S(2)}) collective-permute-start(bf16[8,2,96,128]{3,2,0,1:T(8,128)(2,1)S(1)} %get-tuple-element.17), channel_id=1, source_target_pairs={{0,2},{2,0},{4,6},{6,4},{8,10},{10,8},{12,14},{14,12},{16,18},{18,... | collective-permute-start | bytes 1179656 | tf_op jit(solution)/shard_map/ppermute | solution.py:12
  113.0 12.4 %copy-start.44 = (bf16[1536,128]{1,0:T(8,128)(2,1)S(1)}, bf16[1536,128]{1,0:T(8,128)(2,1)}, u32[]{:S(2)}) copy-start(bf16[1536,128]{1,0:T(8,128)(2,1)} %get-tuple-element.72) | copy-start | bytes 1179652
  113.0 12.5 %copy-start.43 = (bf16[1536,128]{1,0:T(8,128)(2,1)S(1)}, bf16[1536,128]{1,0:T(8,128)(2,1)}, u32[]{:S(2)}) copy-start(bf16[1536,128]{1,0:T(8,128)(2,1)} %get-tuple-element.71) | copy-start | bytes 1179652
  113.0 12.6 %copy-start.42 = (bf16[1536,128]{1,0:T(8,128)(2,1)S(1)}, bf16[1536,128]{1,0:T(8,128)(2,1)}, u32[]{:S(2)}) copy-start(bf16[1536,128]{1,0:T(8,128)(2,1)} %get-tuple-element.70) | copy-start | bytes 1179652
  113.1 12.7 %copy-start.41 = (bf16[1536,128]{1,0:T(8,128)(2,1)S(1)}, bf16[1536,128]{1,0:T(8,128)(2,1)}, u32[]{:S(2)}) copy-start(bf16[1536,128]{1,0:T(8,128)(2,1)} %get-tuple-element.69) | copy-start | bytes 1179652
  126.3 1.7 copy-start.7
  135.5 6.2 %copy-start.26 = (bf16[8,384,1,128]{3,1,0,2:T(8,128)(2,1)S(1)}, bf16[8,384,1,128]{3,1,0,2:T(8,128)(2,1)}, u32[]{:S(2)}) copy-start(bf16[8,384,1,128]{3,1,0,2:T(8,128)(2,1)} %get-tuple-element.78) | copy-start | bytes 2359300
  135.5 6.2 %copy-start.27 = (bf16[8,384,1,128]{3,1,0,2:T(8,128)(2,1)S(1)}, bf16[8,384,1,128]{3,1,0,2:T(8,128)(2,1)}, u32[]{:S(2)}) copy-start(bf16[8,384,1,128]{3,1,0,2:T(8,128)(2,1)} %get-tuple-element.79) | copy-start | bytes 2359300
  138.5 8.1 %copy-start.13 = (f32[8,512,128]{2,1,0:T(8,128)S(1)}, f32[8,512,128]{2,1,0:T(8,128)}, u32[]{:S(2)}) copy-start(f32[8,512,128]{2,1,0:T(8,128)} %fusion.18) | copy-start | bytes 6291460
  141.6 5.0 %copy-start.9 = (f32[8,512,128]{2,1,0:T(8,128)S(1)}, f32[8,512,128]{2,1,0:T(8,128)}, u32[]{:S(2)}) copy-start(f32[8,512,128]{2,1,0:T(8,128)} %fusion.14) | copy-start | bytes 6291460
  141.6 5.0 %copy-start.11 = (f32[8,512,128]{2,1,0:T(8,128)S(1)}, f32[8,512,128]{2,1,0:T(8,128)}, u32[]{:S(2)}) copy-start(f32[8,512,128]{2,1,0:T(8,128)} %fusion.16) | copy-start | bytes 6291460
  141.9 7.8 %copy-start.22 = (bf16[8,192,2,128]{3,1,0,2:T(8,128)(2,1)}, bf16[8,192,2,128]{3,1,0,2:T(8,128)(2,1)S(1)}, u32[]{:S(2)}) copy-start(bf16[8,192,2,128]{3,1,0,2:T(8,128)(2,1)S(1)} %copy_select_fusion.4) | copy-start | bytes 2359300
  143.4 21.5 %collective-permute-start.7 = (bf16[8,2,192,128]{3,2,0,1:T(8,128)(2,1)S(1)}, bf16[8,2,192,128]{3,2,0,1:T(8,128)(2,1)S(1)}, u32[]{:S(2)}, u32[]{:S(2)}) collective-permute-start(bf16[8,2,192,128]{3,2,0,1:T(8,128)(2,1)S(1)} %pad_maximum_fusion.9), channel_id=1, source_target_pairs={{0,4},{2,6},{4,0},{6,2},{8,12},{10,14},{12,8},{14,10},{16,20},{18,... | collective-permute-start | bytes 2359304 | tf_op jit(solution)/shard_map/ppermute | solution.py:12
  150.9 57.5 %collective-permute-start.4 = (bf16[8,2,384,128]{3,2,0,1:T(8,128)(2,1)}, bf16[8,2,384,128]{3,2,0,1:T(8,128)(2,1)}, u32[]{:S(2)}, u32[]{:S(2)}) collective-permute-start(bf16[8,2,384,128]{3,2,0,1:T(8,128)(2,1)} %pad_maximum_fusion.7), channel_id=1, source_target_pairs={{0,4},{2,6},{4,0},{6,2},{8,12},{10,14},{12,8},{14,10},{16,20},{18,... | collective-permute-start | bytes 4718600 | tf_op jit(solution)/shard_map/ppermute | solution.py:12
  168.1 44.1 %collective-permute-start.8 = (bf16[8,2,384,128]{3,2,0,1:T(8,128)(2,1)}, bf16[8,2,384,128]{3,2,0,1:T(8,128)(2,1)}, u32[]{:S(2)}, u32[]{:S(2)}) collective-permute-start(bf16[8,2,384,128]{3,2,0,1:T(8,128)(2,1)} %pad_maximum_fusion.8), channel_id=1, source_target_pairs={{0,8},{2,10},{4,12},{6,14},{8,0},{10,2},{12,4},{14,6},{16,24},{18,... | collective-permute-start | bytes 4718600 | tf_op jit(solution)/shard_map/ppermute | solution.py:12
  206.9 5.3 %copy-start.16 = (bf16[8,2,192,128]{3,2,0,1:T(8,128)(2,1)S(1)}, bf16[8,2,192,128]{3,2,0,1:T(8,128)(2,1)}, u32[]{:S(2)}) copy-start(bf16[8,2,192,128]{3,2,0,1:T(8,128)(2,1)} %copy-done.15) | copy-start | bytes 2359300
  206.9 85.4 %collective-permute-start.2 = (bf16[8,2,768,128]{3,2,0,1:T(8,128)(2,1)}, bf16[8,2,768,128]{3,2,0,1:T(8,128)(2,1)}, u32[]{:S(2)}, u32[]{:S(2)}) collective-permute-start(bf16[8,2,768,128]{3,2,0,1:T(8,128)(2,1)} %pad_maximum_fusion.4), channel_id=1, source_target_pairs={{0,4},{2,6},{4,0},{6,2},{8,12},{10,14},{12,8},{14,10},{16,20},{18,... | collective-permute-start | bytes 9437192 | tf_op jit(solution)/shard_map/ppermute | solution.py:12
  211.8 133.1 %collective-permute-start.5 = (bf16[8,2,768,128]{3,2,0,1:T(8,128)(2,1)}, bf16[8,2,768,128]{3,2,0,1:T(8,128)(2,1)}, u32[]{:S(2)}, u32[]{:S(2)}) collective-permute-start(bf16[8,2,768,128]{3,2,0,1:T(8,128)(2,1)} %pad_maximum_fusion.5), channel_id=1, source_target_pairs={{0,8},{2,10},{4,12},{6,14},{8,0},{10,2},{12,4},{14,6},{16,24},{18,... | collective-permute-start | bytes 9437192 | tf_op jit(solution)/shard_map/ppermute | solution.py:12
  215.2 151.3 %collective-permute-start.9 = (bf16[8,2,768,128]{3,2,0,1:T(8,128)(2,1)}, bf16[8,2,768,128]{3,2,0,1:T(8,128)(2,1)}, u32[]{:S(2)}, u32[]{:S(2)}) collective-permute-start(bf16[8,2,768,128]{3,2,0,1:T(8,128)(2,1)} %pad_maximum_fusion.6), channel_id=1, source_target_pairs={{0,16},{2,18},{4,20},{6,22},{8,24},{10,26},{12,28},{14,30},{16,0},... | collective-permute-start | bytes 9437192 | tf_op jit(solution)/shard_map/ppermute | solution.py:12
  292.4 2.8 copy-start.55
  295.2 11.0 %copy-start.1 = (bf16[8,2,1536,128]{3,2,0,1:T(8,128)(2,1)}, bf16[8,2,1536,128]{3,2,0,1:T(8,128)(2,1)S(1)}, u32[]{:S(2)}) copy-start(bf16[8,2,1536,128]{3,2,0,1:T(8,128)(2,1)S(1)} %pad_maximum_fusion.1) | copy-start | bytes 18874372
  326.0 22.1 %copy-start.18 = (f32[8,384,128]{2,1,0:T(8,128)}, f32[8,384,128]{2,1,0:T(8,128)S(1)}, u32[]{:S(2)}) copy-start(f32[8,384,128]{2,1,0:T(8,128)S(1)} %fusion.26) | copy-start | bytes 4718596
  328.7 19.4 %copy-start.23 = (bf16[8,192,2,128]{3,1,0,2:T(8,128)(2,1)S(1)}, bf16[8,192,2,128]{3,1,0,2:T(8,128)(2,1)}, u32[]{:S(2)}) copy-start(bf16[8,192,2,128]{3,1,0,2:T(8,128)(2,1)} %copy-done.22) | copy-start | bytes 2359300
  328.7 19.4 %copy-start.57 = (pred[8]{0:T(512)(128)(4,1)S(1)}, pred[8]{0:T(512)(128)(4,1)}, u32[]{:S(2)}) copy-start(pred[8]{0:T(512)(128)(4,1)} %copy-done.56) | copy-start | bytes 28
  348.1 5.5 %copy-start.2 = (bf16[8,2,1536,128]{3,2,0,1:T(8,128)(2,1)}, bf16[8,2,1536,128]{3,2,0,1:T(8,128)(2,1)S(1)}, u32[]{:S(2)}) copy-start(bf16[8,2,1536,128]{3,2,0,1:T(8,128)(2,1)S(1)} %pad_maximum_fusion.2) | copy-start | bytes 18874372
  366.4 4.3 copy-start.45
  366.5 4.3 copy-start.61
  373.9 2.2 copy-start
  373.9 3.7 copy-start.59
  373.9 3.7 copy-start.65
  376.1 2.2 copy-start.52
  376.1 2.2 copy-start.53
  376.1 2.2 copy-start.58
  376.1 2.2 copy-start.64
  377.0 2.2 copy-start.46
  377.0 2.2 copy-start.47
  377.0 2.2 copy-start.48
  377.0 2.2 copy-start.49
  377.0 2.2 copy-start.50
  377.0 2.2 copy-start.51
  377.1 2.2 copy-start.63
  377.4 2.4 copy-start.17
  377.4 2.4 copy-start.62
  380.4 4.8 copy-start.24
  380.4 4.8 copy-start.25
  385.3 1.4 copy-start.19
  385.3 1.9 copy-start.20
  385.3 2.3 copy-start.21
  387.6 2.2 copy-start.5
  387.6 2.8 copy-start.6
  388.8 2.8 copy-start.4
  393.6 2.3 copy-start.10
  393.6 2.3 copy-start.12
  393.6 2.8 copy-start.14
  399.3 2.2 copy-start.66
  (14 other events, 15.4 us)
Sparse Core Ops, SparseCore 0:
  410.4 74.2 reduce-scatter.1
where the time goes:
time: 501 us; the launch traced here: 492 us
  matrix products  149 us (30%)
  other arithmetic  106 us (21%)
  local copies, waits for them, and re-layouts  106 us (21%)
  waiting for transfers between devices  104 us (21%)
  between operations  15.1 us (3%)
  starting transfers between devices  11.7 us (2%)
    reduce_scatter x1, waiting for transfers between devices, body(): lax.psum_scatter(jnp.dot(attended, out_weight, preferred_element_type=jnp...  74.5 us
    dot_general x7, matrix products, score_tile(): jnp.einsum('gqk,gkd->gqd', weights.astype(jnp.bfloat16), key_values[:, 1]...  72.4 us
    dot_general x7, matrix products, score_tile(): jnp.einsum('gqd,gkd->gqk', query_block, key_values[:, 0], preferred_eleme...  68.1 us
    reduce_sum x6, other arithmetic, score_tile(): row_total = jnp.sum(weights, axis=2)  64.5 us
    unnamed x174, local copies, waits for them, and re-layouts  35.2 us
    slice x12, local copies, waits for them, and re-layouts, halve(): odd = lax.index_in_dim(shaped, 1, axis + 1, keepdims=False)  34.4 us
    ppermute x10, waiting for transfers between devices, swapped(): return lax.ppermute(value, axis, pairs)  29.5 us
    concatenate x8, other arithmetic, body(): jnp.concatenate((block_rows, swapped(block_rows, 'seq', bit_index)), axis=2)  20.6 us
  transfers between devices with their start and end apart: 11, of which 3 were waited for; matrix products, arithmetic and copies ran while one was open for 61% of the time, Pallas kernels for 0%

commit v1 on v0

--- a/solution.py
+++ b/solution.py
@@ -1,15 +1,413 @@
+import functools
 import math
 
+import numpy as np
 import jax
 import jax.numpy as jnp
 from jax import lax
+from jax.experimental import pallas as pl
+from jax.experimental.pallas import tpu as pltpu
 from jax.sharding import PartitionSpec as P
+
+ROW_TILE = 16
+LOG2E = 1.4426950408889634
+MASKED = -1.0e30
+
+
+def bit_reverse(value, bits):
+    result = 0
+    for bit in range(bits):
+        result |= ((value >> bit) & 1) << (bits - 1 - bit)
+    return result
+
+
+def slot_class(slot, levels):
+    return levels - slot.bit_length()
 
 
 def swapped(value, axis, bit):
     mask = 2**bit
     pairs = [(source, source ^ mask) for source in range(lax.axis_size(axis))]
     return lax.ppermute(value, axis, pairs)
+
+
+def one_hot_order(size, stride, transposed):
+    rows = lax.broadcasted_iota(jnp.int32, (size, size), 0)
+    cols = lax.broadcasted_iota(jnp.int32, (size, size), 1)
+    if transposed:
+        rows, cols = cols, rows
+    inner = size // stride
+    match = (rows % inner) * stride + rows // inner == cols
+    return jnp.where(match, 1.0, 0.0).astype(jnp.bfloat16)
+
+
+def reorder_kernel(table, *refs, sources, groups, slots, cuts):
+    source_refs = refs[:sources]
+    out_refs = refs[sources:-1]
+    scratch = refs[-1]
+    size = source_refs[0].shape[0]
+    order = one_hot_order(size, slots, False)
+    for index in range(sources):
+        moved = jnp.dot(order, source_refs[index][...], preferred_element_type=jnp.float32)
+        scratch[index] = moved.astype(jnp.bfloat16).reshape(slots, ROW_TILE, moved.shape[1])
+    for head in range(groups):
+        for slot in range(slots):
+            residue = table[head, slot]
+            for index in range(sources):
+                piece = scratch[index, residue, :, head * 128 : (head + 1) * 128]
+                for out_ref, (low, high) in zip(out_refs, cuts):
+                    if low <= slot < high:
+                        out_ref[index, head, slot - low] = piece
+
+
+def reorder(table, arrays, slots, cuts):
+    rows, cols = arrays[0].shape
+    groups = cols // 128
+    size = slots * ROW_TILE
+    blocks = rows // size
+    inner = rows // slots
+    sources = len(arrays)
+    out_shape = [
+        jax.ShapeDtypeStruct((sources, groups, high - low, inner, 128), jnp.bfloat16)
+        for low, high in cuts
+    ]
+    total = sum(high - low for low, high in cuts)
+    return pl.pallas_call(
+        functools.partial(
+            reorder_kernel, sources=sources, groups=groups, slots=slots, cuts=cuts
+        ),
+        out_shape=out_shape,
+        grid_spec=pltpu.PrefetchScalarGridSpec(
+            num_scalar_prefetch=1,
+            grid=(blocks,),
+            in_specs=[pl.BlockSpec((size, cols), lambda b, t: (b, 0))] * sources,
+            out_specs=[
+                pl.BlockSpec(
+                    (sources, groups, high - low, ROW_TILE, 128), lambda b, t: (0, 0, 0, b, 0)
+                )
+                for low, high in cuts
+            ],
+            scratch_shapes=[pltpu.VMEM((sources, slots, ROW_TILE, cols), jnp.bfloat16)],
+        ),
+        compiler_params=pltpu.CompilerParams(vmem_limit_bytes=56 << 20),
+        cost_estimate=pl.CostEstimate(
+            flops=2 * sources * rows * size * cols,
+            transcendentals=0,
+            bytes_accessed=2 * sources * rows * cols + 2 * sources * groups * total * inner * 128,
+        ),
+        name="reorder",
+    )(table, *arrays)
+
+
+def attention_kernel(
+    own_x, q_ref, *refs, parts, tiles, has_bias, has_state, state_rows, owners, score_scale
+):
+    refs = list(refs)
+    kv_refs = [refs.pop(0) for _ in range(parts)]
+    bias_ref = refs.pop(0) if has_bias else None
+    state_in = [refs.pop(0) for _ in range(3)] if has_state else None
+    mine_ref = refs.pop(0)
+    theirs_ref = refs.pop(0)
+    state_out = [refs.pop(0) for _ in range(3)] if state_rows else None
+    out_scratch = refs.pop(0)
+
+    def joined(which):
+        pieces = [ref[which, 0] for ref in kv_refs]
+        pieces = [piece.reshape(-1, piece.shape[-1]) for piece in pieces]
+        return pieces[0] if len(pieces) == 1 else jnp.concatenate(pieces, axis=0)
+
+    keys = joined(0)
+    values = joined(1)
+    values = jnp.concatenate([values, jnp.ones_like(values)], axis=1)
+    factor = score_scale * LOG2E
+    slots, inner = q_ref.shape[1], q_ref.shape[2]
+    queries = q_ref[0].reshape(slots * inner, q_ref.shape[3])
+    for first, count, bias_row in tiles:
+        scores = lax.dot_general(
+            queries[first : first + count],
+            keys,
+            (((1,), (1,)), ((), ())),
+            preferred_element_type=jnp.float32,
+        )
+        if has_bias:
+            scores = scores * factor + bias_ref[bias_row : bias_row + 1, :]
+            peak = jnp.max(scores, axis=1, keepdims=True)
+            if has_state:
+                peak = jnp.maximum(peak, state_in[0][0, first : first + count, :1])
+            weights = jnp.exp2(scores - peak)
+        else:
+            peak = jnp.max(scores, axis=1, keepdims=True)
+            weights = jnp.exp2(scores * factor - peak * factor)
+        mixed = jnp.dot(weights.astype(jnp.bfloat16), values, preferred_element_type=jnp.float32)
+        value_sum = mixed[:, :128]
+        total = mixed[:, 128:]
+        if has_state:
+            keep = jnp.exp2(state_in[0][0, first : first + count, :] - peak)
+            value_sum = value_sum + keep * state_in[2][0, first : first + count, :]
+            total = total + keep * state_in[1][0, first : first + count, :]
+        if first < state_rows:
+            state_out[0][0, first : first + count, :] = jnp.broadcast_to(peak, (count, 128))
+            state_out[1][0, first : first + count, :] = total
+            state_out[2][0, first : first + count, :] = value_sum
+        else:
+            low = first - state_rows
+            out_scratch[low : low + count, :] = value_sum / total
+    share = inner // owners
+    me = own_x[0]
+    done = out_scratch.shape[0] // inner
+    for slot in range(done):
+        base = slot * inner
+        mine_start = pl.multiple_of(base + me * share, ROW_TILE)
+        mine_ref[0, slot] = out_scratch[pl.ds(mine_start, share), :].astype(jnp.bfloat16)
+        their_start = pl.multiple_of(base + (owners - 1 - me) * share, ROW_TILE)
+        theirs_ref[0, slot] = out_scratch[pl.ds(their_start, share), :].astype(jnp.bfloat16)
+
+
+def attention(own_x, queries, first_slot, parts, bias, state, state_rows, tiles, score_scale, name):
+    groups, all_slots, inner, width = queries.shape
+    slots = sum(count for _, count, _ in tiles) // inner
+    owners = 2
+    done = slots - state_rows // inner
+    in_specs = [
+        pl.BlockSpec((1, slots, inner, width), lambda h, x: (h, first_slot // slots, 0, 0))
+    ]
+    operands = [queries]
+    for part in parts:
+        in_specs.append(
+            pl.BlockSpec((2, 1) + part.shape[2:], lambda h, x: (0, h, 0, 0, 0))
+        )
+        operands.append(part)
+    key_count = sum(part.shape[2] * part.shape[3] for part in parts)
+    if bias is not None:
+        in_specs.append(pl.BlockSpec(bias.shape, lambda h, x: (0, 0)))
+        operands.append(bias)
+    if state is not None:
+        for item in state:
+            in_specs.append(pl.BlockSpec((1,) + item.shape[1:], lambda h, x: (h, 0, 0)))
+            operands.append(item)
+    share = inner // owners
+    out_shape = [jax.ShapeDtypeStruct((groups, done, share, width), jnp.bfloat16)] * 2
+    out_specs = [pl.BlockSpec((1, done, share, width), lambda h, x: (h, 0, 0, 0))] * 2
+    if state_rows:
+        out_shape += [jax.ShapeDtypeStruct((groups, state_rows, width), jnp.float32)] * 3
+        out_specs += [pl.BlockSpec((1, state_rows, width), lambda h, x: (h, 0, 0))] * 3
+    rows = slots * inner
+    return pl.pallas_call(
+        functools.partial(
+            attention_kernel,
+            parts=len(parts),
+            tiles=tiles,
+            has_bias=bias is not None,
+            has_state=state is not None,
+            state_rows=state_rows,
+            owners=owners,
+            score_scale=score_scale,
+        ),
+        out_shape=out_shape,
+        grid_spec=pltpu.PrefetchScalarGridSpec(
+            num_scalar_prefetch=1,
+            grid=(groups,),
+            in_specs=in_specs,
+            out_specs=out_specs,
+            scratch_shapes=[pltpu.VMEM((done * inner, width), jnp.float32)],
+        ),
+        compiler_params=pltpu.CompilerParams(vmem_limit_bytes=56 << 20),
+        cost_estimate=pl.CostEstimate(
+            flops=12 * groups * rows * key_count * width,
+            transcendentals=groups * rows * key_count,
+            bytes_accessed=4 * groups * width * (rows + key_count),
+        ),
+        name=name,
+    )(own_x, *operands)
+
+
+def project_kernel(table, own_core, *refs, slots, class_slots, groups, inner):
+    count = len(class_slots)
+    sources = [refs[:count], refs[count : 2 * count]]
+    own_weight, same_half, other_half, out_ref, by_slot, by_residue, moved = refs[2 * count :]
+    block = pl.program_id(0)
+    size = slots * ROW_TILE
+    half = groups // 2
+    for source in range(2):
+        for head in range(groups):
+            start = 0
+            for ref, taken in zip(sources[source], class_slots):
+                by_slot[head, start : start + taken] = ref[head]
+                start += taken
+            for residue in range(slots):
+                slot = table[source * groups + head, residue]
+                by_residue[source * 2 + head // half, residue, :, (head % half) * 128 : (head % half + 1) * 128] = by_slot[head, slot]
+    core = own_core[0]
+
+    def rows_of(index):
+        return by_residue[index].reshape(size, half * 128)
+
+    depth = half * 128
+    result = jnp.dot(rows_of(0), own_weight[:depth], preferred_element_type=jnp.float32)
+    result += jnp.dot(rows_of(1), own_weight[depth:], preferred_element_type=jnp.float32)
+    result += jnp.dot(rows_of(2 + core), same_half[...], preferred_element_type=jnp.float32)
+    result += jnp.dot(rows_of(3 - core), other_half[...], preferred_element_type=jnp.float32)
+    moved[...] = result.astype(jnp.bfloat16)
+    order = one_hot_order(size, slots, True)
+    out_ref[...] = jnp.dot(order, moved[...], preferred_element_type=jnp.float32).astype(
+        jnp.bfloat16
+    )
+
+
+def project(table, own_core, mine, received, own_weight, same_half, other_half, slots):
+    groups, _, share, width = mine[0].shape
+    rows = slots * share
+    size = slots * ROW_TILE
+    blocks = rows // size
+    cols = own_weight.shape[1]
+    class_slots = [item.shape[1] for item in mine]
+    attended_specs = [
+        pl.BlockSpec((groups, taken, ROW_TILE, width), lambda b, t, c: (0, 0, b, 0))
+        for taken in class_slots
+    ]
+    whole = lambda b, t, c: (0, 0)
+    return pl.pallas_call(
+        functools.partial(
+            project_kernel, slots=slots, class_slots=class_slots, groups=groups, inner=share
+        ),
+        out_shape=jax.ShapeDtypeStruct((rows, cols), jnp.bfloat16),
+        grid_spec=pltpu.PrefetchScalarGridSpec(
+            num_scalar_prefetch=2,
+            grid=(blocks,),
+            in_specs=attended_specs
+            + attended_specs
+            + [
+                pl.BlockSpec(own_weight.shape, whole, pipeline_mode=pl.Buffered(1)),
+                pl.BlockSpec(same_half.shape, whole, pipeline_mode=pl.Buffered(1)),
+                pl.BlockSpec(other_half.shape, whole, pipeline_mode=pl.Buffered(1)),
+            ],
+            out_specs=pl.BlockSpec((size, cols), lambda b, t, c: (b, 0)),
+            scratch_shapes=[
+                pltpu.VMEM((groups, slots, ROW_TILE, width), jnp.bfloat16),
+                pltpu.VMEM((4, slots, ROW_TILE, groups // 2 * width), jnp.bfloat16),
+                pltpu.VMEM((size, cols), jnp.bfloat16),
+            ],
+        ),
+        compiler_params=pltpu.CompilerParams(vmem_limit_bytes=56 << 20),
+        cost_estimate=pl.CostEstimate(
+            flops=2 * rows * 2 * groups * width * cols,
+            transcendentals=0,
+            bytes_accessed=2 * (4 * groups * width * cols // 2 + rows * cols + rows * 2 * groups * width),
+        ),
+        name="project",
+    )(table, own_core, *mine, *received, own_weight, same_half, other_half)
+
+
+def bias_rows(query_classes, parts, levels, inner):
+    rows = []
+    for query_class in query_classes:
+        row = []
+        for low, high, distance in parts:
+            for slot in range(low, high):
+                shared = min(query_class, slot_class(slot, levels)) - distance + 1
+                row += [math.log2(shared) if shared > 0 else MASKED] * inner
+        rows.append(row)
+    return jnp.asarray(np.array(rows, np.float32))
+
+
+def fast_body(query_rows, key_rows, value_rows, head_phase, out_weight):
+    shards = lax.axis_size("seq")
+    levels = shards.bit_length() - 1
+    groups = head_phase.shape[0]
+    rows = query_rows.shape[0]
+    inner = rows // shards
+    slots = shards
+    score_scale = 1.0 / math.sqrt(query_rows.shape[1] // groups)
+    own_x = lax.axis_index("head").reshape(1)
+    own_core = (lax.axis_index("seq") % 2).reshape(1)
+    reversed_bits = jnp.asarray([bit_reverse(slot, levels) for slot in range(slots)], jnp.int32)
+    phase = head_phase % shards
+    residue_table = reversed_bits[None, :] ^ phase[:, None]
+    other_phase = swapped(phase, "head", 0)
+
+    half_rows = out_weight.shape[0] // 2
+    half_weight = lax.dynamic_slice_in_dim(out_weight, own_core[0] * half_rows, half_rows, 0)
+    cuts = [(slots // 2, slots)] + [(0, slots >> level) for level in range(1, levels + 1)]
+    ordered = reorder(residue_table, [key_rows, value_rows], slots, cuts)
+    first_class, prefixes = ordered[0], ordered[1:]
+    same_half = swapped(half_weight, "head", 0)
+    queries = reorder(residue_table, [query_rows], slots, [(0, slots)])[0][0]
+
+    remote = []
+    for level in range(1, levels + 1):
+        pieces = [swapped(prefixes[level - 1], "seq", level - 1)]
+        for bit in range(level - 2, -1, -1):
+            pieces = pieces + [swapped(piece, "seq", bit) for piece in pieces]
+        remote.append(pieces)
+    other_half = swapped(same_half, "seq", 0)
+
+    own = [prefixes[0], first_class]
+    own_parts = [(0, slots, 0)]
+
+    def remote_parts(level):
+        return [(0, slots >> level, level)] * (2 ** (level - 1))
+
+    mine, theirs = [], []
+    count = slots // 2 * inner
+    tile = 256
+    tiles = [(first, tile, 0) for first in range(0, count, tile)]
+    out = attention(own_x, queries, slots // 2, own, None, None, 0, tiles, score_scale, "class0")
+    mine.append(out[0])
+    theirs.append(out[1])
+    count = slots // 4 * inner
+    tile = 192
+    bias = bias_rows([1], own_parts + remote_parts(1), levels, inner)
+    tiles = [(first, tile, 0) for first in range(0, count, tile)]
+    out = attention(
+        own_x, queries, slots // 4, own + remote[0], bias, None, 0, tiles, score_scale, "class1"
+    )
+    mine.append(out[0])
+    theirs.append(out[1])
+    late = 2 * inner
+    tiles = [(0, inner, 0), (inner, inner, 1), (2 * inner, 2 * inner, 2)]
+    bias = bias_rows(
+        [levels, levels - 1, levels - 2],
+        own_parts + remote_parts(1) + remote_parts(2),
+        levels,
+        inner,
+    )
+    out = attention(
+        own_x,
+        queries,
+        0,
+        own + remote[0] + remote[1],
+        bias,
+        None,
+        late,
+        tiles,
+        score_scale,
+        "class2",
+    )
+    mine.append(out[0])
+    theirs.append(out[1])
+    state = out[2:]
+    tiles = [(0, inner, 0), (inner, inner, 1)]
+    bias = bias_rows([levels, levels - 1], remote_parts(3) + remote_parts(4), levels, inner)
+    out = attention(
+        own_x, queries, 0, remote[2] + remote[3], bias, state, 0, tiles, score_scale, "class3"
+    )
+    mine.append(out[0])
+    theirs.append(out[1])
+
+    received = [swapped(item, "head", 0) for item in theirs]
+    phases = jnp.concatenate([phase, other_phase])
+    inverse = reversed_bits
+    slot_table = inverse[jnp.arange(slots, dtype=jnp.int32)[None, :] ^ phases[:, None]]
+    return project(
+        slot_table,
+        own_core,
+        mine[::-1],
+        received[::-1],
+        out_weight,
+        same_half,
+        other_half,
+        slots,
+    )
 
 
 def halve(block, parity, axis):
@@ -62,7 +460,7 @@
     return score_tile(queries)
 
 
-def body(query_rows, key_rows, value_rows, head_phase, out_weight):
+def any_body(query_rows, key_rows, value_rows, head_phase, out_weight):
     groups = head_phase.shape[0]
     head_width = query_rows.shape[1] // groups
     levels = lax.axis_size("seq").bit_length() - 1
@@ -126,4 +524,12 @@
 def solution(mesh):
     in_specs = (P("seq", "head"), P("seq", "head"), P("seq", "head"), P("head"), P("head", None))
     out_specs = P(("seq", "head"), None)
+
+    def body(query_rows, *others):
+        shards = mesh.shape["seq"]
+        inner = query_rows.shape[0] // shards
+        if shards == 16 and mesh.shape["head"] == 2 and inner % (2 * ROW_TILE) == 0:
+            return fast_body(query_rows, *others)
+        return any_body(query_rows, *others)
+
     return jax.shard_map(body, mesh=mesh, in_specs=in_specs, out_specs=out_specs, check_vma=False)

time: 501 us -> 183 us (0.37); the launches traced: 492 us -> 182 us
  matrix products: 149 us -> 0 us
  other arithmetic: 106 us -> 2.14 us
  local copies, waits for them, and re-layouts: 106 us -> 6.98 us
  Pallas kernels: 0 us -> 98.2 us
  waiting for transfers between devices: 104 us -> 54.8 us
  between operations: 15.1 us -> 0.18 us
  starting transfers between devices: 11.7 us -> 20 us
    dot_general x15 -> x0, matrix products: 149 us -> none  [the longest x7 72.4 us: score_tile(): jnp.einsum('gqk,gkd->gqd', weights.astype(jnp.bfloat16), key_values[:, 1]...]
    pallas_call x0 -> x7, Pallas kernels: none -> 98.2 us  [the longest x4 67 us: attention(): pl.pallas_call(functools.partial(attention_kernel, parts=len(parts), tile...]
    reduce_scatter x1 -> x0, waiting for transfers between devices: 74.5 us -> none  [body(): lax.psum_scatter(jnp.dot(attended, out_weight, preferred_element_type=jnp...]
    reduce_sum x6 -> x0, other arithmetic: 64.5 us -> none  [score_tile(): row_total = jnp.sum(weights, axis=2)]
    slice x19 -> x0, local copies, waits for them, and re-layouts: 39 us -> none  [the longest x12 34.4 us: halve(): odd = lax.index_in_dim(shaped, 1, axis + 1, keepdims=False)]
    unnamed x174 -> x36, local copies, waits for them, and re-layouts: 35.2 us -> 2.63 us
    ppermute x10 -> x22, waiting for transfers between devices: 29.5 us -> 54.8 us  [swapped(): return lax.ppermute(value, axis, pairs)]
    concatenate x11 -> x1, other arithmetic: 24.9 us -> 0.08 us  [fast_body(): phases = jnp.concatenate([phase, other_phase])]
  transfers between devices with their start and end apart: 11 -> 22, of which waited for: 3 -> 6; matrix products, arithmetic and copies ran while one was open for 61% -> 2% of each run, Pallas kernels for 0% -> 41%
where the time goes in v1:
time: 183 us; the launch traced here: 182 us
  Pallas kernels  98.2 us (54%)
  waiting for transfers between devices  54.8 us (30%)
  starting transfers between devices  20 us (11%)
  local copies, waits for them, and re-layouts  6.98 us (4%)
  other arithmetic  2.14 us (1%)
    pallas_call x4, Pallas kernels, attention(): pl.pallas_call(functools.partial(attention_kernel, parts=len(parts), tile...  67 us
    ppermute x22, waiting for transfers between devices, swapped(): return lax.ppermute(value, axis, pairs)  54.8 us
    ppermute x22, starting transfers between devices, swapped(): return lax.ppermute(value, axis, pairs)  20 us
    pallas_call x2, Pallas kernels, reorder(): pl.pallas_call(functools.partial(reorder_kernel, sources=sources, groups=...  17 us
    pallas_call x1, Pallas kernels, project(): pl.pallas_call(functools.partial(project_kernel, slots=slots, class_slots...  14.2 us
  transfers between devices with their start and end apart: 22, of which 6 were waited for; matrix products, arithmetic and copies ran while one was open for 2% of the time, Pallas kernels for 41%

profile of v1, /device:TPU:0, one launch (start us, length us, event | category | flops | bytes accessed | tf_op | source)
XLA Modules:
  0.0 182.3 jit_solution(10917235708770456977)
XLA Ops:
  0.0 0.7 and_select_fusion
  0.7 1.3 broadcast_xor_fusion.table
  2.0 9.9 %reorder.3 = (bf16[2,8,8,96,128]{4,3,2,1,0:T(8,128)(2,1)}, bf16[2,8,8,96,128]{4,3,2,1,0:T(8,128)(2,1)}, bf16[2,8,4,96,128]{4,3,2,1,0:T(8,128)(2,1)}, bf16[2,8,2,...) custom-call(s32[8,16]{1,0:T(8,128)} %broadcast_xor_fusion.table, bf16[1536,1024]{1,0:T(8,128)(2,1)} %refs_0_.3, ...), custom_call_target="tpu_custom_call" | custom-call | flops 1610612736 | bytes 15335424 | tf_op jit(solution)/shard_map/reorder/pallas_call | solution.py:75
  11.9 0.5 collective-permute-start.13
  12.4 2.6 %collective-permute-start.14 = (bf16[2,8,4,96,128]{4,3,2,1,0:T(8,128)(2,1)}, bf16[2,8,4,96,128]{4,3,2,1,0:T(8,128)(2,1)}, u32[]{:S(2)}, u32[]{:S(2)}) collective-permute-start(bf16[2,8,4,96,128]{4,3,2,1,0:T(8,128)(2,1)} %get-tuple-element.25), channel_id=1, source_target_pairs={{0,4},{2,6},{4,0},{6,2},{8,12},{10,14},{12,8},{14,10},{16,20},{18,... | collective-permute-start | bytes 4718600 | tf_op jit(solution)/shard_map/ppermute | solution.py:31
  15.0 2.6 %collective-permute-start.5 = (bf16[2,8,1,96,128]{4,3,2,1,0:T(8,128)(2,1)}, bf16[2,8,1,96,128]{4,3,2,1,0:T(8,128)(2,1)S(1)}, u32[]{:S(2)}, u32[]{:S(2)}) collective-permute-start(bf16[2,8,1,96,128]{4,3,2,1,0:T(8,128)(2,1)} %get-tuple-element.22), channel_id=1, source_target_pairs={{0,16},{2,18},{4,20},{6,22},{8,24},{10,26},{12,28},{14,30},{16,0},... | collective-permute-start | bytes 1179656 | tf_op jit(solution)/shard_map/ppermute | solution.py:31
  17.6 1.7 constant_dynamic-slice_fusion
  19.3 1.6 collective-permute-start.20
  20.9 14.8 %collective-permute-done.5.refs_4_ = bf16[2,8,1,96,128]{4,3,2,1,0:T(8,128)(2,1)S(1)} collective-permute-done((bf16[2,8,1,96,128]{4,3,2,1,0:T(8,128)(2,1)}, bf16[2,8,1,96,128]{4,3,2,1,0:T(8,128)(2,1)S(1)}, u32[]{:S(2)}, u32[]{:S(2)}) %collective-permute-start.5) | collective-permute-done | bytes 393248 | tf_op jit(solution)/shard_map/ppermute | solution.py:31
  35.7 0.8 collective-permute-start.6
  36.5 1.5 collective-permute-start
  38.0 28.9 %collective-permute-done = s32[8]{0:T(128)S(1)} collective-permute-done((s32[8]{0:T(128)S(1)}, s32[8]{0:T(128)S(1)}, u32[]{:S(2)}, u32[]{:S(2)}) %collective-permute-start) | collective-permute-done | bytes 64 | tf_op jit(solution)/shard_map/ppermute | solution.py:31
  66.9 0.5 collective-permute-start.7
  67.4 0.0 collective-permute-done.14.refs_3_
  67.4 0.0 collective-permute-start.15
  67.4 7.1 %reorder.2 = bf16[1,8,16,96,128]{4,3,2,1,0:T(8,128)(2,1)} custom-call(s32[8,16]{1,0:T(8,128)} %broadcast_xor_fusion.table, bf16[1536,1024]{1,0:T(8,128)(2,1)} %refs_0_.2), custom_call_target="tpu_custom_call" | custom-call | flops 805306368 | bytes 6291456 | tf_op jit(solution)/shard_map/reorder/pallas_call | solution.py:75
  74.5 0.0 collective-permute-done.6.refs_5_
  74.5 1.6 collective-permute-start.1
  76.2 0.8 collective-permute-done.7.refs_6_
  76.9 0.0 collective-permute-start.9
  76.9 18.8 %class0.1 = (bf16[8,8,48,128]{3,2,1,0:T(8,128)(2,1)}, bf16[8,8,48,128]{3,2,1,0:T(8,128)(2,1)}) custom-call(s32[1]{0:T(128)} %bitcast.1.own_x, bf16[8,16,96,128]{3,2,1,0:T(8,128)(2,1)} %bitcast.5, bf16[2,8,8,96,128]{4,3,2,1,0:T(8,128)(2,1)} %get-tuple-element.23.refs_0_, bf16[2,8,8,96,128]{4,3,2,1,0:T(8,128)(2,1)} %get-tuple-element.24.refs_1_), custom_call_target="tpu_custom_call" | custom-call | flops 14495514624 | bytes 9437184 | tf_op jit(solution)/shard_map/class0/pallas_call | solution.py:195
  95.8 0.1 pad_add_fusion
  95.9 0.0 collective-permute-done.1.refs_0_
  95.9 0.9 collective-permute-start.8
  96.8 0.0 collective-permute-done.9.refs_8_
  96.8 0.0 collective-permute-start.10
  96.8 0.0 collective-permute-done.20.refs_9_
  96.8 0.5 collective-permute-start.11
  97.3 0.0 collective-permute-done.13.refs_2_
  97.3 1.1 collective-permute-start.2
  98.5 0.0 collective-permute-done.15.refs_4_
  98.5 0.0 collective-permute-start.21
  98.5 20.0 %class2.1 = (bf16[8,2,48,128]{3,2,1,0:T(8,128)(2,1)}, bf16[8,2,48,128]{3,2,1,0:T(8,128)(2,1)}, f32[8,192,128]{2,1,0:T(8,128)}, f32[8,192,128]{2,1,0:T(8,128)}, f32[8,192,128]{2,1,0:T(8,128)}) custom-call(s32[1]{0:T(128)} %bitcast.1.own_x, bf16[8,16,96,128]{3,2,1,0:T(8,128)(2,1)} %bitcast.6, bf16[2,8,8,96,128]{4,3,2,1,0:T(8,128)(2,1)} %get-tuple-element.23.refs_0_, ...), custom_call_target="tpu_custom_call" | custom-call | flops 14495514624 | bytes 14155776 | tf_op jit(solution)/shard_map/class2/pallas_call | solution.py:195
  118.5 0.0 collective-permute-done.8.refs_7_
  118.5 1.6 collective-permute-start.19
  120.1 0.0 collective-permute-done.10.refs_9_
  120.1 0.3 collective-permute-start.3
  120.4 0.0 collective-permute-done.11.refs_10_
  120.4 0.3 collective-permute-start.12
  120.7 3.7 %collective-permute-done.2.refs_1_ = bf16[2,8,2,96,128]{4,3,2,1,0:T(8,128)(2,1)S(1)} collective-permute-done((bf16[2,8,2,96,128]{4,3,2,1,0:T(8,128)(2,1)S(1)}, bf16[2,8,2,96,128]{4,3,2,1,0:T(8,128)(2,1)S(1)}, u32[]{:S(2)}, u32[]{:S(2)}) %collective-permute-start.2) | collective-permute-done | bytes 786464 | tf_op jit(solution)/shard_map/ppermute | solution.py:31
  124.4 0.0 collective-permute-start.4
  124.4 16.9 %class1.1 = (bf16[8,4,48,128]{3,2,1,0:T(8,128)(2,1)}, bf16[8,4,48,128]{3,2,1,0:T(8,128)(2,1)}) custom-call(s32[1]{0:T(128)} %bitcast.1.own_x, bf16[8,16,96,128]{3,2,1,0:T(8,128)(2,1)} %bitcast.7, bf16[2,8,8,96,128]{4,3,2,1,0:T(8,128)(2,1)} %get-tuple-element.23.refs_0_, bf16[2,8,8,96,128]{4,3,2,1,0:T(8,128)(2,1)} %get-tuple-element.24.refs_1_, ...), custom_call_target="tpu_custom_call" | custom-call | flops 10871635968 | bytes 11010048 | tf_op jit(solution)/shard_map/class1/pallas_call | solution.py:195
  141.3 0.0 collective-permute-done.12.refs_11_
  141.3 1.6 collective-permute-start.18
  142.9 0.0 collective-permute-done.3.refs_2_
  142.9 0.0 collective-permute-done.4.refs_3_
  142.9 0.9 copy-done.6
  143.8 0.3 copy-done.7
  144.0 11.3 %class3.1 = (bf16[8,2,48,128]{3,2,1,0:T(8,128)(2,1)}, bf16[8,2,48,128]{3,2,1,0:T(8,128)(2,1)}) custom-call(s32[1]{0:T(128)} %bitcast.1.own_x, bf16[8,16,96,128]{3,2,1,0:T(8,128)(2,1)} %bitcast.8, bf16[2,8,2,96,128]{4,3,2,1,0:T(8,128)(2,1)} %copy-done.3, bf16[2,8,2,96,128]{4,3,2,1,0:T(8,128)(2,1)} %copy-done.5, bf16[2,8,2,96,128]{4,3,2,1,0:T(8,128)(2,1)} %copy-done.6, ...), custom_call_target="tpu_custom_call" | custom-call | flops 3623878656 | bytes 7077888 | tf_op jit(solution)/shard_map/class3/pallas_call | solution.py:195
  155.4 0.0 copy-start
  155.4 0.6 collective-permute-start.16
  156.0 1.5 collective-permute-start.17
  157.5 0.1 compare_select_fusion
  157.5 0.1 reshape.52
  157.6 1.9 %gather_fusion = s32[256]{0:T(256)S(1)} fusion(s32[16]{0:T(128)S(1)} %copy-done, s32[1024]{0:T(1024)S(1)} %pad_clamp_fusion), kind=kCustom, calls=%fused_computation | custom fusion | bytes 3072 | tf_op jit(solution)/shard_map/gather | solution.py:400
  159.5 0.7 reshape.51.table
  160.2 0.0 collective-permute-done.19.refs_7_
  160.2 3.3 %collective-permute-done.16.refs_4_ = bf16[8,2,48,128]{3,2,1,0:T(8,128)(2,1)} collective-permute-done((bf16[8,2,48,128]{3,2,1,0:T(8,128)(2,1)}, bf16[8,2,48,128]{3,2,1,0:T(8,128)(2,1)}, u32[]{:S(2)}, u32[]{:S(2)}) %collective-permute-start.16) | collective-permute-done | bytes 196640 | tf_op jit(solution)/shard_map/ppermute | solution.py:31
  163.5 3.2 %collective-permute-done.17.refs_5_ = bf16[8,2,48,128]{3,2,1,0:T(8,128)(2,1)} collective-permute-done((bf16[8,2,48,128]{3,2,1,0:T(8,128)(2,1)S(1)}, bf16[8,2,48,128]{3,2,1,0:T(8,128)(2,1)}, u32[]{:S(2)}, u32[]{:S(2)}) %collective-permute-start.17) | collective-permute-done | bytes 196640 | tf_op jit(solution)/shard_map/ppermute | solution.py:31
  166.7 0.0 collective-permute-done.18.refs_6_
  166.7 0.0 collective-permute-done.21.refs_10_
  166.7 0.7 copy-done.15
  167.5 0.7 copy-done.1
  168.2 14.2 %project.1 = bf16[768,2048]{1,0:T(8,128)(2,1)} custom-call(s32[16,16]{1,0:T(8,128)} %reshape.51.table, s32[1]{0:T(128)} %bitcast.own_core, bf16[8,2,48,128]{3,2,1,0:T(8,128)(2,1)} %get-tuple-element.29.refs_0_, bf16[8,2,48,128]{3,2,1,0:T(8,128)(2,1)} %get-tuple-element.30.refs_1_, bf16[8,4,48,128]{3,2,1,0:T(8,128)(2,1)} %get-tuple-element.31.refs_2_, ...), custom_call_target="tpu_custom_call" | custom-call | flops 6442450944 | bytes 14680064 | tf_op jit(solution)/shard_map/project/pallas_call | solution.py:269
  (32 shorter events, 0.1 us)
Async XLA Ops:
  11.9 85.4 %collective-permute-start.13 = (bf16[2,8,8,96,128]{4,3,2,1,0:T(8,128)(2,1)}, bf16[2,8,8,96,128]{4,3,2,1,0:T(8,128)(2,1)}, u32[]{:S(2)}, u32[]{:S(2)}) collective-permute-start(bf16[2,8,8,96,128]{4,3,2,1,0:T(8,128)(2,1)} %get-tuple-element.23.refs_0_), channel_id=1, source_target_pairs={{0,2},{2,0},{4,6},{6,4},{8,10},{10,8},{12,14},{14,12},{16,18},{18,... | collective-permute-start | bytes 9437192 | tf_op jit(solution)/shard_map/ppermute | solution.py:31
  12.4 55.0 %collective-permute-start.14 = (bf16[2,8,4,96,128]{4,3,2,1,0:T(8,128)(2,1)}, bf16[2,8,4,96,128]{4,3,2,1,0:T(8,128)(2,1)}, u32[]{:S(2)}, u32[]{:S(2)}) collective-permute-start(bf16[2,8,4,96,128]{4,3,2,1,0:T(8,128)(2,1)} %get-tuple-element.25), channel_id=1, source_target_pairs={{0,4},{2,6},{4,0},{6,2},{8,12},{10,14},{12,8},{14,10},{16,20},{18,... | collective-permute-start | bytes 4718600 | tf_op jit(solution)/shard_map/ppermute | solution.py:31
  15.0 20.7 %collective-permute-start.5 = (bf16[2,8,1,96,128]{4,3,2,1,0:T(8,128)(2,1)}, bf16[2,8,1,96,128]{4,3,2,1,0:T(8,128)(2,1)S(1)}, u32[]{:S(2)}, u32[]{:S(2)}) collective-permute-start(bf16[2,8,1,96,128]{4,3,2,1,0:T(8,128)(2,1)} %get-tuple-element.22), channel_id=1, source_target_pairs={{0,16},{2,18},{4,20},{6,22},{8,24},{10,26},{12,28},{14,30},{16,0},... | collective-permute-start | bytes 1179656 | tf_op jit(solution)/shard_map/ppermute | solution.py:31
  19.3 77.5 %collective-permute-start.20 = (bf16[512,2048]{1,0:T(8,128)(2,1)S(1)}, bf16[512,2048]{1,0:T(8,128)(2,1)}, u32[]{:S(2)}, u32[]{:S(2)}) collective-permute-start(bf16[512,2048]{1,0:T(8,128)(2,1)S(1)} %constant_dynamic-slice_fusion), channel_id=1, source_target_pairs={{0,1},{1,0},{2,3},{3,2},{4,5},{5,4},{6,7},{7,6},{8,9},{9,8},{10,11... | collective-permute-start | bytes 6291464 | tf_op jit(solution)/shard_map/ppermute | solution.py:31
  35.7 41.2 %copy-start.8 = (bf16[2,8,1,96,128]{4,3,2,1,0:T(8,128)(2,1)}, bf16[2,8,1,96,128]{4,3,2,1,0:T(8,128)(2,1)S(1)}, u32[]{:S(2)}) copy-start(bf16[2,8,1,96,128]{4,3,2,1,0:T(8,128)(2,1)S(1)} %collective-permute-done.5.refs_4_) | copy-start | bytes 1179652
  35.7 38.8 %collective-permute-start.6 = (bf16[2,8,1,96,128]{4,3,2,1,0:T(8,128)(2,1)S(1)}, bf16[2,8,1,96,128]{4,3,2,1,0:T(8,128)(2,1)S(1)}, u32[]{:S(2)}, u32[]{:S(2)}) collective-permute-start(bf16[2,8,1,96,128]{4,3,2,1,0:T(8,128)(2,1)S(1)} %collective-permute-done.5.refs_4_), channel_id=1, source_target_pairs={{0,8},{2,10},{4,12},{6,14},{8,0},{10,2},{12,4},{14,6},{16,24},{18,... | collective-permute-start | bytes 1179656 | tf_op jit(solution)/shard_map/ppermute | solution.py:31
  36.5 30.4 %collective-permute-start = (s32[8]{0:T(128)S(1)}, s32[8]{0:T(128)S(1)}, u32[]{:S(2)}, u32[]{:S(2)}) collective-permute-start(s32[8]{0:T(128)S(1)} %and_select_fusion), channel_id=1, source_target_pairs={{0,1},{1,0},{2,3},{3,2},{4,5},{5,4},{6,7},{7,6},{8,9},{9,8},{10,11... | collective-permute-start | bytes 104 | tf_op jit(solution)/shard_map/ppermute | solution.py:31
  66.9 10.0 %collective-permute-start.7 = (bf16[2,8,1,96,128]{4,3,2,1,0:T(8,128)(2,1)S(1)}, bf16[2,8,1,96,128]{4,3,2,1,0:T(8,128)(2,1)S(1)}, u32[]{:S(2)}, u32[]{:S(2)}) collective-permute-start(bf16[2,8,1,96,128]{4,3,2,1,0:T(8,128)(2,1)S(1)} %collective-permute-done.5.refs_4_), channel_id=1, source_target_pairs={{0,4},{2,6},{4,0},{6,2},{8,12},{10,14},{12,8},{14,10},{16,20},{18,... | collective-permute-start | bytes 1179656 | tf_op jit(solution)/shard_map/ppermute | solution.py:31
  67.4 31.1 %collective-permute-start.15 = (bf16[2,8,4,96,128]{4,3,2,1,0:T(8,128)(2,1)}, bf16[2,8,4,96,128]{4,3,2,1,0:T(8,128)(2,1)}, u32[]{:S(2)}, u32[]{:S(2)}) collective-permute-start(bf16[2,8,4,96,128]{4,3,2,1,0:T(8,128)(2,1)} %collective-permute-done.14.refs_3_), channel_id=1, source_target_pairs={{0,2},{2,0},{4,6},{6,4},{8,10},{10,8},{12,14},{14,12},{16,18},{18,... | collective-permute-start | bytes 4718600 | tf_op jit(solution)/shard_map/ppermute | solution.py:31
  67.4 7.1 %copy-start.4 = (bf16[2,8,2,96,128]{4,3,2,1,0:T(8,128)(2,1)S(1)}, bf16[2,8,2,96,128]{4,3,2,1,0:T(8,128)(2,1)}, u32[]{:S(2)}) copy-start(bf16[2,8,2,96,128]{4,3,2,1,0:T(8,128)(2,1)} %get-tuple-element.21) | copy-start | bytes 2359300
  74.5 21.2 %copy-start.9 = (bf16[2,8,1,96,128]{4,3,2,1,0:T(8,128)(2,1)}, bf16[2,8,1,96,128]{4,3,2,1,0:T(8,128)(2,1)S(1)}, u32[]{:S(2)}) copy-start(bf16[2,8,1,96,128]{4,3,2,1,0:T(8,128)(2,1)S(1)} %collective-permute-done.6.refs_5_) | copy-start | bytes 1179652
  74.5 21.3 %collective-permute-start.1 = (bf16[2,8,2,96,128]{4,3,2,1,0:T(8,128)(2,1)S(1)}, bf16[2,8,2,96,128]{4,3,2,1,0:T(8,128)(2,1)S(1)}, u32[]{:S(2)}, u32[]{:S(2)}) collective-permute-start(bf16[2,8,2,96,128]{4,3,2,1,0:T(8,128)(2,1)S(1)} %copy-done.4), channel_id=1, source_target_pairs={{0,8},{2,10},{4,12},{6,14},{8,0},{10,2},{12,4},{14,6},{16,24},{18,... | collective-permute-start | bytes 2359304 | tf_op jit(solution)/shard_map/ppermute | solution.py:31
  76.9 18.8 %copy-start.10 = (bf16[2,8,1,96,128]{4,3,2,1,0:T(8,128)(2,1)}, bf16[2,8,1,96,128]{4,3,2,1,0:T(8,128)(2,1)S(1)}, u32[]{:S(2)}) copy-start(bf16[2,8,1,96,128]{4,3,2,1,0:T(8,128)(2,1)S(1)} %collective-permute-done.7.refs_6_) | copy-start | bytes 1179652
  76.9 19.9 %collective-permute-start.9 = (bf16[2,8,1,96,128]{4,3,2,1,0:T(8,128)(2,1)S(1)}, bf16[2,8,1,96,128]{4,3,2,1,0:T(8,128)(2,1)S(1)}, u32[]{:S(2)}, u32[]{:S(2)}) collective-permute-start(bf16[2,8,1,96,128]{4,3,2,1,0:T(8,128)(2,1)S(1)} %collective-permute-done.5.refs_4_), channel_id=1, source_target_pairs={{0,2},{2,0},{4,6},{6,4},{8,10},{10,8},{12,14},{14,12},{16,18},{18,... | collective-permute-start | bytes 1179656 | tf_op jit(solution)/shard_map/ppermute | solution.py:31
  95.9 22.7 %copy-start.2 = (bf16[8,8,48,128]{3,2,1,0:T(8,128)(2,1)S(1)}, bf16[8,8,48,128]{3,2,1,0:T(8,128)(2,1)}, u32[]{:S(2)}) copy-start(bf16[8,8,48,128]{3,2,1,0:T(8,128)(2,1)} %get-tuple-element.36) | copy-start | bytes 2359300
  95.9 24.2 %copy-start.3 = (bf16[2,8,2,96,128]{4,3,2,1,0:T(8,128)(2,1)}, bf16[2,8,2,96,128]{4,3,2,1,0:T(8,128)(2,1)S(1)}, u32[]{:S(2)}) copy-start(bf16[2,8,2,96,128]{4,3,2,1,0:T(8,128)(2,1)S(1)} %collective-permute-done.1.refs_0_) | copy-start | bytes 2359300
  95.9 22.6 %collective-permute-start.8 = (bf16[2,8,1,96,128]{4,3,2,1,0:T(8,128)(2,1)}, bf16[2,8,1,96,128]{4,3,2,1,0:T(8,128)(2,1)S(1)}, u32[]{:S(2)}, u32[]{:S(2)}) collective-permute-start(bf16[2,8,1,96,128]{4,3,2,1,0:T(8,128)(2,1)} %copy-done.9), channel_id=1, source_target_pairs={{0,4},{2,6},{4,0},{6,2},{8,12},{10,14},{12,8},{14,10},{16,20},{18,... | collective-permute-start | bytes 1179656 | tf_op jit(solution)/shard_map/ppermute | solution.py:31
  96.8 21.7 %copy-start.11 = (bf16[2,8,1,96,128]{4,3,2,1,0:T(8,128)(2,1)}, bf16[2,8,1,96,128]{4,3,2,1,0:T(8,128)(2,1)S(1)}, u32[]{:S(2)}) copy-start(bf16[2,8,1,96,128]{4,3,2,1,0:T(8,128)(2,1)S(1)} %collective-permute-done.9.refs_8_) | copy-start | bytes 1179652
  96.8 23.3 %collective-permute-start.10 = (bf16[2,8,1,96,128]{4,3,2,1,0:T(8,128)(2,1)}, bf16[2,8,1,96,128]{4,3,2,1,0:T(8,128)(2,1)S(1)}, u32[]{:S(2)}, u32[]{:S(2)}) collective-permute-start(bf16[2,8,1,96,128]{4,3,2,1,0:T(8,128)(2,1)} %copy-done.9), channel_id=1, source_target_pairs={{0,2},{2,0},{4,6},{6,4},{8,10},{10,8},{12,14},{14,12},{16,18},{18,... | collective-permute-start | bytes 1179656 | tf_op jit(solution)/shard_map/ppermute | solution.py:31
  96.8 23.5 %collective-permute-start.11 = (bf16[2,8,1,96,128]{4,3,2,1,0:T(8,128)(2,1)}, bf16[2,8,1,96,128]{4,3,2,1,0:T(8,128)(2,1)S(1)}, u32[]{:S(2)}, u32[]{:S(2)}) collective-permute-start(bf16[2,8,1,96,128]{4,3,2,1,0:T(8,128)(2,1)} %copy-done.10), channel_id=1, source_target_pairs={{0,2},{2,0},{4,6},{6,4},{8,10},{10,8},{12,14},{14,12},{16,18},{18,... | collective-permute-start | bytes 1179656 | tf_op jit(solution)/shard_map/ppermute | solution.py:31
  97.3 27.0 %collective-permute-start.2 = (bf16[2,8,2,96,128]{4,3,2,1,0:T(8,128)(2,1)S(1)}, bf16[2,8,2,96,128]{4,3,2,1,0:T(8,128)(2,1)S(1)}, u32[]{:S(2)}, u32[]{:S(2)}) collective-permute-start(bf16[2,8,2,96,128]{4,3,2,1,0:T(8,128)(2,1)S(1)} %collective-permute-done.1.refs_0_), channel_id=1, source_target_pairs={{0,4},{2,6},{4,0},{6,2},{8,12},{10,14},{12,8},{14,10},{16,20},{18,... | collective-permute-start | bytes 2359304 | tf_op jit(solution)/shard_map/ppermute | solution.py:31
  98.5 68.2 %collective-permute-start.21 = (bf16[512,2048]{1,0:T(8,128)(2,1)}, bf16[512,2048]{1,0:T(8,128)(2,1)S(1)}, u32[]{:S(2)}, u32[]{:S(2)}) collective-permute-start(bf16[512,2048]{1,0:T(8,128)(2,1)} %collective-permute-done.20.refs_9_), channel_id=1, source_target_pairs={{0,2},{2,0},{4,6},{6,4},{8,10},{10,8},{12,14},{14,12},{16,18},{18,... | collective-permute-start | bytes 6291464 | tf_op jit(solution)/shard_map/ppermute | solution.py:31
  118.5 22.8 %copy-start.12 = (bf16[2,8,1,96,128]{4,3,2,1,0:T(8,128)(2,1)}, bf16[2,8,1,96,128]{4,3,2,1,0:T(8,128)(2,1)S(1)}, u32[]{:S(2)}) copy-start(bf16[2,8,1,96,128]{4,3,2,1,0:T(8,128)(2,1)S(1)} %collective-permute-done.8.refs_7_) | copy-start | bytes 1179652
  118.5 41.7 %collective-permute-start.19 = (bf16[8,8,48,128]{3,2,1,0:T(8,128)(2,1)S(1)}, bf16[8,8,48,128]{3,2,1,0:T(8,128)(2,1)}, u32[]{:S(2)}, u32[]{:S(2)}) collective-permute-start(bf16[8,8,48,128]{3,2,1,0:T(8,128)(2,1)S(1)} %copy-done.2), channel_id=1, source_target_pairs={{0,1},{1,0},{2,3},{3,2},{4,5},{5,4},{6,7},{7,6},{8,9},{9,8},{10,11... | collective-permute-start | bytes 2359304 | tf_op jit(solution)/shard_map/ppermute | solution.py:31
  120.1 21.2 %copy-start.13 = (bf16[2,8,1,96,128]{4,3,2,1,0:T(8,128)(2,1)}, bf16[2,8,1,96,128]{4,3,2,1,0:T(8,128)(2,1)S(1)}, u32[]{:S(2)}) copy-start(bf16[2,8,1,96,128]{4,3,2,1,0:T(8,128)(2,1)S(1)} %collective-permute-done.10.refs_9_) | copy-start | bytes 1179652
  120.1 22.8 %collective-permute-start.3 = (bf16[2,8,2,96,128]{4,3,2,1,0:T(8,128)(2,1)S(1)}, bf16[2,8,2,96,128]{4,3,2,1,0:T(8,128)(2,1)S(1)}, u32[]{:S(2)}, u32[]{:S(2)}) collective-permute-start(bf16[2,8,2,96,128]{4,3,2,1,0:T(8,128)(2,1)S(1)} %collective-permute-done.1.refs_0_), channel_id=1, source_target_pairs={{0,2},{2,0},{4,6},{6,4},{8,10},{10,8},{12,14},{14,12},{16,18},{18,... | collective-permute-start | bytes 2359304 | tf_op jit(solution)/shard_map/ppermute | solution.py:31
  120.4 20.9 %copy-start.14 = (bf16[2,8,1,96,128]{4,3,2,1,0:T(8,128)(2,1)}, bf16[2,8,1,96,128]{4,3,2,1,0:T(8,128)(2,1)S(1)}, u32[]{:S(2)}) copy-start(bf16[2,8,1,96,128]{4,3,2,1,0:T(8,128)(2,1)S(1)} %collective-permute-done.11.refs_10_) | copy-start | bytes 1179652
  120.4 20.9 %collective-permute-start.12 = (bf16[2,8,1,96,128]{4,3,2,1,0:T(8,128)(2,1)S(1)}, bf16[2,8,1,96,128]{4,3,2,1,0:T(8,128)(2,1)S(1)}, u32[]{:S(2)}, u32[]{:S(2)}) collective-permute-start(bf16[2,8,1,96,128]{4,3,2,1,0:T(8,128)(2,1)S(1)} %collective-permute-done.8.refs_7_), channel_id=1, source_target_pairs={{0,2},{2,0},{4,6},{6,4},{8,10},{10,8},{12,14},{14,12},{16,18},{18,... | collective-permute-start | bytes 1179656 | tf_op jit(solution)/shard_map/ppermute | solution.py:31
  124.4 16.9 %copy-start.5 = (bf16[2,8,2,96,128]{4,3,2,1,0:T(8,128)(2,1)}, bf16[2,8,2,96,128]{4,3,2,1,0:T(8,128)(2,1)S(1)}, u32[]{:S(2)}) copy-start(bf16[2,8,2,96,128]{4,3,2,1,0:T(8,128)(2,1)S(1)} %collective-permute-done.2.refs_1_) | copy-start | bytes 2359300
  124.4 18.5 %collective-permute-start.4 = (bf16[2,8,2,96,128]{4,3,2,1,0:T(8,128)(2,1)S(1)}, bf16[2,8,2,96,128]{4,3,2,1,0:T(8,128)(2,1)S(1)}, u32[]{:S(2)}, u32[]{:S(2)}) collective-permute-start(bf16[2,8,2,96,128]{4,3,2,1,0:T(8,128)(2,1)S(1)} %collective-permute-done.2.refs_1_), channel_id=1, source_target_pairs={{0,2},{2,0},{4,6},{6,4},{8,10},{10,8},{12,14},{14,12},{16,18},{18,... | collective-permute-start | bytes 2359304 | tf_op jit(solution)/shard_map/ppermute | solution.py:31
  141.3 1.6 copy-start.16
  141.3 25.4 %collective-permute-start.18 = (bf16[8,4,48,128]{3,2,1,0:T(8,128)(2,1)}, bf16[8,4,48,128]{3,2,1,0:T(8,128)(2,1)S(1)}, u32[]{:S(2)}, u32[]{:S(2)}) collective-permute-start(bf16[8,4,48,128]{3,2,1,0:T(8,128)(2,1)} %get-tuple-element.35), channel_id=1, source_target_pairs={{0,1},{1,0},{2,3},{3,2},{4,5},{5,4},{6,7},{7,6},{8,9},{9,8},{10,11... | collective-permute-start | bytes 1179656 | tf_op jit(solution)/shard_map/ppermute | solution.py:31
  142.9 0.9 copy-start.6
  142.9 1.2 copy-start.7
  144.0 11.9 %copy-start.17 = (bf16[8,2,48,128]{3,2,1,0:T(8,128)(2,1)S(1)}, bf16[8,2,48,128]{3,2,1,0:T(8,128)(2,1)}, u32[]{:S(2)}) copy-start(bf16[8,2,48,128]{3,2,1,0:T(8,128)(2,1)} %get-tuple-element.34) | copy-start | bytes 589828
  155.4 2.3 %copy-start = (s32[16]{0:T(128)S(1)}, s32[16]{0:T(128)}, u32[]{:S(2)}) copy-start(s32[16]{0:T(128)} %constant.50.clone) | copy-start | bytes 196
  155.4 8.2 %collective-permute-start.16 = (bf16[8,2,48,128]{3,2,1,0:T(8,128)(2,1)}, bf16[8,2,48,128]{3,2,1,0:T(8,128)(2,1)}, u32[]{:S(2)}, u32[]{:S(2)}) collective-permute-start(bf16[8,2,48,128]{3,2,1,0:T(8,128)(2,1)} %get-tuple-element.33), channel_id=1, source_target_pairs={{0,1},{1,0},{2,3},{3,2},{4,5},{5,4},{6,7},{7,6},{8,9},{9,8},{10,11... | collective-permute-start | bytes 589832 | tf_op jit(solution)/shard_map/ppermute | solution.py:31
  156.0 10.7 %collective-permute-start.17 = (bf16[8,2,48,128]{3,2,1,0:T(8,128)(2,1)S(1)}, bf16[8,2,48,128]{3,2,1,0:T(8,128)(2,1)}, u32[]{:S(2)}, u32[]{:S(2)}) collective-permute-start(bf16[8,2,48,128]{3,2,1,0:T(8,128)(2,1)S(1)} %copy-done.17), channel_id=1, source_target_pairs={{0,1},{1,0},{2,3},{3,2},{4,5},{5,4},{6,7},{7,6},{8,9},{9,8},{10,11... | collective-permute-start | bytes 589832 | tf_op jit(solution)/shard_map/ppermute | solution.py:31
  166.7 0.7 copy-start.15
  166.7 1.4 copy-start.1

commit v2 on v0

--- a/solution.py
+++ b/solution.py
@@ -1,15 +1,464 @@
+import functools
 import math
 
+import numpy as np
 import jax
 import jax.numpy as jnp
 from jax import lax
+from jax.experimental import pallas as pl
+from jax.experimental.pallas import tpu as pltpu
 from jax.sharding import PartitionSpec as P
+
+ROW_TILE = 16
+LOG2E = 1.4426950408889634
+MASKED = -1.0e30
+
+
+def bit_reverse(value, bits):
+    result = 0
+    for bit in range(bits):
+        result |= ((value >> bit) & 1) << (bits - 1 - bit)
+    return result
+
+
+def slot_class(slot, levels):
+    return levels - slot.bit_length()
 
 
 def swapped(value, axis, bit):
     mask = 2**bit
     pairs = [(source, source ^ mask) for source in range(lax.axis_size(axis))]
     return lax.ppermute(value, axis, pairs)
+
+
+def one_hot_order(size, stride, transposed):
+    rows = lax.broadcasted_iota(jnp.int32, (size, size), 0)
+    cols = lax.broadcasted_iota(jnp.int32, (size, size), 1)
+    if transposed:
+        rows, cols = cols, rows
+    inner = size // stride
+    match = (rows % inner) * stride + rows // inner == cols
+    return jnp.where(match, 1.0, 0.0).astype(jnp.bfloat16)
+
+
+def reorder_kernel(table, *refs, sources, groups, slots, cuts):
+    source_refs = refs[:sources]
+    out_refs = refs[sources:-1]
+    orders = refs[-1]
+    size = slots * ROW_TILE
+
+    @pl.when(pl.program_id(0) == 0)
+    def _():
+        cols = lax.broadcasted_iota(jnp.int32, (ROW_TILE, size), 1)
+        offset = cols - slots * lax.broadcasted_iota(jnp.int32, (ROW_TILE, size), 0)
+        for head in range(groups):
+            for slot in range(slots):
+                match = jnp.where(offset == table[head, slot], 1.0, 0.0)
+                orders[head, slot * ROW_TILE : (slot + 1) * ROW_TILE] = match.astype(jnp.bfloat16)
+
+    for head in range(groups):
+        pieces = [ref[:, head * 128 : (head + 1) * 128] for ref in source_refs]
+        block = pieces[0] if sources == 1 else jnp.concatenate(pieces, axis=1)
+        moved = jnp.dot(orders[head], block, preferred_element_type=jnp.float32)
+        moved = moved.astype(jnp.bfloat16)
+        for index in range(sources):
+            piece = moved[:, index * 128 : (index + 1) * 128].reshape(slots, ROW_TILE, 128)
+            for out_ref, (low, high) in zip(out_refs, cuts):
+                out_ref[index, head] = piece[low:high]
+
+
+def reorder(table, arrays, slots, cuts, name):
+    rows, cols = arrays[0].shape
+    groups = cols // 128
+    size = slots * ROW_TILE
+    blocks = rows // size
+    inner = rows // slots
+    sources = len(arrays)
+    out_shape = [
+        jax.ShapeDtypeStruct((sources, groups, high - low, inner, 128), jnp.bfloat16)
+        for low, high in cuts
+    ]
+    total = sum(high - low for low, high in cuts)
+    return pl.pallas_call(
+        functools.partial(
+            reorder_kernel, sources=sources, groups=groups, slots=slots, cuts=cuts
+        ),
+        out_shape=out_shape,
+        grid_spec=pltpu.PrefetchScalarGridSpec(
+            num_scalar_prefetch=1,
+            grid=(blocks,),
+            in_specs=[pl.BlockSpec((size, cols), lambda b, t: (b, 0))] * sources,
+            out_specs=[
+                pl.BlockSpec(
+                    (sources, groups, high - low, ROW_TILE, 128), lambda b, t: (0, 0, 0, b, 0)
+                )
+                for low, high in cuts
+            ],
+            scratch_shapes=[pltpu.VMEM((groups, size, size), jnp.bfloat16)],
+        ),
+        compiler_params=pltpu.CompilerParams(vmem_limit_bytes=56 << 20),
+        cost_estimate=pl.CostEstimate(
+            flops=2 * sources * rows * size * cols,
+            transcendentals=0,
+            bytes_accessed=2 * sources * rows * cols + 2 * sources * groups * total * inner * 128,
+        ),
+        name=name,
+    )(table, *arrays)
+
+
+def attention_kernel(
+    own_x, q_ref, *refs, heads, parts, tiles, has_bias, has_state, state_rows, owners, score_scale
+):
+    refs = list(refs)
+    kv_refs = [refs.pop(0) for _ in range(parts)]
+    bias_ref = refs.pop(0) if has_bias else None
+    state_in = [refs.pop(0) for _ in range(3)] if has_state else None
+    mine_ref = refs.pop(0)
+    theirs_ref = refs.pop(0)
+    state_out = [refs.pop(0) for _ in range(3)] if state_rows else None
+    out_scratch = refs.pop(0)
+    factor = score_scale * LOG2E
+    slots, inner, width = q_ref.shape[1:]
+
+    def joined(which, head):
+        pieces = [ref[which, head].reshape(-1, width) for ref in kv_refs]
+        return pieces[0] if len(pieces) == 1 else jnp.concatenate(pieces, axis=0)
+
+    def score(unit):
+        head, (first, count, _) = unit
+        queries = q_ref[head].reshape(slots * inner, width)[first : first + count]
+        return lax.dot_general(
+            queries, joined(0, head), (((1,), (1,)), ((), ())), preferred_element_type=jnp.float32
+        )
+
+    def finish(unit, scores):
+        head, (first, count, subs) = unit
+        weights, peaks = [], []
+        row = 0
+        for sub_count, bias_row in subs:
+            block = scores[row : row + sub_count]
+            if has_bias:
+                block = block * factor + bias_ref[bias_row : bias_row + 1, :]
+                peak = jnp.max(block, axis=1, keepdims=True)
+                if has_state:
+                    low = first + row
+                    peak = jnp.maximum(peak, state_in[0][head, low : low + sub_count, :1])
+                weight = jnp.exp2(block - peak)
+            else:
+                peak = jnp.max(block, axis=1, keepdims=True)
+                weight = jnp.exp2(block * factor - peak * factor)
+            weights.append(weight.astype(jnp.bfloat16))
+            peaks.append(peak)
+            row += sub_count
+        weight = weights[0] if len(weights) == 1 else jnp.concatenate(weights, axis=0)
+        values = joined(1, head)
+        values = jnp.concatenate([values, jnp.ones_like(values)], axis=1)
+        mixed = jnp.dot(weight, values, preferred_element_type=jnp.float32)
+        value_sum = mixed[:, :width]
+        total = mixed[:, width:]
+        if has_state or first < state_rows:
+            peak = peaks[0] if len(peaks) == 1 else jnp.concatenate(peaks, axis=0)
+        if has_state:
+            keep = jnp.exp2(state_in[0][head, first : first + count, :] - peak)
+            value_sum = value_sum + keep * state_in[2][head, first : first + count, :]
+            total = total + keep * state_in[1][head, first : first + count, :]
+        if first < state_rows:
+            state_out[0][head, first : first + count, :] = jnp.broadcast_to(peak, (count, width))
+            state_out[1][head, first : first + count, :] = total
+            state_out[2][head, first : first + count, :] = value_sum
+        else:
+            low = first - state_rows
+            out_scratch[head, low : low + count, :] = (value_sum / total).astype(jnp.bfloat16)
+
+    units = [(head, tile) for head in range(heads) for tile in tiles]
+    scores = score(units[0])
+    for index, unit in enumerate(units):
+        following = score(units[index + 1]) if index + 1 < len(units) else None
+        finish(unit, scores)
+        scores = following
+
+    share = inner // owners
+    me = own_x[0]
+    for head in range(heads):
+        for slot in range(out_scratch.shape[1] // inner):
+            base = slot * inner
+            start = pl.multiple_of(base + me * share, ROW_TILE)
+            mine_ref[head, slot] = out_scratch[head, pl.ds(start, share), :]
+            start = pl.multiple_of(base + (owners - 1 - me) * share, ROW_TILE)
+            theirs_ref[head, slot] = out_scratch[head, pl.ds(start, share), :]
+
+
+def attention(
+    own_x, queries, first_slot, parts, bias, state, state_rows, tiles, heads, score_scale, name
+):
+    groups, all_slots, inner, width = queries.shape
+    slots = sum(count for _, count, _ in tiles) // inner
+    owners = 2
+    done = slots - state_rows // inner
+    in_specs = [
+        pl.BlockSpec((heads, slots, inner, width), lambda h, x: (h, first_slot // slots, 0, 0))
+    ]
+    operands = [queries]
+    for part in parts:
+        in_specs.append(
+            pl.BlockSpec((2, heads) + part.shape[2:], lambda h, x: (0, h, 0, 0, 0))
+        )
+        operands.append(part)
+    key_count = sum(part.shape[2] * part.shape[3] for part in parts)
+    if bias is not None:
+        in_specs.append(pl.BlockSpec(bias.shape, lambda h, x: (0, 0)))
+        operands.append(bias)
+    if state is not None:
+        for item in state:
+            in_specs.append(pl.BlockSpec((heads,) + item.shape[1:], lambda h, x: (h, 0, 0)))
+            operands.append(item)
+    share = inner // owners
+    out_shape = [jax.ShapeDtypeStruct((groups, done, share, width), jnp.bfloat16)] * 2
+    out_specs = [pl.BlockSpec((heads, done, share, width), lambda h, x: (h, 0, 0, 0))] * 2
+    if state_rows:
+        out_shape += [jax.ShapeDtypeStruct((groups, state_rows, width), jnp.float32)] * 3
+        out_specs += [pl.BlockSpec((heads, state_rows, width), lambda h, x: (h, 0, 0))] * 3
+    rows = slots * inner
+    return pl.pallas_call(
+        functools.partial(
+            attention_kernel,
+            heads=heads,
+            parts=len(parts),
+            tiles=tiles,
+            has_bias=bias is not None,
+            has_state=state is not None,
+            state_rows=state_rows,
+            owners=owners,
+            score_scale=score_scale,
+        ),
+        out_shape=out_shape,
+        grid_spec=pltpu.PrefetchScalarGridSpec(
+            num_scalar_prefetch=1,
+            grid=(groups // heads,),
+            in_specs=in_specs,
+            out_specs=out_specs,
+            scratch_shapes=[pltpu.VMEM((heads, done * inner, width), jnp.bfloat16)],
+        ),
+        compiler_params=pltpu.CompilerParams(vmem_limit_bytes=60 << 20),
+        cost_estimate=pl.CostEstimate(
+            flops=12 * groups * rows * key_count * width,
+            transcendentals=groups * rows * key_count,
+            bytes_accessed=groups * rows * key_count,
+        ),
+        name=name,
+    )(own_x, *operands)
+
+
+def project_kernel(table, halves, *refs, classes, groups, slots, share, last):
+    refs = list(refs)
+    attended = [refs.pop(0) for _ in classes]
+    weights = [refs.pop(0) for _ in range(2)]
+    partial_ref = refs.pop(0) if last else None
+    out_ref = refs.pop(0)
+    by_residue = refs.pop(0)
+    half = groups // 2
+
+    @pl.when(pl.program_id(0) == 0)
+    def _():
+        for head in range(groups):
+            slot = 0
+            for ref in attended:
+                for index in range(ref.shape[1]):
+                    start = pl.multiple_of(table[head, slot] * share, ROW_TILE)
+                    by_residue[
+                        head // half,
+                        pl.ds(start, share),
+                        (head % half) * 128 : (head % half + 1) * 128,
+                    ] = ref[head, index]
+                    slot += 1
+
+    result = jnp.dot(by_residue[halves[0]], weights[0][...], preferred_element_type=jnp.float32)
+    result += jnp.dot(by_residue[halves[1]], weights[1][...], preferred_element_type=jnp.float32)
+    if not last:
+        out_ref[...] = result.astype(jnp.bfloat16)
+        return
+    result = (result + partial_ref[...].astype(jnp.float32)).astype(jnp.bfloat16)
+    size = slots * ROW_TILE
+    order = one_hot_order(size, slots, True)
+    result = result.reshape(slots, share, result.shape[1])
+    for block in range(share // ROW_TILE):
+        rows = result[:, block * ROW_TILE : (block + 1) * ROW_TILE].reshape(size, -1)
+        out_ref[block * size : (block + 1) * size] = jnp.dot(
+            order, rows, preferred_element_type=jnp.float32
+        ).astype(jnp.bfloat16)
+
+
+def project(table, halves, attended, weights, partial, name):
+    groups, _, share, width = attended[0].shape[-4:]
+    classes = [item.shape[-3] for item in attended]
+    slots = sum(classes)
+    rows = slots * share
+    step = 512
+    cols = weights[0].shape[-1]
+    if len(weights) == 1:
+        depth = weights[0].shape[0] // 2
+        weights = weights * 2
+        in_specs = [pl.BlockSpec(item.shape, lambda n, t, c: (0, 0, 0, 0)) for item in attended]
+        for place in (0, 1):
+            in_specs.append(pl.BlockSpec((depth, step), lambda n, t, c, place=place: (place, n)))
+    else:
+        depth = weights[0].shape[0]
+        in_specs = [pl.BlockSpec(item.shape, lambda n, t, c: (0, 0, 0, 0)) for item in attended]
+        in_specs += [pl.BlockSpec((depth, step), lambda n, t, c: (0, n))] * 2
+    operands = list(attended) + list(weights)
+    if partial is not None:
+        in_specs.append(pl.BlockSpec((rows, step), lambda n, t, c: (0, n)))
+        operands.append(partial)
+    return pl.pallas_call(
+        functools.partial(
+            project_kernel,
+            classes=classes,
+            groups=groups,
+            slots=slots,
+            share=share,
+            last=partial is not None,
+        ),
+        out_shape=jax.ShapeDtypeStruct((rows, cols), jnp.bfloat16),
+        grid_spec=pltpu.PrefetchScalarGridSpec(
+            num_scalar_prefetch=2,
+            grid=(cols // step,),
+            in_specs=in_specs,
+            out_specs=pl.BlockSpec((rows, step), lambda n, t, c: (0, n)),
+            scratch_shapes=[pltpu.VMEM((2, rows, groups // 2 * width), jnp.bfloat16)],
+        ),
+        compiler_params=pltpu.CompilerParams(vmem_limit_bytes=56 << 20),
+        cost_estimate=pl.CostEstimate(
+            flops=2 * rows * groups * width * cols,
+            transcendentals=0,
+            bytes_accessed=2 * (groups * width * cols + rows * cols + rows * groups * width),
+        ),
+        name=name,
+    )(table, halves, *operands)
+
+
+def bias_rows(query_classes, parts, levels, inner):
+    rows = []
+    for query_class in query_classes:
+        row = []
+        for low, high, distance in parts:
+            for slot in range(low, high):
+                shared = min(query_class, slot_class(slot, levels)) - distance + 1
+                row += [math.log2(shared) if shared > 0 else MASKED] * inner
+        rows.append(row)
+    return jnp.asarray(np.array(rows, np.float32))
+
+
+def after(values, *earlier):
+    return lax.optimization_barrier((tuple(values), earlier))[0]
+
+
+def fast_body(query_rows, key_rows, value_rows, head_phase, out_weight):
+    shards = lax.axis_size("seq")
+    levels = shards.bit_length() - 1
+    groups = head_phase.shape[0]
+    rows = query_rows.shape[0]
+    inner = rows // shards
+    slots = shards
+    score_scale = 1.0 / math.sqrt(query_rows.shape[1] // groups)
+    own_x = lax.axis_index("head").reshape(1)
+    own_core = lax.axis_index("seq") % 2
+    reversed_bits = jnp.asarray([bit_reverse(slot, levels) for slot in range(slots)], jnp.int32)
+    phase = head_phase % shards
+    residue_table = reversed_bits[None, :] ^ phase[:, None]
+    over = lambda value, mask: lax.ppermute(
+        value, "seq", [(source, source ^ mask) for source in range(shards)]
+    )
+    head_swap = lambda value: swapped(value, "head", 0)
+
+    half_rows = out_weight.shape[0] // 2
+    half_weight = lax.dynamic_slice_in_dim(out_weight, own_core * half_rows, half_rows, 0)
+    same_half = head_swap(half_weight)
+
+    (value_rows,) = after([value_rows], half_weight)
+    cuts = [(slots // 2, slots)] + [(0, slots >> level) for level in range(1, levels + 1)]
+    class_0, level_1, level_2, level_3, level_4 = reorder(
+        residue_table, [key_rows, value_rows], slots, cuts, "reorder_kv"
+    )
+    y_level_2 = over(level_2, 2)
+    z_level_3 = over(level_3, 4)
+    core_level_1 = over(level_1, 1)
+    w_level_4 = over(level_4, 8)
+    (query_rows,) = after([query_rows], class_0)
+    queries = reorder(residue_table, [query_rows], slots, [(0, slots)], "reorder_q")[0][0]
+    (core_level_1,) = after([core_level_1], queries)
+    queries, sent_level_4 = after([queries, level_4], core_level_1)
+    zw_level_4 = over(sent_level_4, 12)
+
+    own = [level_1, class_0]
+    own_parts = [(0, slots, 0)]
+    near = own + [core_level_1]
+    near_parts = own_parts + [(0, slots // 2, 1)]
+
+    def plain(total, tile, bias_row):
+        return [(first, tile, [(tile, bias_row)]) for first in range(0, total, tile)]
+
+    attend = functools.partial(attention, own_x, queries)
+    tiles = plain(slots // 2 * inner, 256, 0)
+    mine_0, theirs_0 = attend(slots // 2, own, None, None, 0, tiles, 2, score_scale, "class0")
+    z_level_3, core_level_1 = after([z_level_3, core_level_1], mine_0)
+    near[-1] = core_level_1
+    cz_level_3 = over(z_level_3, 1)
+    bias = bias_rows([1], near_parts, levels, inner)
+    tiles = plain(slots // 4 * inner, 192, 0)
+    mine_1, theirs_1 = attend(slots // 4, near, bias, None, 0, tiles, 2, score_scale, "class1")
+    y_level_2, w_level_4, zw_level_4, cz_level_3, same_half, theirs_0 = after(
+        [y_level_2, w_level_4, zw_level_4, cz_level_3, same_half, theirs_0], mine_1
+    )
+    cy_level_2 = over(y_level_2, 1)
+    got_0 = head_swap(theirs_0)
+    yz_level_3 = over(y_level_2[:, :, :2], 4)
+    own_level_4 = jnp.concatenate([w_level_4, zw_level_4], axis=2)
+    y_level_4 = over(own_level_4, 2)
+    got_1 = head_swap(theirs_1)
+    late = 2 * inner
+    tiles = [
+        (0, late, [(inner, 0), (inner, 1)]),
+        (late, late, [(late, 2)]),
+    ]
+    parts = near_parts + [(0, 4, 2)] * 2
+    bias = bias_rows([levels, levels - 1, levels - 2], parts, levels, inner)
+    mid = [y_level_2, cy_level_2]
+    out = attend(0, near + mid, bias, None, late, tiles, 2, score_scale, "class2")
+    mine_2, theirs_2 = out[:2]
+    state = out[2:]
+    yz_level_3, y_level_4, own_level_4, same_half, got_0 = after(
+        [yz_level_3, y_level_4, own_level_4, same_half, got_0], mine_2
+    )
+    cyz_level_3 = over(yz_level_3, 1)
+    c_level_4 = over(own_level_4, 1)
+    cy_level_4 = over(y_level_4, 1)
+    got_2 = head_swap(theirs_2)
+    (sent_phase,) = after([phase], mine_2)
+    other_phase = head_swap(sent_phase)
+    tiles = [(0, late, [(inner, 0), (inner, 1)])]
+    parts = [(0, 2, 3)] * 4 + [(0, 1, 4)] * 8
+    bias = bias_rows([levels, levels - 1], parts, levels, inner)
+    far = [z_level_3, cz_level_3, yz_level_3, cyz_level_3]
+    far += [own_level_4, c_level_4, y_level_4, cy_level_4]
+    mine_3, theirs_3 = attend(0, far, bias, state, 0, tiles, 4, score_scale, "class3")
+    got_3 = head_swap(theirs_3)
+    (same_half, got_1, got_2, other_phase) = after([same_half, got_1, got_2, other_phase], mine_3)
+    other_half = over(same_half, 1)
+    other_table = reversed_bits[None, :] ^ other_phase[:, None]
+
+    partial = project(
+        residue_table,
+        jnp.asarray([0, 1], jnp.int32),
+        [mine_3, mine_2, mine_1, mine_0],
+        [out_weight],
+        None,
+        "project_own",
+    )
+    (got_3,) = after([got_3], partial)
+    halves = jnp.stack([own_core, 1 - own_core])
+    return project(
+        other_table, halves, [got_3, got_2, got_1, got_0], [same_half, other_half], partial, "project"
+    )
 
 
 def halve(block, parity, axis):
@@ -62,7 +511,7 @@
     return score_tile(queries)
 
 
-def body(query_rows, key_rows, value_rows, head_phase, out_weight):
+def any_body(query_rows, key_rows, value_rows, head_phase, out_weight):
     groups = head_phase.shape[0]
     head_width = query_rows.shape[1] // groups
     levels = lax.axis_size("seq").bit_length() - 1
@@ -126,4 +575,12 @@
 def solution(mesh):
     in_specs = (P("seq", "head"), P("seq", "head"), P("seq", "head"), P("head"), P("head", None))
     out_specs = P(("seq", "head"), None)
+
+    def body(query_rows, *others):
+        shards = mesh.shape["seq"]
+        inner = query_rows.shape[0] // shards
+        if shards == 16 and mesh.shape["head"] == 2 and inner % (2 * ROW_TILE) == 0:
+            return fast_body(query_rows, *others)
+        return any_body(query_rows, *others)
+
     return jax.shard_map(body, mesh=mesh, in_specs=in_specs, out_specs=out_specs, check_vma=False)

time: 501 us -> 126 us (0.25); the launches traced: 492 us -> 126 us
  matrix products: 149 us -> 0 us
  other arithmetic: 106 us -> 1.9 us
  local copies, waits for them, and re-layouts: 106 us -> 6.6 us
  waiting for transfers between devices: 104 us -> 10.9 us
  Pallas kernels: 0 us -> 84.4 us
  between operations: 15.1 us -> 0.15 us
  starting transfers between devices: 11.7 us -> 21.5 us
    dot_general x15 -> x0, matrix products: 149 us -> none  [the longest x7 72.4 us: score_tile(): jnp.einsum('gqk,gkd->gqd', weights.astype(jnp.bfloat16), key_values[:, 1]...]
    pallas_call x0 -> x8, Pallas kernels: none -> 84.4 us  [the longest x4 49.7 us: attention(): pl.pallas_call(functools.partial(attention_kernel, heads=heads, parts=len...]
    reduce_scatter x1 -> x0, waiting for transfers between devices: 74.5 us -> none  [body(): lax.psum_scatter(jnp.dot(attended, out_weight, preferred_element_type=jnp...]
    reduce_sum x6 -> x0, other arithmetic: 64.5 us -> none  [score_tile(): row_total = jnp.sum(weights, axis=2)]
    slice x19 -> x1, local copies, waits for them, and re-layouts: 39 us -> 1.19 us  [fast_body(): yz_level_3 = over(y_level_2[:, :, :2], 4)]
    unnamed x174 -> x27, local copies, waits for them, and re-layouts: 35.2 us -> 3.09 us
    concatenate x11 -> x0, other arithmetic: 24.9 us -> none  [the longest x8 20.6 us: body(): jnp.concatenate((block_rows, swapped(block_rows, 'seq', bit_index)), axis=2)]
    ppermute x10 -> x6, waiting for transfers between devices: 29.5 us -> 7.76 us  [swapped(): return lax.ppermute(value, axis, pairs)]
  transfers between devices with their start and end apart: 11 -> 19, of which waited for: 3 -> 8; matrix products, arithmetic and copies ran while one was open for 61% -> 2% of each run, Pallas kernels for 0% -> 52%
where the time goes in v2:
time: 126 us
  Pallas kernels  84.4 us (67%)
  starting transfers between devices  21.5 us (17%)
  waiting for transfers between devices  10.9 us (9%)
  local copies, waits for them, and re-layouts  6.6 us (5%)
  other arithmetic  1.9 us (2%)
    pallas_call x4, Pallas kernels, attention(): pl.pallas_call(functools.partial(attention_kernel, heads=heads, parts=len...  49.7 us
    pallas_call x2, Pallas kernels, project(): pl.pallas_call(functools.partial(project_kernel, classes=classes, groups=...  18.1 us
    pallas_call x2, Pallas kernels, reorder(): pl.pallas_call(functools.partial(reorder_kernel, sources=sources, groups=...  16.6 us
    ppermute x13, starting transfers between devices, fast_body(): lax.ppermute(value, 'seq', [(source, source ^ mask) for source in range(s...  14.3 us
    ppermute x6, waiting for transfers between devices, swapped(): return lax.ppermute(value, axis, pairs)  7.76 us
    ppermute x6, starting transfers between devices, swapped(): return lax.ppermute(value, axis, pairs)  7.16 us
    ppermute x13, waiting for transfers between devices, fast_body(): lax.ppermute(value, 'seq', [(source, source ^ mask) for source in range(s...  3.16 us
    unnamed x27, local copies, waits for them, and re-layouts  3.09 us
  transfers between devices with their start and end apart: 19, of which 8 were waited for; matrix products, arithmetic and copies ran while one was open for 2% of the time, Pallas kernels for 52%

profile of v2, /device:TPU:0, one launch (start us, length us, event | category | flops | bytes accessed | tf_op | source)
XLA Modules:
  0.0 125.5 jit_solution(10768409545152428765)
XLA Ops:
  0.0 1.8 %constant_dynamic-slice_fusion = bf16[512,2048]{1,0:T(8,128)(2,1)S(1)} fusion(bf16[1024,2048]{1,0:T(8,128)(2,1)} %refs_5_.2, s32[]{:T(128)S(6)} %select_n.18), kind=kLoop, calls=%fused_computation.9 | loop fusion | bytes 4194308 | tf_op jit(solution)/shard_map/dynamic_slice | solution.py:374
  1.8 0.0 copy-done.12
  1.8 0.0 copy-done.6
  1.8 0.7 broadcast_xor_fusion.1.table
  2.5 9.4 %reorder_kv.1 = (bf16[2,8,8,96,128]{4,3,2,1,0:T(8,128)(2,1)}, bf16[2,8,8,96,128]{4,3,2,1,0:T(8,128)(2,1)}, bf16[2,8,4,96,128]{4,3,2,1,0:T(8,128)(2,1)}, bf16[2,8...) custom-call(s32[8,16]{1,0:T(8,128)} %broadcast_xor_fusion.1.table, bf16[1536,1024]{1,0:T(8,128)(2,1)} %refs_0_.1, ...), custom_call_target="tpu_custom_call" | custom-call | flops 1610612736 | bytes 15335424 | tf_op jit(solution)/shard_map/reorder_kv/pallas_call | solution.py:82
  11.9 0.5 collective-permute-start.2
  12.4 2.6 %collective-permute-start.6 = (bf16[512,2048]{1,0:T(8,128)(2,1)S(1)}, bf16[512,2048]{1,0:T(8,128)(2,1)}, u32[]{:S(2)}, u32[]{:S(2)}) collective-permute-start(bf16[512,2048]{1,0:T(8,128)(2,1)S(1)} %constant_dynamic-slice_fusion), channel_id=1, source_target_pairs={{0,1},{1,0},{2,3},{3,2},{4,5},{5,4},{6,7},{7,6},{8,9},{9,8},{10,11... | collective-permute-start | bytes 6291464 | tf_op jit(solution)/shard_map/ppermute | solution.py:31
  14.9 1.6 %collective-permute-start.4 = (bf16[2,8,2,96,128]{4,3,2,1,0:T(8,128)(2,1)}, bf16[2,8,2,96,128]{4,3,2,1,0:T(8,128)(2,1)}, u32[]{:S(2)}, u32[]{:S(2)}) collective-permute-start(bf16[2,8,2,96,128]{4,3,2,1,0:T(8,128)(2,1)} %get-tuple-element.53), channel_id=1, source_target_pairs={{0,8},{2,10},{4,12},{6,14},{8,0},{10,2},{12,4},{14,6},{16,24},{18,... | collective-permute-start | bytes 2359304 | tf_op jit(solution)/shard_map/ppermute | solution.py:368
  16.5 1.5 %collective-permute-start = (bf16[2,8,4,96,128]{4,3,2,1,0:T(8,128)(2,1)}, bf16[2,8,4,96,128]{4,3,2,1,0:T(8,128)(2,1)}, u32[]{:S(2)}, u32[]{:S(2)}) collective-permute-start(bf16[2,8,4,96,128]{4,3,2,1,0:T(8,128)(2,1)} %get-tuple-element.46), channel_id=1, source_target_pairs={{0,4},{2,6},{4,0},{6,2},{8,12},{10,14},{12,8},{14,10},{16,20},{18,... | collective-permute-start | bytes 4718600 | tf_op jit(solution)/shard_map/ppermute | solution.py:368
  18.0 2.6 %collective-permute-start.1 = (bf16[2,8,1,96,128]{4,3,2,1,0:T(8,128)(2,1)}, bf16[2,8,1,96,128]{4,3,2,1,0:T(8,128)(2,1)S(1)}, u32[]{:S(2)}, u32[]{:S(2)}) collective-permute-start(bf16[2,8,1,96,128]{4,3,2,1,0:T(8,128)(2,1)} %get-tuple-element.52), channel_id=1, source_target_pairs={{0,16},{2,18},{4,20},{6,22},{8,24},{10,26},{12,28},{14,30},{16,0},... | collective-permute-start | bytes 1179656 | tf_op jit(solution)/shard_map/ppermute | solution.py:368
  20.6 7.2 %reorder_q.1 = bf16[1,8,16,96,128]{4,3,2,1,0:T(8,128)(2,1)} custom-call(s32[8,16]{1,0:T(8,128)} %broadcast_xor_fusion.1.table, bf16[1536,1024]{1,0:T(8,128)(2,1)} %refs_0_.2), custom_call_target="tpu_custom_call" | custom-call | flops 805306368 | bytes 6291456 | tf_op jit(solution)/shard_map/reorder_q/pallas_call | solution.py:82
  27.8 0.0 collective-permute-done.2.refs_2_
  27.8 14.9 %class0.1 = (bf16[8,8,48,128]{3,2,1,0:T(8,128)(2,1)}, bf16[8,8,48,128]{3,2,1,0:T(8,128)(2,1)}) custom-call(s32[1]{0:T(128)} %bitcast.1.own_x, bf16[8,16,96,128]{3,2,1,0:T(8,128)(2,1)} %bitcast.4, bf16[2,8,8,96,128]{4,3,2,1,0:T(8,128)(2,1)} %get-tuple-element.50.refs_0_, bf16[2,8,8,96,128]{4,3,2,1,0:T(8,128)(2,1)} %get-tuple-element.48.refs_1_), custom_call_target="tpu_custom_call" | custom-call | flops 14495514624 | bytes 9437184 | tf_op jit(solution)/shard_map/class0/pallas_call | solution.py:222
  42.6 0.6 collective-permute-done.4.refs_0_
  43.3 0.0 collective-permute-start.5
  43.3 3.6 %collective-permute-start.3 = (bf16[2,8,1,96,128]{4,3,2,1,0:T(8,128)(2,1)S(1)}, bf16[2,8,1,96,128]{4,3,2,1,0:T(8,128)(2,1)S(1)}, u32[]{:S(2)}, u32[]{:S(2)}) collective-permute-start(bf16[2,8,1,96,128]{4,3,2,1,0:T(8,128)(2,1)S(1)} %copy-done.11), channel_id=1, source_target_pairs={{0,24},{2,26},{4,28},{6,30},{8,16},{10,18},{12,20},{14,22},{16,8},... | collective-permute-start | bytes 1179656 | tf_op jit(solution)/shard_map/ppermute | solution.py:368
  46.9 12.1 %class1.1 = (bf16[8,4,48,128]{3,2,1,0:T(8,128)(2,1)}, bf16[8,4,48,128]{3,2,1,0:T(8,128)(2,1)}) custom-call(s32[1]{0:T(128)} %bitcast.1.own_x, bf16[8,16,96,128]{3,2,1,0:T(8,128)(2,1)} %bitcast.5, bf16[2,8,8,96,128]{4,3,2,1,0:T(8,128)(2,1)} %get-tuple-element.50.refs_0_, bf16[2,8,8,96,128]{4,3,2,1,0:T(8,128)(2,1)} %get-tuple-element.48.refs_1_, ...), custom_call_target="tpu_custom_call" | custom-call | flops 10871635968 | bytes 7077888 | tf_op jit(solution)/shard_map/class1/pallas_call | solution.py:222
  59.0 0.0 collective-permute-done.1
  59.0 0.0 collective-permute-done.refs_3_
  59.0 2.2 %collective-permute-done.6.refs_4_ = bf16[512,2048]{1,0:T(8,128)(2,1)} collective-permute-done((bf16[512,2048]{1,0:T(8,128)(2,1)S(1)}, bf16[512,2048]{1,0:T(8,128)(2,1)}, u32[]{:S(2)}, u32[]{:S(2)}) %collective-permute-start.6) | collective-permute-done | bytes 2097184 | tf_op jit(solution)/shard_map/ppermute | solution.py:31
  61.3 0.0 collective-permute-done.3
  61.3 0.0 collective-permute-done.5.refs_1_
  61.3 0.0 collective-permute-start.10
  61.3 1.2 slice.3
  62.5 0.1 constant_dynamic-update-slice_fusion.refs_4_
  62.6 1.8 %collective-permute-start.8 = (bf16[2,8,2,96,128]{4,3,2,1,0:T(8,128)(2,1)S(1)}, bf16[2,8,2,96,128]{4,3,2,1,0:T(8,128)(2,1)S(1)}, u32[]{:S(2)}, u32[]{:S(2)}) collective-permute-start(bf16[2,8,2,96,128]{4,3,2,1,0:T(8,128)(2,1)S(1)} %constant_dynamic-update-slice_fusion.refs_4_), channel_id=1, source_target_pairs={{0,4},{2,6},{4,0},{6,2},{8,12},{10,14},{12,8},{14,10},{16,20},{18,... | collective-permute-start | bytes 2359304 | tf_op jit(solution)/shard_map/ppermute | solution.py:368
  64.4 2.2 %collective-permute-start.7 = (bf16[2,8,2,96,128]{4,3,2,1,0:T(8,128)(2,1)S(1)}, bf16[2,8,2,96,128]{4,3,2,1,0:T(8,128)(2,1)}, u32[]{:S(2)}, u32[]{:S(2)}) collective-permute-start(bf16[2,8,2,96,128]{4,3,2,1,0:T(8,128)(2,1)S(1)} %slice.3), channel_id=1, source_target_pairs={{0,8},{2,10},{4,12},{6,14},{8,0},{10,2},{12,4},{14,6},{16,24},{18,... | collective-permute-start | bytes 2359304 | tf_op jit(solution)/shard_map/ppermute | solution.py:368
  66.6 0.9 collective-permute-start.9
  67.5 0.0 collective-permute-done.10.refs_4_
  67.5 15.7 %class2.1 = (bf16[8,2,48,128]{3,2,1,0:T(8,128)(2,1)}, bf16[8,2,48,128]{3,2,1,0:T(8,128)(2,1)}, f32[8,192,128]{2,1,0:T(8,128)}, f32[8,192,128]{2,1,0:T(8,128)}, f32[8,192,128]{2,1,0:T(8,128)}) custom-call(s32[1]{0:T(128)} %bitcast.1.own_x, bf16[8,16,96,128]{3,2,1,0:T(8,128)(2,1)} %bitcast.6, bf16[2,8,8,96,128]{4,3,2,1,0:T(8,128)(2,1)} %get-tuple-element.50.refs_0_, ...), custom_call_target="tpu_custom_call" | custom-call | flops 14495514624 | bytes 9437184 | tf_op jit(solution)/shard_map/class2/pallas_call | solution.py:222
  83.2 0.0 collective-permute-done.8.refs_6_
  83.2 0.0 copy-start.7
  83.2 1.4 %collective-permute-done.7.refs_2_ = bf16[2,8,2,96,128]{4,3,2,1,0:T(8,128)(2,1)} collective-permute-done((bf16[2,8,2,96,128]{4,3,2,1,0:T(8,128)(2,1)S(1)}, bf16[2,8,2,96,128]{4,3,2,1,0:T(8,128)(2,1)}, u32[]{:S(2)}, u32[]{:S(2)}) %collective-permute-start.7) | collective-permute-done | bytes 786464 | tf_op jit(solution)/shard_map/ppermute | solution.py:368
  84.7 1.6 %collective-permute-done.9.refs_3_ = bf16[8,8,48,128]{3,2,1,0:T(8,128)(2,1)S(1)} collective-permute-done((bf16[8,8,48,128]{3,2,1,0:T(8,128)(2,1)}, bf16[8,8,48,128]{3,2,1,0:T(8,128)(2,1)S(1)}, u32[]{:S(2)}, u32[]{:S(2)}) %collective-permute-start.9) | collective-permute-done | bytes 786464 | tf_op jit(solution)/shard_map/ppermute | solution.py:31
  86.2 0.0 collective-permute-start.14
  86.2 0.0 copy-done.3
  86.2 0.5 collective-permute-start.15
  86.7 0.1 collective-permute-start.16
  86.8 0.9 collective-permute-start.11
  87.7 1.2 collective-permute-start.12
  88.8 0.3 collective-permute-done.14.refs_3_
  89.1 0.9 collective-permute-start.13
  90.0 0.0 collective-permute-done.15.refs_5_
  90.0 0.8 collective-permute-done.16.refs_7_
  90.8 0.1 copy-done.9
  90.9 0.9 copy-done.10
  91.8 0.0 copy-done.7
  91.8 7.0 %class3.1 = (bf16[8,2,48,128]{3,2,1,0:T(8,128)(2,1)}, bf16[8,2,48,128]{3,2,1,0:T(8,128)(2,1)}) custom-call(s32[1]{0:T(128)} %bitcast.1.own_x, bf16[8,16,96,128]{3,2,1,0:T(8,128)(2,1)} %bitcast.7, bf16[2,8,2,96,128]{4,3,2,1,0:T(8,128)(2,1)} %collective-permute-done.4.refs_0_, bf16[2,8,2,96,128]{4,3,2,1,0:T(8,128)(2,1)} %collective-permute-done.5.refs_1_, ...), custom_call_target="tpu_custom_call" | custom-call | flops 3623878656 | bytes 2359296 | tf_op jit(solution)/shard_map/class3/pallas_call | solution.py:222
  98.8 0.0 copy-done.1
  98.8 0.1 collective-permute-done.11.refs_2_
  98.9 3.8 %collective-permute-done.13 = s32[8]{0:T(128)S(1)} collective-permute-done((s32[8]{0:T(128)S(1)}, s32[8]{0:T(128)S(1)}, u32[]{:S(2)}, u32[]{:S(2)}) %collective-permute-start.13) | collective-permute-done | bytes 64 | tf_op jit(solution)/shard_map/ppermute | solution.py:31
  102.8 0.0 collective-permute-done.12.refs_1_
  102.8 0.0 collective-permute-start.18
  102.8 0.6 pad_add_fusion.halves
  103.4 0.9 collective-permute-start.17
  104.2 0.5 call_exported.0.halves
  104.7 8.2 %project_own.1.refs_6_ = bf16[768,2048]{1,0:T(8,128)(2,1)} custom-call(s32[8,16]{1,0:T(8,128)} %broadcast_xor_fusion.1.table, s32[2]{0:T(128)} %call_exported.0.halves, bf16[8,2,48,128]{3,2,1,0:T(8,128)(2,1)} %get-tuple-element.77.refs_0_, bf16[8,2,48,128]{3,2,1,0:T(8,128)(2,1)} %get-tuple-element.65.refs_1_, ...), custom_call_target="tpu_custom_call" | custom-call | flops 3221225472 | bytes 8912896 | tf_op jit(solution)/shard_map/project_own/pallas_call | solution.py:312
  113.0 0.0 copy-done.4
  113.0 0.7 broadcast_xor_fusion.table
  113.6 0.0 collective-permute-done.17.refs_0_
  113.6 0.0 collective-permute-done.18.refs_5_
  113.6 0.7 copy-done.5
  114.3 1.3 %copy-done = bf16[512,2048]{1,0:T(8,128)(2,1)} copy-done((bf16[512,2048]{1,0:T(8,128)(2,1)}, bf16[512,2048]{1,0:T(8,128)(2,1)S(1)}, u32[]{:S(2)}) %copy-start) | copy-done | bytes 2097176
  115.7 9.9 %project.1 = bf16[768,2048]{1,0:T(8,128)(2,1)} custom-call(s32[8,16]{1,0:T(8,128)} %broadcast_xor_fusion.table, s32[2]{0:T(128)} %pad_add_fusion.halves, bf16[8,2,48,128]{3,2,1,0:T(8,128)(2,1)} %copy-done.5, bf16[8,2,48,128]{3,2,1,0:T(8,128)(2,1)} %copy-done.4, bf16[8,4,48,128]{3,2,1,0:T(8,128)(2,1)} %copy-done.2, bf16[8,8,48,128]{3,2,1,0:T(8,128)(2,1)} %copy-done.1, ...), custom_call_target="tpu_custom_call" | custom-call | flops 3221225472 | bytes 8912896 | tf_op jit(solution)/shard_map/project/pallas_call | solution.py:312
  (17 shorter events, 0.1 us)
Async XLA Ops:
  0.0 1.8 %copy-start.6 = (s32[16]{0:T(128)S(1)}, s32[16]{0:T(128)}, u32[]{:S(2)}) copy-start(s32[16]{0:T(128)} %constant.51.clone) | copy-start | bytes 196
  0.0 1.8 %copy-start.12 = (s32[8]{0:T(128)S(1)}, s32[8]{0:T(128)}, u32[]{:S(2)}) copy-start(s32[8]{0:T(128)} %param.13) | copy-start | bytes 100
  11.9 15.9 %collective-permute-start.2 = (bf16[2,8,8,96,128]{4,3,2,1,0:T(8,128)(2,1)}, bf16[2,8,8,96,128]{4,3,2,1,0:T(8,128)(2,1)}, u32[]{:S(2)}, u32[]{:S(2)}) collective-permute-start(bf16[2,8,8,96,128]{4,3,2,1,0:T(8,128)(2,1)} %get-tuple-element.50.refs_0_), channel_id=1, source_target_pairs={{0,2},{2,0},{4,6},{6,4},{8,10},{10,8},{12,14},{14,12},{16,18},{18,... | collective-permute-start | bytes 9437192 | tf_op jit(solution)/shard_map/ppermute | solution.py:368
  12.4 48.9 %collective-permute-start.6 = (bf16[512,2048]{1,0:T(8,128)(2,1)S(1)}, bf16[512,2048]{1,0:T(8,128)(2,1)}, u32[]{:S(2)}, u32[]{:S(2)}) collective-permute-start(bf16[512,2048]{1,0:T(8,128)(2,1)S(1)} %constant_dynamic-slice_fusion), channel_id=1, source_target_pairs={{0,1},{1,0},{2,3},{3,2},{4,5},{5,4},{6,7},{7,6},{8,9},{9,8},{10,11... | collective-permute-start | bytes 6291464 | tf_op jit(solution)/shard_map/ppermute | solution.py:31
  14.9 28.4 %collective-permute-start.4 = (bf16[2,8,2,96,128]{4,3,2,1,0:T(8,128)(2,1)}, bf16[2,8,2,96,128]{4,3,2,1,0:T(8,128)(2,1)}, u32[]{:S(2)}, u32[]{:S(2)}) collective-permute-start(bf16[2,8,2,96,128]{4,3,2,1,0:T(8,128)(2,1)} %get-tuple-element.53), channel_id=1, source_target_pairs={{0,8},{2,10},{4,12},{6,14},{8,0},{10,2},{12,4},{14,6},{16,24},{18,... | collective-permute-start | bytes 2359304 | tf_op jit(solution)/shard_map/ppermute | solution.py:368
  16.5 42.5 %collective-permute-start = (bf16[2,8,4,96,128]{4,3,2,1,0:T(8,128)(2,1)}, bf16[2,8,4,96,128]{4,3,2,1,0:T(8,128)(2,1)}, u32[]{:S(2)}, u32[]{:S(2)}) collective-permute-start(bf16[2,8,4,96,128]{4,3,2,1,0:T(8,128)(2,1)} %get-tuple-element.46), channel_id=1, source_target_pairs={{0,4},{2,6},{4,0},{6,2},{8,12},{10,14},{12,8},{14,10},{16,20},{18,... | collective-permute-start | bytes 4718600 | tf_op jit(solution)/shard_map/ppermute | solution.py:368
  18.0 41.0 %collective-permute-start.1 = (bf16[2,8,1,96,128]{4,3,2,1,0:T(8,128)(2,1)}, bf16[2,8,1,96,128]{4,3,2,1,0:T(8,128)(2,1)S(1)}, u32[]{:S(2)}, u32[]{:S(2)}) collective-permute-start(bf16[2,8,1,96,128]{4,3,2,1,0:T(8,128)(2,1)} %get-tuple-element.52), channel_id=1, source_target_pairs={{0,16},{2,18},{4,20},{6,22},{8,24},{10,26},{12,28},{14,30},{16,0},... | collective-permute-start | bytes 1179656 | tf_op jit(solution)/shard_map/ppermute | solution.py:368
  27.8 15.5 %copy-start.11 = (bf16[2,8,1,96,128]{4,3,2,1,0:T(8,128)(2,1)S(1)}, bf16[2,8,1,96,128]{4,3,2,1,0:T(8,128)(2,1)}, u32[]{:S(2)}) copy-start(bf16[2,8,1,96,128]{4,3,2,1,0:T(8,128)(2,1)} %get-tuple-element.52) | copy-start | bytes 1179652
  43.3 18.0 %collective-permute-start.5 = (bf16[2,8,2,96,128]{4,3,2,1,0:T(8,128)(2,1)}, bf16[2,8,2,96,128]{4,3,2,1,0:T(8,128)(2,1)}, u32[]{:S(2)}, u32[]{:S(2)}) collective-permute-start(bf16[2,8,2,96,128]{4,3,2,1,0:T(8,128)(2,1)} %collective-permute-done.4.refs_0_), channel_id=1, source_target_pairs={{0,2},{2,0},{4,6},{6,4},{8,10},{10,8},{12,14},{14,12},{16,18},{18,... | collective-permute-start | bytes 2359304 | tf_op jit(solution)/shard_map/ppermute | solution.py:368
  43.3 18.0 %collective-permute-start.3 = (bf16[2,8,1,96,128]{4,3,2,1,0:T(8,128)(2,1)S(1)}, bf16[2,8,1,96,128]{4,3,2,1,0:T(8,128)(2,1)S(1)}, u32[]{:S(2)}, u32[]{:S(2)}) collective-permute-start(bf16[2,8,1,96,128]{4,3,2,1,0:T(8,128)(2,1)S(1)} %copy-done.11), channel_id=1, source_target_pairs={{0,24},{2,26},{4,28},{6,30},{8,16},{10,18},{12,20},{14,22},{16,8},... | collective-permute-start | bytes 1179656 | tf_op jit(solution)/shard_map/ppermute | solution.py:368
  61.3 6.2 %collective-permute-start.10 = (bf16[2,8,4,96,128]{4,3,2,1,0:T(8,128)(2,1)}, bf16[2,8,4,96,128]{4,3,2,1,0:T(8,128)(2,1)}, u32[]{:S(2)}, u32[]{:S(2)}) collective-permute-start(bf16[2,8,4,96,128]{4,3,2,1,0:T(8,128)(2,1)} %collective-permute-done.refs_3_), channel_id=1, source_target_pairs={{0,2},{2,0},{4,6},{6,4},{8,10},{10,8},{12,14},{14,12},{16,18},{18,... | collective-permute-start | bytes 4718600 | tf_op jit(solution)/shard_map/ppermute | solution.py:368
  62.6 23.7 %copy-start.3 = (bf16[2,8,2,96,128]{4,3,2,1,0:T(8,128)(2,1)}, bf16[2,8,2,96,128]{4,3,2,1,0:T(8,128)(2,1)S(1)}, u32[]{:S(2)}) copy-start(bf16[2,8,2,96,128]{4,3,2,1,0:T(8,128)(2,1)S(1)} %constant_dynamic-update-slice_fusion.refs_4_) | copy-start | bytes 2359300
  62.6 20.6 %collective-permute-start.8 = (bf16[2,8,2,96,128]{4,3,2,1,0:T(8,128)(2,1)S(1)}, bf16[2,8,2,96,128]{4,3,2,1,0:T(8,128)(2,1)S(1)}, u32[]{:S(2)}, u32[]{:S(2)}) collective-permute-start(bf16[2,8,2,96,128]{4,3,2,1,0:T(8,128)(2,1)S(1)} %constant_dynamic-update-slice_fusion.refs_4_), channel_id=1, source_target_pairs={{0,4},{2,6},{4,0},{6,2},{8,12},{10,14},{12,8},{14,10},{16,20},{18,... | collective-permute-start | bytes 2359304 | tf_op jit(solution)/shard_map/ppermute | solution.py:368
  64.4 20.2 %collective-permute-start.7 = (bf16[2,8,2,96,128]{4,3,2,1,0:T(8,128)(2,1)S(1)}, bf16[2,8,2,96,128]{4,3,2,1,0:T(8,128)(2,1)}, u32[]{:S(2)}, u32[]{:S(2)}) collective-permute-start(bf16[2,8,2,96,128]{4,3,2,1,0:T(8,128)(2,1)S(1)} %slice.3), channel_id=1, source_target_pairs={{0,8},{2,10},{4,12},{6,14},{8,0},{10,2},{12,4},{14,6},{16,24},{18,... | collective-permute-start | bytes 2359304 | tf_op jit(solution)/shard_map/ppermute | solution.py:368
  66.6 19.6 %collective-permute-start.9 = (bf16[8,8,48,128]{3,2,1,0:T(8,128)(2,1)}, bf16[8,8,48,128]{3,2,1,0:T(8,128)(2,1)S(1)}, u32[]{:S(2)}, u32[]{:S(2)}) collective-permute-start(bf16[8,8,48,128]{3,2,1,0:T(8,128)(2,1)} %get-tuple-element.64), channel_id=1, source_target_pairs={{0,1},{1,0},{2,3},{3,2},{4,5},{5,4},{6,7},{7,6},{8,9},{9,8},{10,11... | collective-permute-start | bytes 2359304 | tf_op jit(solution)/shard_map/ppermute | solution.py:31
  83.2 8.6 %copy-start.7 = (bf16[2,8,2,96,128]{4,3,2,1,0:T(8,128)(2,1)}, bf16[2,8,2,96,128]{4,3,2,1,0:T(8,128)(2,1)S(1)}, u32[]{:S(2)}) copy-start(bf16[2,8,2,96,128]{4,3,2,1,0:T(8,128)(2,1)S(1)} %collective-permute-done.8.refs_6_) | copy-start | bytes 2359300
  86.2 12.6 %copy-start.1 = (bf16[8,8,48,128]{3,2,1,0:T(8,128)(2,1)}, bf16[8,8,48,128]{3,2,1,0:T(8,128)(2,1)S(1)}, u32[]{:S(2)}) copy-start(bf16[8,8,48,128]{3,2,1,0:T(8,128)(2,1)S(1)} %collective-permute-done.9.refs_3_) | copy-start | bytes 2359300
  86.2 2.9 %collective-permute-start.14 = (bf16[2,8,2,96,128]{4,3,2,1,0:T(8,128)(2,1)}, bf16[2,8,2,96,128]{4,3,2,1,0:T(8,128)(2,1)S(1)}, u32[]{:S(2)}, u32[]{:S(2)}) collective-permute-start(bf16[2,8,2,96,128]{4,3,2,1,0:T(8,128)(2,1)} %collective-permute-done.7.refs_2_), channel_id=1, source_target_pairs={{0,2},{2,0},{4,6},{6,4},{8,10},{10,8},{12,14},{14,12},{16,18},{18,... | collective-permute-start | bytes 2359304 | tf_op jit(solution)/shard_map/ppermute | solution.py:368
  86.2 3.7 %collective-permute-start.15 = (bf16[2,8,2,96,128]{4,3,2,1,0:T(8,128)(2,1)S(1)}, bf16[2,8,2,96,128]{4,3,2,1,0:T(8,128)(2,1)S(1)}, u32[]{:S(2)}, u32[]{:S(2)}) collective-permute-start(bf16[2,8,2,96,128]{4,3,2,1,0:T(8,128)(2,1)S(1)} %constant_dynamic-update-slice_fusion.refs_4_), channel_id=1, source_target_pairs={{0,2},{2,0},{4,6},{6,4},{8,10},{10,8},{12,14},{14,12},{16,18},{18,... | collective-permute-start | bytes 2359304 | tf_op jit(solution)/shard_map/ppermute | solution.py:368
  86.7 4.0 %collective-permute-start.16 = (bf16[2,8,2,96,128]{4,3,2,1,0:T(8,128)(2,1)S(1)}, bf16[2,8,2,96,128]{4,3,2,1,0:T(8,128)(2,1)S(1)}, u32[]{:S(2)}, u32[]{:S(2)}) collective-permute-start(bf16[2,8,2,96,128]{4,3,2,1,0:T(8,128)(2,1)S(1)} %collective-permute-done.8.refs_6_), channel_id=1, source_target_pairs={{0,2},{2,0},{4,6},{6,4},{8,10},{10,8},{12,14},{14,12},{16,18},{18,... | collective-permute-start | bytes 2359304 | tf_op jit(solution)/shard_map/ppermute | solution.py:368
  86.8 12.1 %collective-permute-start.11 = (bf16[8,4,48,128]{3,2,1,0:T(8,128)(2,1)}, bf16[8,4,48,128]{3,2,1,0:T(8,128)(2,1)S(1)}, u32[]{:S(2)}, u32[]{:S(2)}) collective-permute-start(bf16[8,4,48,128]{3,2,1,0:T(8,128)(2,1)} %get-tuple-element.67), channel_id=1, source_target_pairs={{0,1},{1,0},{2,3},{3,2},{4,5},{5,4},{6,7},{7,6},{8,9},{9,8},{10,11... | collective-permute-start | bytes 1179656 | tf_op jit(solution)/shard_map/ppermute | solution.py:31
  87.7 15.1 %collective-permute-start.12 = (bf16[8,2,48,128]{3,2,1,0:T(8,128)(2,1)}, bf16[8,2,48,128]{3,2,1,0:T(8,128)(2,1)S(1)}, u32[]{:S(2)}, u32[]{:S(2)}) collective-permute-start(bf16[8,2,48,128]{3,2,1,0:T(8,128)(2,1)} %get-tuple-element.68), channel_id=1, source_target_pairs={{0,1},{1,0},{2,3},{3,2},{4,5},{5,4},{6,7},{7,6},{8,9},{9,8},{10,11... | collective-permute-start | bytes 589832 | tf_op jit(solution)/shard_map/ppermute | solution.py:31
  89.1 2.7 %copy-start.8 = (bf16[2,8,2,96,128]{4,3,2,1,0:T(8,128)(2,1)}, bf16[2,8,2,96,128]{4,3,2,1,0:T(8,128)(2,1)S(1)}, u32[]{:S(2)}) copy-start(bf16[2,8,2,96,128]{4,3,2,1,0:T(8,128)(2,1)S(1)} %collective-permute-done.14.refs_3_) | copy-start | bytes 2359300
  89.1 13.6 %collective-permute-start.13 = (s32[8]{0:T(128)S(1)}, s32[8]{0:T(128)S(1)}, u32[]{:S(2)}, u32[]{:S(2)}) collective-permute-start(s32[8]{0:T(128)S(1)} %and_select_fusion), channel_id=1, source_target_pairs={{0,1},{1,0},{2,3},{3,2},{4,5},{5,4},{6,7},{7,6},{8,9},{9,8},{10,11... | collective-permute-start | bytes 104 | tf_op jit(solution)/shard_map/ppermute | solution.py:31
  90.0 0.9 copy-start.9
  90.9 0.9 copy-start.10
  98.9 14.0 %copy-start.2 = (bf16[8,4,48,128]{3,2,1,0:T(8,128)(2,1)}, bf16[8,4,48,128]{3,2,1,0:T(8,128)(2,1)S(1)}, u32[]{:S(2)}) copy-start(bf16[8,4,48,128]{3,2,1,0:T(8,128)(2,1)S(1)} %collective-permute-done.11.refs_2_) | copy-start | bytes 1179652
  102.8 10.2 %copy-start.4 = (bf16[8,2,48,128]{3,2,1,0:T(8,128)(2,1)}, bf16[8,2,48,128]{3,2,1,0:T(8,128)(2,1)S(1)}, u32[]{:S(2)}) copy-start(bf16[8,2,48,128]{3,2,1,0:T(8,128)(2,1)S(1)} %collective-permute-done.12.refs_1_) | copy-start | bytes 589828
  102.8 10.9 %collective-permute-start.18 = (bf16[512,2048]{1,0:T(8,128)(2,1)}, bf16[512,2048]{1,0:T(8,128)(2,1)S(1)}, u32[]{:S(2)}, u32[]{:S(2)}) collective-permute-start(bf16[512,2048]{1,0:T(8,128)(2,1)} %collective-permute-done.6.refs_4_), channel_id=1, source_target_pairs={{0,2},{2,0},{4,6},{6,4},{8,10},{10,8},{12,14},{14,12},{16,18},{18,... | collective-permute-start | bytes 6291464 | tf_op jit(solution)/shard_map/ppermute | solution.py:368
  103.4 10.3 %collective-permute-start.17 = (bf16[8,2,48,128]{3,2,1,0:T(8,128)(2,1)}, bf16[8,2,48,128]{3,2,1,0:T(8,128)(2,1)S(1)}, u32[]{:S(2)}, u32[]{:S(2)}) collective-permute-start(bf16[8,2,48,128]{3,2,1,0:T(8,128)(2,1)} %get-tuple-element.79), channel_id=1, source_target_pairs={{0,1},{1,0},{2,3},{3,2},{4,5},{5,4},{6,7},{7,6},{8,9},{9,8},{10,11... | collective-permute-start | bytes 589832 | tf_op jit(solution)/shard_map/ppermute | solution.py:31
  113.6 0.7 copy-start.5
  114.3 1.3 %copy-start = (bf16[512,2048]{1,0:T(8,128)(2,1)}, bf16[512,2048]{1,0:T(8,128)(2,1)S(1)}, u32[]{:S(2)}) copy-start(bf16[512,2048]{1,0:T(8,128)(2,1)S(1)} %collective-permute-done.18.refs_5_) | copy-start | bytes 6291460

commit v3 on v2

--- a/solution.py
+++ b/solution.py
@@ -41,73 +41,123 @@
     return jnp.where(match, 1.0, 0.0).astype(jnp.bfloat16)
 
 
-def reorder_kernel(table, *refs, sources, groups, slots, cuts):
-    source_refs = refs[:sources]
-    out_refs = refs[sources:-1]
-    orders = refs[-1]
+def slot_order(table, head, slots):
     size = slots * ROW_TILE
-
-    @pl.when(pl.program_id(0) == 0)
-    def _():
-        cols = lax.broadcasted_iota(jnp.int32, (ROW_TILE, size), 1)
-        offset = cols - slots * lax.broadcasted_iota(jnp.int32, (ROW_TILE, size), 0)
+    cols = lax.broadcasted_iota(jnp.int32, (ROW_TILE, size), 1)
+    offset = cols - slots * lax.broadcasted_iota(jnp.int32, (ROW_TILE, size), 0)
+    pieces = [
+        jnp.where(offset == table[head, slot], 1.0, 0.0).astype(jnp.bfloat16)
+        for slot in range(slots)
+    ]
+    return jnp.concatenate(pieces, axis=0)
+
+
+def reorder_kernel(table, key_ref, value_ref, *refs, groups, slots, cuts, blocks):
+    count = len(cuts)
+    out_refs = refs[:count]
+    source, orders = refs[count : count + 2]
+    moved_refs = refs[count + 2 : 2 * count + 2]
+    in_sems, out_sems = refs[2 * count + 2 :]
+    size = slots * ROW_TILE
+
+    def fetch(block, index):
+        rows = pl.ds(block * size, size)
+        ref = (key_ref, value_ref)[index]
+        return pltpu.make_async_copy(
+            ref.at[rows], source.at[index, rows], in_sems.at[block, index]
+        )
+
+    def send(block, place):
+        return pltpu.make_async_copy(
+            moved_refs[place].at[block],
+            out_refs[place].at[:, :, :, pl.ds(block * ROW_TILE, ROW_TILE)],
+            out_sems.at[block, place],
+        )
+
+    for block in range(blocks):
+        for index in range(2):
+            fetch(block, index).start()
+    for head in range(groups):
+        orders[head] = slot_order(table, head, slots)
+    for block in range(blocks):
+        for index in range(2):
+            fetch(block, index).wait()
         for head in range(groups):
-            for slot in range(slots):
-                match = jnp.where(offset == table[head, slot], 1.0, 0.0)
-                orders[head, slot * ROW_TILE : (slot + 1) * ROW_TILE] = match.astype(jnp.bfloat16)
-
-    for head in range(groups):
-        pieces = [ref[:, head * 128 : (head + 1) * 128] for ref in source_refs]
-        block = pieces[0] if sources == 1 else jnp.concatenate(pieces, axis=1)
-        moved = jnp.dot(orders[head], block, preferred_element_type=jnp.float32)
-        moved = moved.astype(jnp.bfloat16)
-        for index in range(sources):
-            piece = moved[:, index * 128 : (index + 1) * 128].reshape(slots, ROW_TILE, 128)
-            for out_ref, (low, high) in zip(out_refs, cuts):
-                out_ref[index, head] = piece[low:high]
-
-
-def reorder(table, arrays, slots, cuts, name):
-    rows, cols = arrays[0].shape
+            rows = slice(block * size, (block + 1) * size)
+            cols = slice(head * 128, (head + 1) * 128)
+            pair = jnp.concatenate([source[0, rows, cols], source[1, rows, cols]], axis=1)
+            moved = jnp.dot(orders[head], pair, preferred_element_type=jnp.float32)
+            moved = moved.astype(jnp.bfloat16)
+            for index in range(2):
+                piece = moved[:, index * 128 : (index + 1) * 128].reshape(slots, ROW_TILE, 128)
+                for ref, (low, high) in zip(moved_refs, cuts):
+                    ref[block, index, head] = piece[low:high]
+        for place in range(count):
+            send(block, place).start()
+    for block in range(blocks):
+        for place in range(count):
+            send(block, place).wait()
+
+
+def reorder(table, key_rows, value_rows, slots, cuts, name):
+    rows, cols = key_rows.shape
     groups = cols // 128
     size = slots * ROW_TILE
     blocks = rows // size
     inner = rows // slots
-    sources = len(arrays)
     out_shape = [
-        jax.ShapeDtypeStruct((sources, groups, high - low, inner, 128), jnp.bfloat16)
+        jax.ShapeDtypeStruct((2, groups, high - low, inner, 128), jnp.bfloat16)
         for low, high in cuts
     ]
     total = sum(high - low for low, high in cuts)
+    any_spec = pl.BlockSpec(memory_space=pl.ANY)
     return pl.pallas_call(
-        functools.partial(
-            reorder_kernel, sources=sources, groups=groups, slots=slots, cuts=cuts
-        ),
+        functools.partial(reorder_kernel, groups=groups, slots=slots, cuts=cuts, blocks=blocks),
         out_shape=out_shape,
         grid_spec=pltpu.PrefetchScalarGridSpec(
             num_scalar_prefetch=1,
-            grid=(blocks,),
-            in_specs=[pl.BlockSpec((size, cols), lambda b, t: (b, 0))] * sources,
-            out_specs=[
-                pl.BlockSpec(
-                    (sources, groups, high - low, ROW_TILE, 128), lambda b, t: (0, 0, 0, b, 0)
-                )
+            grid=(1,),
+            in_specs=[any_spec] * 2,
+            out_specs=[any_spec] * len(cuts),
+            scratch_shapes=[
+                pltpu.VMEM((2, rows, cols), jnp.bfloat16),
+                pltpu.VMEM((groups, size, size), jnp.bfloat16),
+            ]
+            + [
+                pltpu.VMEM((blocks, 2, groups, high - low, ROW_TILE, 128), jnp.bfloat16)
                 for low, high in cuts
+            ]
+            + [
+                pltpu.SemaphoreType.DMA((blocks, 2)),
+                pltpu.SemaphoreType.DMA((blocks, len(cuts))),
             ],
-            scratch_shapes=[pltpu.VMEM((groups, size, size), jnp.bfloat16)],
-        ),
-        compiler_params=pltpu.CompilerParams(vmem_limit_bytes=56 << 20),
+        ),
+        compiler_params=pltpu.CompilerParams(vmem_limit_bytes=60 << 20),
         cost_estimate=pl.CostEstimate(
-            flops=2 * sources * rows * size * cols,
+            flops=4 * rows * size * cols,
             transcendentals=0,
-            bytes_accessed=2 * sources * rows * cols + 2 * sources * groups * total * inner * 128,
+            bytes_accessed=4 * rows * cols + 4 * groups * total * inner * 128,
         ),
         name=name,
-    )(table, *arrays)
+    )(table, key_rows, value_rows)
 
 
 def attention_kernel(
-    own_x, q_ref, *refs, heads, parts, tiles, has_bias, has_state, state_rows, owners, score_scale
+    own_x,
+    table,
+    q_ref,
+    *refs,
+    heads,
+    parts,
+    first_row,
+    tiles,
+    moves_queries,
+    has_bias,
+    has_state,
+    state_rows,
+    inner,
+    owners,
+    score_scale,
 ):
     refs = list(refs)
     kv_refs = [refs.pop(0) for _ in range(parts)]
@@ -116,17 +166,42 @@
     mine_ref = refs.pop(0)
     theirs_ref = refs.pop(0)
     state_out = [refs.pop(0) for _ in range(3)] if state_rows else None
+    rest_ref = refs.pop(0) if moves_queries else None
     out_scratch = refs.pop(0)
+    by_slot = refs.pop(0) if moves_queries else None
     factor = score_scale * LOG2E
-    slots, inner, width = q_ref.shape[1:]
+    slots = table.shape[1]
+    width = 128
+
+    def arrange(head):
+        order = slot_order(table, pl.program_id(0) * heads + head, slots)
+        size = slots * ROW_TILE
+        for block in range(q_ref.shape[0] // size):
+            tokens = q_ref[block * size : (block + 1) * size, head * width : (head + 1) * width]
+            moved = jnp.dot(order, tokens, preferred_element_type=jnp.float32)
+            moved = moved.astype(jnp.bfloat16).reshape(slots, ROW_TILE, width)
+            by_slot[head, :, block * ROW_TILE : (block + 1) * ROW_TILE] = moved
+        rest_ref[head] = by_slot[head, : slots // 2]
 
     def joined(which, head):
-        pieces = [ref[which, head].reshape(-1, width) for ref in kv_refs]
+        pieces = []
+        for ref in kv_refs:
+            if len(ref.shape) == 5:
+                pieces.append(ref[which, head].reshape(-1, width))
+            else:
+                for index in range(ref.shape[0]):
+                    pieces.append(ref[index, which, head].reshape(-1, width))
         return pieces[0] if len(pieces) == 1 else jnp.concatenate(pieces, axis=0)
 
     def score(unit):
         head, (first, count, _) = unit
-        queries = q_ref[head].reshape(slots * inner, width)[first : first + count]
+        if moves_queries:
+            if first == tiles[0][0]:
+                arrange(head)
+            queries = by_slot[head].reshape(slots * inner, width)
+            queries = queries[first_row + first : first_row + first + count]
+        else:
+            queries = q_ref[head].reshape(-1, width)[first : first + count]
         return lax.dot_general(
             queries, joined(0, head), (((1,), (1,)), ((), ())), preferred_element_type=jnp.float32
         )
@@ -189,55 +264,86 @@
 
 
 def attention(
-    own_x, queries, first_slot, parts, bias, state, state_rows, tiles, heads, score_scale, name
+    own_x,
+    table,
+    queries,
+    first_slot,
+    parts,
+    bias,
+    state,
+    state_rows,
+    tiles,
+    heads,
+    score_scale,
+    name,
 ):
-    groups, all_slots, inner, width = queries.shape
-    slots = sum(count for _, count, _ in tiles) // inner
+    moves_queries = queries.ndim == 2
+    groups, slots = table.shape
+    inner, width = parts[0].shape[-2:]
     owners = 2
-    done = slots - state_rows // inner
-    in_specs = [
-        pl.BlockSpec((heads, slots, inner, width), lambda h, x: (h, first_slot // slots, 0, 0))
-    ]
-    operands = [queries]
+    rows = sum(count for _, count, _ in tiles)
+    taken = rows // inner
+    done = (rows - state_rows) // inner
+    if moves_queries:
+        in_specs = [pl.BlockSpec((queries.shape[0], heads * width), lambda h, x, t: (0, h))]
+    else:
+        in_specs = [
+            pl.BlockSpec((heads, taken, inner, width), lambda h, x, t: (h, first_slot // taken, 0, 0))
+        ]
+    operands = [queries] + list(parts)
     for part in parts:
-        in_specs.append(
-            pl.BlockSpec((2, heads) + part.shape[2:], lambda h, x: (0, h, 0, 0, 0))
-        )
-        operands.append(part)
-    key_count = sum(part.shape[2] * part.shape[3] for part in parts)
+        if part.ndim == 5:
+            in_specs.append(
+                pl.BlockSpec((2, heads) + part.shape[2:], lambda h, x, t: (0, h, 0, 0, 0))
+            )
+        else:
+            in_specs.append(
+                pl.BlockSpec(
+                    part.shape[:2] + (heads,) + part.shape[3:], lambda h, x, t: (0, 0, h, 0, 0, 0)
+                )
+            )
+    key_count = sum(part.size // (2 * groups * width) for part in parts)
     if bias is not None:
-        in_specs.append(pl.BlockSpec(bias.shape, lambda h, x: (0, 0)))
+        in_specs.append(pl.BlockSpec(bias.shape, lambda h, x, t: (0, 0)))
         operands.append(bias)
     if state is not None:
         for item in state:
-            in_specs.append(pl.BlockSpec((heads,) + item.shape[1:], lambda h, x: (h, 0, 0)))
+            in_specs.append(pl.BlockSpec((heads,) + item.shape[1:], lambda h, x, t: (h, 0, 0)))
             operands.append(item)
     share = inner // owners
     out_shape = [jax.ShapeDtypeStruct((groups, done, share, width), jnp.bfloat16)] * 2
-    out_specs = [pl.BlockSpec((heads, done, share, width), lambda h, x: (h, 0, 0, 0))] * 2
+    out_specs = [pl.BlockSpec((heads, done, share, width), lambda h, x, t: (h, 0, 0, 0))] * 2
+    scratch = [pltpu.VMEM((heads, done * inner, width), jnp.bfloat16)]
     if state_rows:
         out_shape += [jax.ShapeDtypeStruct((groups, state_rows, width), jnp.float32)] * 3
-        out_specs += [pl.BlockSpec((heads, state_rows, width), lambda h, x: (h, 0, 0))] * 3
-    rows = slots * inner
+        out_specs += [pl.BlockSpec((heads, state_rows, width), lambda h, x, t: (h, 0, 0))] * 3
+    if moves_queries:
+        rest = (slots // 2, inner, width)
+        out_shape.append(jax.ShapeDtypeStruct((groups,) + rest, jnp.bfloat16))
+        out_specs.append(pl.BlockSpec((heads,) + rest, lambda h, x, t: (h, 0, 0, 0)))
+        scratch.append(pltpu.VMEM((heads, slots, inner, width), jnp.bfloat16))
     return pl.pallas_call(
         functools.partial(
             attention_kernel,
             heads=heads,
             parts=len(parts),
+            first_row=first_slot * inner,
             tiles=tiles,
+            moves_queries=moves_queries,
             has_bias=bias is not None,
             has_state=state is not None,
             state_rows=state_rows,
+            inner=inner,
             owners=owners,
             score_scale=score_scale,
         ),
         out_shape=out_shape,
         grid_spec=pltpu.PrefetchScalarGridSpec(
-            num_scalar_prefetch=1,
+            num_scalar_prefetch=2,
             grid=(groups // heads,),
             in_specs=in_specs,
             out_specs=out_specs,
-            scratch_shapes=[pltpu.VMEM((heads, done * inner, width), jnp.bfloat16)],
+            scratch_shapes=scratch,
         ),
         compiler_params=pltpu.CompilerParams(vmem_limit_bytes=60 << 20),
         cost_estimate=pl.CostEstimate(
@@ -246,13 +352,13 @@
             bytes_accessed=groups * rows * key_count,
         ),
         name=name,
-    )(own_x, *operands)
-
-
-def project_kernel(table, halves, *refs, classes, groups, slots, share, last):
+    )(own_x, table, *operands)
+
+
+def project_kernel(table, halves, *refs, classes, sources, groups, slots, share, last):
     refs = list(refs)
     attended = [refs.pop(0) for _ in classes]
-    weights = [refs.pop(0) for _ in range(2)]
+    weights = [refs.pop(0) for _ in range(sources)]
     partial_ref = refs.pop(0) if last else None
     out_ref = refs.pop(0)
     by_residue = refs.pop(0)
@@ -266,14 +372,15 @@
                 for index in range(ref.shape[1]):
                     start = pl.multiple_of(table[head, slot] * share, ROW_TILE)
                     by_residue[
-                        head // half,
+                        halves[head // half],
                         pl.ds(start, share),
                         (head % half) * 128 : (head % half + 1) * 128,
                     ] = ref[head, index]
                     slot += 1
 
-    result = jnp.dot(by_residue[halves[0]], weights[0][...], preferred_element_type=jnp.float32)
-    result += jnp.dot(by_residue[halves[1]], weights[1][...], preferred_element_type=jnp.float32)
+    rows = jnp.concatenate([by_residue[0], by_residue[1]], axis=1)
+    weight = jnp.concatenate([ref[...] for ref in weights], axis=0)
+    result = jnp.dot(rows, weight, preferred_element_type=jnp.float32)
     if not last:
         out_ref[...] = result.astype(jnp.bfloat16)
         return
@@ -295,16 +402,8 @@
     rows = slots * share
     step = 512
     cols = weights[0].shape[-1]
-    if len(weights) == 1:
-        depth = weights[0].shape[0] // 2
-        weights = weights * 2
-        in_specs = [pl.BlockSpec(item.shape, lambda n, t, c: (0, 0, 0, 0)) for item in attended]
-        for place in (0, 1):
-            in_specs.append(pl.BlockSpec((depth, step), lambda n, t, c, place=place: (place, n)))
-    else:
-        depth = weights[0].shape[0]
-        in_specs = [pl.BlockSpec(item.shape, lambda n, t, c: (0, 0, 0, 0)) for item in attended]
-        in_specs += [pl.BlockSpec((depth, step), lambda n, t, c: (0, n))] * 2
+    in_specs = [pl.BlockSpec(item.shape, lambda n, t, c: (0, 0, 0, 0)) for item in attended]
+    in_specs += [pl.BlockSpec((item.shape[0], step), lambda n, t, c: (0, n)) for item in weights]
     operands = list(attended) + list(weights)
     if partial is not None:
         in_specs.append(pl.BlockSpec((rows, step), lambda n, t, c: (0, n)))
@@ -313,6 +412,7 @@
         functools.partial(
             project_kernel,
             classes=classes,
+            sources=len(weights),
             groups=groups,
             slots=slots,
             share=share,
@@ -326,7 +426,7 @@
             out_specs=pl.BlockSpec((rows, step), lambda n, t, c: (0, n)),
             scratch_shapes=[pltpu.VMEM((2, rows, groups // 2 * width), jnp.bfloat16)],
         ),
-        compiler_params=pltpu.CompilerParams(vmem_limit_bytes=56 << 20),
+        compiler_params=pltpu.CompilerParams(vmem_limit_bytes=60 << 20),
         cost_estimate=pl.CostEstimate(
             flops=2 * rows * groups * width * cols,
             transcendentals=0,
@@ -373,21 +473,21 @@
     half_rows = out_weight.shape[0] // 2
     half_weight = lax.dynamic_slice_in_dim(out_weight, own_core * half_rows, half_rows, 0)
     same_half = head_swap(half_weight)
+    other_phase = head_swap(phase)
 
     (value_rows,) = after([value_rows], half_weight)
     cuts = [(slots // 2, slots)] + [(0, slots >> level) for level in range(1, levels + 1)]
     class_0, level_1, level_2, level_3, level_4 = reorder(
-        residue_table, [key_rows, value_rows], slots, cuts, "reorder_kv"
+        residue_table, key_rows, value_rows, slots, cuts, "reorder_kv"
     )
     y_level_2 = over(level_2, 2)
     z_level_3 = over(level_3, 4)
     core_level_1 = over(level_1, 1)
     w_level_4 = over(level_4, 8)
-    (query_rows,) = after([query_rows], class_0)
-    queries = reorder(residue_table, [query_rows], slots, [(0, slots)], "reorder_q")[0][0]
-    (core_level_1,) = after([core_level_1], queries)
-    queries, sent_level_4 = after([queries, level_4], core_level_1)
-    zw_level_4 = over(sent_level_4, 12)
+    zw_level_4 = over(level_4, 12)
+    query_rows, other_phase = after([query_rows, other_phase], class_0)
+    other_table = reversed_bits[None, :] ^ other_phase[:, None]
+    query_rows, other_table = after([query_rows], other_table) + (other_table,)
 
     own = [level_1, class_0]
     own_parts = [(0, slots, 0)]
@@ -397,23 +497,27 @@
     def plain(total, tile, bias_row):
         return [(first, tile, [(tile, bias_row)]) for first in range(0, total, tile)]
 
-    attend = functools.partial(attention, own_x, queries)
+    attend = functools.partial(attention, own_x, residue_table)
     tiles = plain(slots // 2 * inner, 256, 0)
-    mine_0, theirs_0 = attend(slots // 2, own, None, None, 0, tiles, 2, score_scale, "class0")
+    mine_0, theirs_0, queries = attend(
+        query_rows, slots // 2, own, None, None, 0, tiles, 2, score_scale, "class0"
+    )
     z_level_3, core_level_1 = after([z_level_3, core_level_1], mine_0)
     near[-1] = core_level_1
     cz_level_3 = over(z_level_3, 1)
     bias = bias_rows([1], near_parts, levels, inner)
     tiles = plain(slots // 4 * inner, 192, 0)
-    mine_1, theirs_1 = attend(slots // 4, near, bias, None, 0, tiles, 2, score_scale, "class1")
+    mine_1, theirs_1 = attend(
+        queries, slots // 4, near, bias, None, 0, tiles, 2, score_scale, "class1"
+    )
     y_level_2, w_level_4, zw_level_4, cz_level_3, same_half, theirs_0 = after(
         [y_level_2, w_level_4, zw_level_4, cz_level_3, same_half, theirs_0], mine_1
     )
     cy_level_2 = over(y_level_2, 1)
     got_0 = head_swap(theirs_0)
     yz_level_3 = over(y_level_2[:, :, :2], 4)
-    own_level_4 = jnp.concatenate([w_level_4, zw_level_4], axis=2)
-    y_level_4 = over(own_level_4, 2)
+    far_level_4 = jnp.stack([w_level_4, zw_level_4])
+    y_level_4 = over(far_level_4, 2)
     got_1 = head_swap(theirs_1)
     late = 2 * inner
     tiles = [
@@ -423,28 +527,29 @@
     parts = near_parts + [(0, 4, 2)] * 2
     bias = bias_rows([levels, levels - 1, levels - 2], parts, levels, inner)
     mid = [y_level_2, cy_level_2]
-    out = attend(0, near + mid, bias, None, late, tiles, 2, score_scale, "class2")
+    out = attend(
+        queries, 0, near + mid, bias, None, late, tiles, 2, score_scale, "class2"
+    )
     mine_2, theirs_2 = out[:2]
     state = out[2:]
-    yz_level_3, y_level_4, own_level_4, same_half, got_0 = after(
-        [yz_level_3, y_level_4, own_level_4, same_half, got_0], mine_2
+    yz_level_3, y_level_4, far_level_4, same_half, got_0 = after(
+        [yz_level_3, y_level_4, far_level_4, same_half, got_0], mine_2
     )
     cyz_level_3 = over(yz_level_3, 1)
-    c_level_4 = over(own_level_4, 1)
+    c_level_4 = over(far_level_4, 1)
     cy_level_4 = over(y_level_4, 1)
     got_2 = head_swap(theirs_2)
-    (sent_phase,) = after([phase], mine_2)
-    other_phase = head_swap(sent_phase)
     tiles = [(0, late, [(inner, 0), (inner, 1)])]
     parts = [(0, 2, 3)] * 4 + [(0, 1, 4)] * 8
     bias = bias_rows([levels, levels - 1], parts, levels, inner)
     far = [z_level_3, cz_level_3, yz_level_3, cyz_level_3]
-    far += [own_level_4, c_level_4, y_level_4, cy_level_4]
-    mine_3, theirs_3 = attend(0, far, bias, state, 0, tiles, 4, score_scale, "class3")
+    far += [far_level_4, c_level_4, y_level_4, cy_level_4]
+    mine_3, theirs_3 = attend(
+        queries, 0, far, bias, state, 0, tiles, 4, score_scale, "class3"
+    )
     got_3 = head_swap(theirs_3)
-    (same_half, got_1, got_2, other_phase) = after([same_half, got_1, got_2, other_phase], mine_3)
+    (same_half, got_1, got_2) = after([same_half, got_1, got_2], mine_3)
     other_half = over(same_half, 1)
-    other_table = reversed_bits[None, :] ^ other_phase[:, None]
 
     partial = project(
         residue_table,

time: 126 us -> 122 us (0.968)
  Pallas kernels: 84.4 us -> 80 us
  starting transfers between devices: 21.5 us -> 19.9 us
  waiting for transfers between devices: 10.9 us -> 12.4 us
    pallas_call x4 -> x3, Pallas kernels: 34.7 us -> 24.3 us  [the longest x2 18.1 us: project(): pl.pallas_call(functools.partial(project_kernel, classes=classes, sources...]
    pallas_call x4, Pallas kernels: 49.7 us -> 55.6 us  [attention(): pl.pallas_call(functools.partial(attention_kernel, heads=heads, parts=len...]
    ppermute x13, waiting for transfers between devices: 3.16 us -> 5.68 us  [fast_body(): lax.ppermute(value, 'seq', [(source, source ^ mask) for source in range(s...]
    ppermute x6, starting transfers between devices: 7.16 us -> 5.78 us  [swapped(): return lax.ppermute(value, axis, pairs)]
    unnamed x27 -> x26, local copies, waits for them, and re-layouts: 3.09 us -> 3.81 us
  transfers between devices with their start and end apart: 19 -> 19, of which waited for: 8 -> 7; matrix products, arithmetic and copies ran while one was open for 2% -> 2% of each run, Pallas kernels for 52% -> 53%
where the time goes in v3:
time: 122 us
  Pallas kernels  80 us (66%)
  starting transfers between devices  19.9 us (16%)
  waiting for transfers between devices  12.4 us (10%)
  local copies, waits for them, and re-layouts  7.26 us (6%)
  other arithmetic  1.99 us (2%)
    pallas_call x4, Pallas kernels, attention(): pl.pallas_call(functools.partial(attention_kernel, heads=heads, parts=len...  55.6 us
    pallas_call x2, Pallas kernels, project(): pl.pallas_call(functools.partial(project_kernel, classes=classes, sources...  18.1 us
    ppermute x13, starting transfers between devices, fast_body(): lax.ppermute(value, 'seq', [(source, source ^ mask) for source in range(s...  14.2 us
    ppermute x6, waiting for transfers between devices, swapped(): return lax.ppermute(value, axis, pairs)  6.68 us
    pallas_call x1, Pallas kernels, reorder(): pl.pallas_call(functools.partial(reorder_kernel, groups=groups, slots=slo...  6.21 us
    ppermute x6, starting transfers between devices, swapped(): return lax.ppermute(value, axis, pairs)  5.78 us
    ppermute x13, waiting for transfers between devices, fast_body(): lax.ppermute(value, 'seq', [(source, source ^ mask) for source in range(s...  5.68 us
    unnamed x26, local copies, waits for them, and re-layouts  3.81 us
  transfers between devices with their start and end apart: 19, of which 7 were waited for; matrix products, arithmetic and copies ran while one was open for 2% of the time, Pallas kernels for 53%

profile of v3, /device:TPU:0, one launch (start us, length us, event | category | flops | bytes accessed | tf_op | source)
XLA Modules:
  0.0 121.7 jit_solution(3528744271628985989)
XLA Ops:
  0.0 1.8 %constant_dynamic-slice_fusion = bf16[512,2048]{1,0:T(8,128)(2,1)S(1)} fusion(bf16[1024,2048]{1,0:T(8,128)(2,1)} %refs_4_.1, s32[]{:T(128)S(6)} %select_n.18), kind=kLoop, calls=%fused_computation.8 | loop fusion | bytes 4194308 | tf_op jit(solution)/shard_map/dynamic_slice | solution.py:474
  1.8 0.0 copy-done.12
  1.8 0.0 copy-done.6
  1.8 0.7 broadcast_xor_fusion.1.table
  2.5 6.2 %reorder_kv.1 = (bf16[2,8,8,96,128]{4,3,2,1,0:T(8,128)(2,1)}, bf16[2,8,8,96,128]{4,3,2,1,0:T(8,128)(2,1)}, bf16[2,8,4,96,128]{4,3,2,1,0:T(8,128)(2,1)}, bf16[2,8...) custom-call(s32[8,16]{1,0:T(8,128)} %broadcast_xor_fusion.1.table, bf16[1536,1024]{1,0:T(8,128)(2,1)} %key_ref.1, ...), custom_call_target="tpu_custom_call" | custom-call | flops 1610612736 | bytes 15335424 | tf_op jit(solution)/shard_map/reorder_kv/pallas_call | solution.py:114
  8.7 0.5 collective-permute-start.2
  9.2 2.6 %collective-permute-start = (s32[8]{0:T(128)S(1)}, s32[8]{0:T(128)S(1)}, u32[]{:S(2)}, u32[]{:S(2)}) collective-permute-start(s32[8]{0:T(128)S(1)} %and_select_fusion), channel_id=1, source_target_pairs={{0,1},{1,0},{2,3},{3,2},{4,5},{5,4},{6,7},{7,6},{8,9},{9,8},{10,11... | collective-permute-start | bytes 104 | tf_op jit(solution)/shard_map/ppermute | solution.py:31
  11.8 0.1 collective-permute-start.7
  11.9 2.0 %collective-permute-start.1 = (bf16[2,8,2,96,128]{4,3,2,1,0:T(8,128)(2,1)}, bf16[2,8,2,96,128]{4,3,2,1,0:T(8,128)(2,1)S(1)}, u32[]{:S(2)}, u32[]{:S(2)}) collective-permute-start(bf16[2,8,2,96,128]{4,3,2,1,0:T(8,128)(2,1)} %get-tuple-element.50), channel_id=1, source_target_pairs={{0,8},{2,10},{4,12},{6,14},{8,0},{10,2},{12,4},{14,6},{16,24},{18,... | collective-permute-start | bytes 2359304 | tf_op jit(solution)/shard_map/ppermute | solution.py:468
  13.9 1.5 %collective-permute-start.3 = (bf16[2,8,4,96,128]{4,3,2,1,0:T(8,128)(2,1)}, bf16[2,8,4,96,128]{4,3,2,1,0:T(8,128)(2,1)}, u32[]{:S(2)}, u32[]{:S(2)}) collective-permute-start(bf16[2,8,4,96,128]{4,3,2,1,0:T(8,128)(2,1)} %get-tuple-element.53), channel_id=1, source_target_pairs={{0,4},{2,6},{4,0},{6,2},{8,12},{10,14},{12,8},{14,10},{16,20},{18,... | collective-permute-start | bytes 4718600 | tf_op jit(solution)/shard_map/ppermute | solution.py:468
  15.4 0.0 collective-permute-done
  15.4 2.6 %collective-permute-start.4 = (bf16[2,8,1,96,128]{4,3,1,0,2:T(8,128)(2,1)}, bf16[2,8,1,96,128]{4,3,1,0,2:T(8,128)(2,1)S(1)}, u32[]{:S(2)}, u32[]{:S(2)}) collective-permute-start(bf16[2,8,1,96,128]{4,3,1,0,2:T(8,128)(2,1)} %bitcast.8), channel_id=1, source_target_pairs={{0,16},{2,18},{4,20},{6,22},{8,24},{10,26},{12,28},{14,30},{16,0},... | collective-permute-start | bytes 1179656 | tf_op jit(solution)/shard_map/ppermute | solution.py:468
  18.0 0.7 broadcast_xor_fusion.table
  18.7 18.6 %class0.1 = (bf16[8,8,48,128]{3,2,1,0:T(8,128)(2,1)}, bf16[8,8,48,128]{3,2,1,0:T(8,128)(2,1)}, bf16[8,8,96,128]{3,2,1,0:T(8,128)(2,1)}) custom-call(s32[1]{0:T(128)} %bitcast.2.own_x, s32[8,16]{1,0:T(8,128)} %broadcast_xor_fusion.1.table, bf16[1536,1024]{1,0:T(8,128)(2,1)} %q_ref, bf16[2,8,8,96,128]{4,3,2,1,0:T(8,128)(2,1)} %get-tuple-element.48.refs_0_, ...), custom_call_target="tpu_custom_call" | custom-call | flops 14495514624 | bytes 9437184 | tf_op jit(solution)/shard_map/class0/pallas_call | solution.py:325
  37.3 2.8 %collective-permute-done.1.refs_0_ = bf16[2,8,2,96,128]{4,3,2,1,0:T(8,128)(2,1)S(1)} collective-permute-done((bf16[2,8,2,96,128]{4,3,2,1,0:T(8,128)(2,1)}, bf16[2,8,2,96,128]{4,3,2,1,0:T(8,128)(2,1)S(1)}, u32[]{:S(2)}, u32[]{:S(2)}) %collective-permute-start.1) | collective-permute-done | bytes 786464 | tf_op jit(solution)/shard_map/ppermute | solution.py:468
  40.1 3.8 %collective-permute-start.5 = (bf16[2,8,1,96,128]{4,3,1,0,2:T(8,128)(2,1)}, bf16[2,8,1,96,128]{4,3,1,0,2:T(8,128)(2,1)S(1)}, u32[]{:S(2)}, u32[]{:S(2)}) collective-permute-start(bf16[2,8,1,96,128]{4,3,1,0,2:T(8,128)(2,1)} %bitcast.9), channel_id=1, source_target_pairs={{0,24},{2,26},{4,28},{6,30},{8,16},{10,18},{12,20},{14,22},{16,8},... | collective-permute-start | bytes 1179656 | tf_op jit(solution)/shard_map/ppermute | solution.py:468
  43.9 0.0 collective-permute-done.2.refs_2_
  43.9 0.0 collective-permute-start.6
  43.9 12.9 %class1.1 = (bf16[8,4,48,128]{3,2,1,0:T(8,128)(2,1)}, bf16[8,4,48,128]{3,2,1,0:T(8,128)(2,1)}) custom-call(s32[1]{0:T(128)} %bitcast.2.own_x, s32[8,16]{1,0:T(8,128)} %broadcast_xor_fusion.1.table, bf16[8,8,96,128]{3,2,1,0:T(8,128)(2,1)} %get-tuple-element.49.q_ref, bf16[2,8,8,96,128]{4,3,2,1,0:T(8,128)(2,1)} %get-tuple-element.48.refs_0_, ...), custom_call_target="tpu_custom_call" | custom-call | flops 10871635968 | bytes 7077888 | tf_op jit(solution)/shard_map/class1/pallas_call | solution.py:325
  56.8 0.0 copy-done.7
  56.8 0.0 collective-permute-done.4
  56.8 0.0 collective-permute-done.5
  56.8 0.0 collective-permute-done.3.refs_3_
  56.8 2.8 %collective-permute-done.7.refs_4_ = bf16[512,2048]{1,0:T(8,128)(2,1)} collective-permute-done((bf16[512,2048]{1,0:T(8,128)(2,1)S(1)}, bf16[512,2048]{1,0:T(8,128)(2,1)}, u32[]{:S(2)}, u32[]{:S(2)}) %collective-permute-start.7) | collective-permute-done | bytes 2097184 | tf_op jit(solution)/shard_map/ppermute | solution.py:31
  59.6 0.0 collective-permute-done.6.refs_1_
  59.6 0.0 collective-permute-start.11
  59.6 1.2 slice.3
  60.8 0.1 pad_maximum_fusion.refs_4_
  60.8 0.0 copy-start.2
  60.9 0.0 copy-start.11
  60.9 1.6 %collective-permute-start.9 = (bf16[2,2,8,1,96,128]{5,4,3,2,1,0:T(8,128)(2,1)S(1)}, bf16[2,2,8,1,96,128]{5,4,3,2,1,0:T(8,128)(2,1)}, u32[]{:S(2)}, u32[]{:S(2)}) collective-permute-start(bf16[2,2,8,1,96,128]{5,4,3,2,1,0:T(8,128)(2,1)S(1)} %pad_maximum_fusion.refs_4_), channel_id=1, source_target_pairs={{0,4},{2,6},{4,0},{6,2},{8,12},{10,14},{12,8},{14,10},{16,20},{18,... | collective-permute-start | bytes 2359304 | tf_op jit(solution)/shard_map/ppermute | solution.py:468
  62.5 1.6 %collective-permute-start.8 = (bf16[2,8,2,96,128]{4,3,2,1,0:T(8,128)(2,1)S(1)}, bf16[2,8,2,96,128]{4,3,2,1,0:T(8,128)(2,1)}, u32[]{:S(2)}, u32[]{:S(2)}) collective-permute-start(bf16[2,8,2,96,128]{4,3,2,1,0:T(8,128)(2,1)S(1)} %slice.3), channel_id=1, source_target_pairs={{0,8},{2,10},{4,12},{6,14},{8,0},{10,2},{12,4},{14,6},{16,24},{18,... | collective-permute-start | bytes 2359304 | tf_op jit(solution)/shard_map/ppermute | solution.py:468
  64.0 0.5 collective-permute-start.10
  64.6 0.0 collective-permute-done.11.refs_4_
  64.6 16.4 %class2.1 = (bf16[8,2,48,128]{3,2,1,0:T(8,128)(2,1)}, bf16[8,2,48,128]{3,2,1,0:T(8,128)(2,1)}, f32[8,192,128]{2,1,0:T(8,128)}, f32[8,192,128]{2,1,0:T(8,128)}, f32[8,192,128]{2,1,0:T(8,128)}) custom-call(s32[1]{0:T(128)} %bitcast.2.own_x, s32[8,16]{1,0:T(8,128)} %broadcast_xor_fusion.1.table, bf16[8,8,96,128]{3,2,1,0:T(8,128)(2,1)} %get-tuple-element.49.q_ref, ...), custom_call_target="tpu_custom_call" | custom-call | flops 14495514624 | bytes 9437184 | tf_op jit(solution)/shard_map/class2/pallas_call | solution.py:325
  81.0 0.0 collective-permute-done.9.refs_6_
  81.0 1.3 %collective-permute-done.8.refs_2_ = bf16[2,8,2,96,128]{4,3,2,1,0:T(8,128)(2,1)} collective-permute-done((bf16[2,8,2,96,128]{4,3,2,1,0:T(8,128)(2,1)S(1)}, bf16[2,8,2,96,128]{4,3,2,1,0:T(8,128)(2,1)}, u32[]{:S(2)}, u32[]{:S(2)}) %collective-permute-start.8) | collective-permute-done | bytes 786464 | tf_op jit(solution)/shard_map/ppermute | solution.py:468
  82.2 1.4 %collective-permute-done.10.refs_3_ = bf16[8,8,48,128]{3,2,1,0:T(8,128)(2,1)S(1)} collective-permute-done((bf16[8,8,48,128]{3,2,1,0:T(8,128)(2,1)}, bf16[8,8,48,128]{3,2,1,0:T(8,128)(2,1)S(1)}, u32[]{:S(2)}, u32[]{:S(2)}) %collective-permute-start.10) | collective-permute-done | bytes 786464 | tf_op jit(solution)/shard_map/ppermute | solution.py:31
  83.6 0.0 collective-permute-start.12
  83.6 0.0 copy-done.2
  83.6 0.5 collective-permute-start.13
  84.2 0.1 collective-permute-start.14
  84.2 0.0 copy-done.11
  84.2 0.5 collective-permute-start.16
  84.8 1.5 %collective-permute-start.17 = (bf16[8,2,48,128]{3,2,1,0:T(8,128)(2,1)}, bf16[8,2,48,128]{3,2,1,0:T(8,128)(2,1)S(1)}, u32[]{:S(2)}, u32[]{:S(2)}) collective-permute-start(bf16[8,2,48,128]{3,2,1,0:T(8,128)(2,1)} %get-tuple-element.76), channel_id=1, source_target_pairs={{0,1},{1,0},{2,3},{3,2},{4,5},{5,4},{6,7},{7,6},{8,9},{9,8},{10,11... | collective-permute-start | bytes 589832 | tf_op jit(solution)/shard_map/ppermute | solution.py:31
  86.3 0.3 collective-permute-done.12.refs_3_
  86.5 1.3 %collective-permute-done.13.refs_5_ = bf16[2,2,8,1,96,128]{5,4,3,2,1,0:T(8,128)(2,1)S(1)} collective-permute-done((bf16[2,2,8,1,96,128]{5,4,3,2,1,0:T(8,128)(2,1)S(1)}, bf16[2,2,8,1,96,128]{5,4,3,2,1,0:T(8,128)(2,1)S(1)}, u32[]{:S(2)}, u32[]{:S(2)}) %collective-permute-start.13) | collective-permute-done | bytes 786464 | tf_op jit(solution)/shard_map/ppermute | solution.py:468
  87.8 0.9 copy-done.9
  88.7 0.0 collective-permute-done.14.refs_7_
  88.7 0.9 copy-done.10
  89.6 7.8 %class3.1 = (bf16[8,2,48,128]{3,2,1,0:T(8,128)(2,1)}, bf16[8,2,48,128]{3,2,1,0:T(8,128)(2,1)}) custom-call(s32[1]{0:T(128)} %bitcast.2.own_x, s32[8,16]{1,0:T(8,128)} %broadcast_xor_fusion.1.table, bf16[8,8,96,128]{3,2,1,0:T(8,128)(2,1)} %get-tuple-element.49.q_ref, bf16[2,8,2,96,128]{4,3,2,1,0:T(8,128)(2,1)} %copy-done.7, ...), custom_call_target="tpu_custom_call" | custom-call | flops 3623878656 | bytes 2359296 | tf_op jit(solution)/shard_map/class3/pallas_call | solution.py:325
  97.4 0.0 copy-done.1
  97.4 0.0 collective-permute-done.16.refs_2_
  97.4 2.5 %collective-permute-done.17.refs_1_ = bf16[8,2,48,128]{3,2,1,0:T(8,128)(2,1)S(1)} collective-permute-done((bf16[8,2,48,128]{3,2,1,0:T(8,128)(2,1)}, bf16[8,2,48,128]{3,2,1,0:T(8,128)(2,1)S(1)}, u32[]{:S(2)}, u32[]{:S(2)}) %collective-permute-start.17) | collective-permute-done | bytes 196640 | tf_op jit(solution)/shard_map/ppermute | solution.py:31
  99.9 0.0 collective-permute-start.18
  99.9 0.6 pad_add_fusion.halves
  100.5 0.5 collective-permute-start.15
  101.0 0.5 call_exported.0.halves
  101.5 8.3 %project_own.1.refs_6_ = bf16[768,2048]{1,0:T(8,128)(2,1)} custom-call(s32[8,16]{1,0:T(8,128)} %broadcast_xor_fusion.1.table, s32[2]{0:T(128)} %call_exported.0.halves, bf16[8,2,48,128]{3,2,1,0:T(8,128)(2,1)} %get-tuple-element.72.refs_0_, bf16[8,2,48,128]{3,2,1,0:T(8,128)(2,1)} %get-tuple-element.64.refs_1_, ...), custom_call_target="tpu_custom_call" | custom-call | flops 3221225472 | bytes 8912896 | tf_op jit(solution)/shard_map/project_own/pallas_call | solution.py:411
  109.8 0.0 collective-permute-done.15.refs_0_
  109.8 0.0 collective-permute-done.18.refs_5_
  109.8 0.7 copy-done.5
  110.5 1.3 %copy-done = bf16[512,2048]{1,0:T(8,128)(2,1)} copy-done((bf16[512,2048]{1,0:T(8,128)(2,1)}, bf16[512,2048]{1,0:T(8,128)(2,1)S(1)}, u32[]{:S(2)}) %copy-start) | copy-done | bytes 2097176
  111.8 9.9 %project.1 = bf16[768,2048]{1,0:T(8,128)(2,1)} custom-call(s32[8,16]{1,0:T(8,128)} %broadcast_xor_fusion.table, s32[2]{0:T(128)} %pad_add_fusion.halves, bf16[8,2,48,128]{3,2,1,0:T(8,128)(2,1)} %copy-done.5, bf16[8,2,48,128]{3,2,1,0:T(8,128)(2,1)} %copy-done.4, bf16[8,4,48,128]{3,2,1,0:T(8,128)(2,1)} %copy-done.3, bf16[8,8,48,128]{3,2,1,0:T(8,128)(2,1)} %copy-done.1, ...), custom_call_target="tpu_custom_call" | custom-call | flops 3221225472 | bytes 8912896 | tf_op jit(solution)/shard_map/project/pallas_call | solution.py:411
  (15 shorter events, 0.0 us)
Async XLA Ops:
  0.0 1.8 %copy-start.6 = (s32[16]{0:T(128)S(1)}, s32[16]{0:T(128)}, u32[]{:S(2)}) copy-start(s32[16]{0:T(128)} %constant.51.clone) | copy-start | bytes 196
  0.0 1.8 %copy-start.12 = (s32[8]{0:T(128)S(1)}, s32[8]{0:T(128)}, u32[]{:S(2)}) copy-start(s32[8]{0:T(128)} %param.13) | copy-start | bytes 100
  8.7 35.2 %collective-permute-start.2 = (bf16[2,8,8,96,128]{4,3,2,1,0:T(8,128)(2,1)}, bf16[2,8,8,96,128]{4,3,2,1,0:T(8,128)(2,1)}, u32[]{:S(2)}, u32[]{:S(2)}) collective-permute-start(bf16[2,8,8,96,128]{4,3,2,1,0:T(8,128)(2,1)} %get-tuple-element.48.refs_0_), channel_id=1, source_target_pairs={{0,2},{2,0},{4,6},{6,4},{8,10},{10,8},{12,14},{14,12},{16,18},{18,... | collective-permute-start | bytes 9437192 | tf_op jit(solution)/shard_map/ppermute | solution.py:468
  9.2 6.2 %collective-permute-start = (s32[8]{0:T(128)S(1)}, s32[8]{0:T(128)S(1)}, u32[]{:S(2)}, u32[]{:S(2)}) collective-permute-start(s32[8]{0:T(128)S(1)} %and_select_fusion), channel_id=1, source_target_pairs={{0,1},{1,0},{2,3},{3,2},{4,5},{5,4},{6,7},{7,6},{8,9},{9,8},{10,11... | collective-permute-start | bytes 104 | tf_op jit(solution)/shard_map/ppermute | solution.py:31
  11.8 47.8 %collective-permute-start.7 = (bf16[512,2048]{1,0:T(8,128)(2,1)S(1)}, bf16[512,2048]{1,0:T(8,128)(2,1)}, u32[]{:S(2)}, u32[]{:S(2)}) collective-permute-start(bf16[512,2048]{1,0:T(8,128)(2,1)S(1)} %constant_dynamic-slice_fusion), channel_id=1, source_target_pairs={{0,1},{1,0},{2,3},{3,2},{4,5},{5,4},{6,7},{7,6},{8,9},{9,8},{10,11... | collective-permute-start | bytes 6291464 | tf_op jit(solution)/shard_map/ppermute | solution.py:31
  11.9 28.3 %collective-permute-start.1 = (bf16[2,8,2,96,128]{4,3,2,1,0:T(8,128)(2,1)}, bf16[2,8,2,96,128]{4,3,2,1,0:T(8,128)(2,1)S(1)}, u32[]{:S(2)}, u32[]{:S(2)}) collective-permute-start(bf16[2,8,2,96,128]{4,3,2,1,0:T(8,128)(2,1)} %get-tuple-element.50), channel_id=1, source_target_pairs={{0,8},{2,10},{4,12},{6,14},{8,0},{10,2},{12,4},{14,6},{16,24},{18,... | collective-permute-start | bytes 2359304 | tf_op jit(solution)/shard_map/ppermute | solution.py:468
  13.9 42.9 %collective-permute-start.3 = (bf16[2,8,4,96,128]{4,3,2,1,0:T(8,128)(2,1)}, bf16[2,8,4,96,128]{4,3,2,1,0:T(8,128)(2,1)}, u32[]{:S(2)}, u32[]{:S(2)}) collective-permute-start(bf16[2,8,4,96,128]{4,3,2,1,0:T(8,128)(2,1)} %get-tuple-element.53), channel_id=1, source_target_pairs={{0,4},{2,6},{4,0},{6,2},{8,12},{10,14},{12,8},{14,10},{16,20},{18,... | collective-permute-start | bytes 4718600 | tf_op jit(solution)/shard_map/ppermute | solution.py:468
  15.4 41.4 %collective-permute-start.4 = (bf16[2,8,1,96,128]{4,3,1,0,2:T(8,128)(2,1)}, bf16[2,8,1,96,128]{4,3,1,0,2:T(8,128)(2,1)S(1)}, u32[]{:S(2)}, u32[]{:S(2)}) collective-permute-start(bf16[2,8,1,96,128]{4,3,1,0,2:T(8,128)(2,1)} %bitcast.8), channel_id=1, source_target_pairs={{0,16},{2,18},{4,20},{6,22},{8,24},{10,26},{12,28},{14,30},{16,0},... | collective-permute-start | bytes 1179656 | tf_op jit(solution)/shard_map/ppermute | solution.py:468
  40.1 16.7 %copy-start.7 = (bf16[2,8,2,96,128]{4,3,2,1,0:T(8,128)(2,1)}, bf16[2,8,2,96,128]{4,3,2,1,0:T(8,128)(2,1)S(1)}, u32[]{:S(2)}) copy-start(bf16[2,8,2,96,128]{4,3,2,1,0:T(8,128)(2,1)S(1)} %collective-permute-done.1.refs_0_) | copy-start | bytes 2359300
  40.1 16.7 %collective-permute-start.5 = (bf16[2,8,1,96,128]{4,3,1,0,2:T(8,128)(2,1)}, bf16[2,8,1,96,128]{4,3,1,0,2:T(8,128)(2,1)S(1)}, u32[]{:S(2)}, u32[]{:S(2)}) collective-permute-start(bf16[2,8,1,96,128]{4,3,1,0,2:T(8,128)(2,1)} %bitcast.9), channel_id=1, source_target_pairs={{0,24},{2,26},{4,28},{6,30},{8,16},{10,18},{12,20},{14,22},{16,8},... | collective-permute-start | bytes 1179656 | tf_op jit(solution)/shard_map/ppermute | solution.py:468
  43.9 15.7 %collective-permute-start.6 = (bf16[2,8,2,96,128]{4,3,2,1,0:T(8,128)(2,1)S(1)}, bf16[2,8,2,96,128]{4,3,2,1,0:T(8,128)(2,1)}, u32[]{:S(2)}, u32[]{:S(2)}) collective-permute-start(bf16[2,8,2,96,128]{4,3,2,1,0:T(8,128)(2,1)S(1)} %collective-permute-done.1.refs_0_), channel_id=1, source_target_pairs={{0,2},{2,0},{4,6},{6,4},{8,10},{10,8},{12,14},{14,12},{16,18},{18,... | collective-permute-start | bytes 2359304 | tf_op jit(solution)/shard_map/ppermute | solution.py:468
  59.6 5.0 %collective-permute-start.11 = (bf16[2,8,4,96,128]{4,3,2,1,0:T(8,128)(2,1)}, bf16[2,8,4,96,128]{4,3,2,1,0:T(8,128)(2,1)}, u32[]{:S(2)}, u32[]{:S(2)}) collective-permute-start(bf16[2,8,4,96,128]{4,3,2,1,0:T(8,128)(2,1)} %collective-permute-done.3.refs_3_), channel_id=1, source_target_pairs={{0,2},{2,0},{4,6},{6,4},{8,10},{10,8},{12,14},{14,12},{16,18},{18,... | collective-permute-start | bytes 4718600 | tf_op jit(solution)/shard_map/ppermute | solution.py:468
  60.8 22.8 %copy-start.2 = (bf16[2,2,8,1,96,128]{5,4,3,2,1,0:T(8,128)(2,1)}, bf16[2,2,8,1,96,128]{5,4,3,2,1,0:T(8,128)(2,1)S(1)}, u32[]{:S(2)}) copy-start(bf16[2,2,8,1,96,128]{5,4,3,2,1,0:T(8,128)(2,1)S(1)} %pad_maximum_fusion.refs_4_) | copy-start | bytes 2359300
  60.9 23.4 %copy-start.11 = (bf16[8,4,48,128]{3,2,1,0:T(8,128)(2,1)S(1)}, bf16[8,4,48,128]{3,2,1,0:T(8,128)(2,1)}, u32[]{:S(2)}) copy-start(bf16[8,4,48,128]{3,2,1,0:T(8,128)(2,1)} %get-tuple-element.75) | copy-start | bytes 1179652
  60.9 20.1 %collective-permute-start.9 = (bf16[2,2,8,1,96,128]{5,4,3,2,1,0:T(8,128)(2,1)S(1)}, bf16[2,2,8,1,96,128]{5,4,3,2,1,0:T(8,128)(2,1)}, u32[]{:S(2)}, u32[]{:S(2)}) collective-permute-start(bf16[2,2,8,1,96,128]{5,4,3,2,1,0:T(8,128)(2,1)S(1)} %pad_maximum_fusion.refs_4_), channel_id=1, source_target_pairs={{0,4},{2,6},{4,0},{6,2},{8,12},{10,14},{12,8},{14,10},{16,20},{18,... | collective-permute-start | bytes 2359304 | tf_op jit(solution)/shard_map/ppermute | solution.py:468
  62.5 19.8 %collective-permute-start.8 = (bf16[2,8,2,96,128]{4,3,2,1,0:T(8,128)(2,1)S(1)}, bf16[2,8,2,96,128]{4,3,2,1,0:T(8,128)(2,1)}, u32[]{:S(2)}, u32[]{:S(2)}) collective-permute-start(bf16[2,8,2,96,128]{4,3,2,1,0:T(8,128)(2,1)S(1)} %slice.3), channel_id=1, source_target_pairs={{0,8},{2,10},{4,12},{6,14},{8,0},{10,2},{12,4},{14,6},{16,24},{18,... | collective-permute-start | bytes 2359304 | tf_op jit(solution)/shard_map/ppermute | solution.py:468
  64.0 19.6 %collective-permute-start.10 = (bf16[8,8,48,128]{3,2,1,0:T(8,128)(2,1)}, bf16[8,8,48,128]{3,2,1,0:T(8,128)(2,1)S(1)}, u32[]{:S(2)}, u32[]{:S(2)}) collective-permute-start(bf16[8,8,48,128]{3,2,1,0:T(8,128)(2,1)} %get-tuple-element.63), channel_id=1, source_target_pairs={{0,1},{1,0},{2,3},{3,2},{4,5},{5,4},{6,7},{7,6},{8,9},{9,8},{10,11... | collective-permute-start | bytes 2359304 | tf_op jit(solution)/shard_map/ppermute | solution.py:31
  83.6 13.7 %copy-start.1 = (bf16[8,8,48,128]{3,2,1,0:T(8,128)(2,1)}, bf16[8,8,48,128]{3,2,1,0:T(8,128)(2,1)S(1)}, u32[]{:S(2)}) copy-start(bf16[8,8,48,128]{3,2,1,0:T(8,128)(2,1)S(1)} %collective-permute-done.10.refs_3_) | copy-start | bytes 2359300
  83.6 2.9 %collective-permute-start.12 = (bf16[2,8,2,96,128]{4,3,2,1,0:T(8,128)(2,1)}, bf16[2,8,2,96,128]{4,3,2,1,0:T(8,128)(2,1)S(1)}, u32[]{:S(2)}, u32[]{:S(2)}) collective-permute-start(bf16[2,8,2,96,128]{4,3,2,1,0:T(8,128)(2,1)} %collective-permute-done.8.refs_2_), channel_id=1, source_target_pairs={{0,2},{2,0},{4,6},{6,4},{8,10},{10,8},{12,14},{14,12},{16,18},{18,... | collective-permute-start | bytes 2359304 | tf_op jit(solution)/shard_map/ppermute | solution.py:468
  83.6 4.2 %collective-permute-start.13 = (bf16[2,2,8,1,96,128]{5,4,3,2,1,0:T(8,128)(2,1)S(1)}, bf16[2,2,8,1,96,128]{5,4,3,2,1,0:T(8,128)(2,1)S(1)}, u32[]{:S(2)}, u32[]{:S(2)}) collective-permute-start(bf16[2,2,8,1,96,128]{5,4,3,2,1,0:T(8,128)(2,1)S(1)} %pad_maximum_fusion.refs_4_), channel_id=1, source_target_pairs={{0,2},{2,0},{4,6},{6,4},{8,10},{10,8},{12,14},{14,12},{16,18},{18,... | collective-permute-start | bytes 2359304 | tf_op jit(solution)/shard_map/ppermute | solution.py:468
  84.2 4.5 %collective-permute-start.14 = (bf16[2,2,8,1,96,128]{5,4,3,2,1,0:T(8,128)(2,1)}, bf16[2,2,8,1,96,128]{5,4,3,2,1,0:T(8,128)(2,1)S(1)}, u32[]{:S(2)}, u32[]{:S(2)}) collective-permute-start(bf16[2,2,8,1,96,128]{5,4,3,2,1,0:T(8,128)(2,1)} %collective-permute-done.9.refs_6_), channel_id=1, source_target_pairs={{0,2},{2,0},{4,6},{6,4},{8,10},{10,8},{12,14},{14,12},{16,18},{18,... | collective-permute-start | bytes 2359304 | tf_op jit(solution)/shard_map/ppermute | solution.py:468
  84.2 13.1 %collective-permute-start.16 = (bf16[8,4,48,128]{3,2,1,0:T(8,128)(2,1)S(1)}, bf16[8,4,48,128]{3,2,1,0:T(8,128)(2,1)S(1)}, u32[]{:S(2)}, u32[]{:S(2)}) collective-permute-start(bf16[8,4,48,128]{3,2,1,0:T(8,128)(2,1)S(1)} %copy-done.11), channel_id=1, source_target_pairs={{0,1},{1,0},{2,3},{3,2},{4,5},{5,4},{6,7},{7,6},{8,9},{9,8},{10,11... | collective-permute-start | bytes 1179656 | tf_op jit(solution)/shard_map/ppermute | solution.py:31
  84.8 15.1 %collective-permute-start.17 = (bf16[8,2,48,128]{3,2,1,0:T(8,128)(2,1)}, bf16[8,2,48,128]{3,2,1,0:T(8,128)(2,1)S(1)}, u32[]{:S(2)}, u32[]{:S(2)}) collective-permute-start(bf16[8,2,48,128]{3,2,1,0:T(8,128)(2,1)} %get-tuple-element.76), channel_id=1, source_target_pairs={{0,1},{1,0},{2,3},{3,2},{4,5},{5,4},{6,7},{7,6},{8,9},{9,8},{10,11... | collective-permute-start | bytes 589832 | tf_op jit(solution)/shard_map/ppermute | solution.py:31
  86.5 3.1 %copy-start.8 = (bf16[2,8,2,96,128]{4,3,2,1,0:T(8,128)(2,1)}, bf16[2,8,2,96,128]{4,3,2,1,0:T(8,128)(2,1)S(1)}, u32[]{:S(2)}) copy-start(bf16[2,8,2,96,128]{4,3,2,1,0:T(8,128)(2,1)S(1)} %collective-permute-done.12.refs_3_) | copy-start | bytes 2359300
  87.8 0.9 copy-start.9
  88.7 0.9 copy-start.10
  97.4 12.4 %copy-start.3 = (bf16[8,4,48,128]{3,2,1,0:T(8,128)(2,1)}, bf16[8,4,48,128]{3,2,1,0:T(8,128)(2,1)S(1)}, u32[]{:S(2)}) copy-start(bf16[8,4,48,128]{3,2,1,0:T(8,128)(2,1)S(1)} %collective-permute-done.16.refs_2_) | copy-start | bytes 1179652
  99.9 9.9 %copy-start.4 = (bf16[8,2,48,128]{3,2,1,0:T(8,128)(2,1)}, bf16[8,2,48,128]{3,2,1,0:T(8,128)(2,1)S(1)}, u32[]{:S(2)}) copy-start(bf16[8,2,48,128]{3,2,1,0:T(8,128)(2,1)S(1)} %collective-permute-done.17.refs_1_) | copy-start | bytes 589828
  99.9 9.9 %collective-permute-start.18 = (bf16[512,2048]{1,0:T(8,128)(2,1)}, bf16[512,2048]{1,0:T(8,128)(2,1)S(1)}, u32[]{:S(2)}, u32[]{:S(2)}) collective-permute-start(bf16[512,2048]{1,0:T(8,128)(2,1)} %collective-permute-done.7.refs_4_), channel_id=1, source_target_pairs={{0,2},{2,0},{4,6},{6,4},{8,10},{10,8},{12,14},{14,12},{16,18},{18,... | collective-permute-start | bytes 6291464 | tf_op jit(solution)/shard_map/ppermute | solution.py:468
  100.5 9.3 %collective-permute-start.15 = (bf16[8,2,48,128]{3,2,1,0:T(8,128)(2,1)}, bf16[8,2,48,128]{3,2,1,0:T(8,128)(2,1)S(1)}, u32[]{:S(2)}, u32[]{:S(2)}) collective-permute-start(bf16[8,2,48,128]{3,2,1,0:T(8,128)(2,1)} %get-tuple-element.71), channel_id=1, source_target_pairs={{0,1},{1,0},{2,3},{3,2},{4,5},{5,4},{6,7},{7,6},{8,9},{9,8},{10,11... | collective-permute-start | bytes 589832 | tf_op jit(solution)/shard_map/ppermute | solution.py:31
  109.8 0.7 copy-start.5
  110.5 1.3 %copy-start = (bf16[512,2048]{1,0:T(8,128)(2,1)}, bf16[512,2048]{1,0:T(8,128)(2,1)S(1)}, u32[]{:S(2)}) copy-start(bf16[512,2048]{1,0:T(8,128)(2,1)S(1)} %collective-permute-done.18.refs_5_) | copy-start | bytes 6291460
